TPU v7x, 1024 devices: a whole 4x4x32 slice. The times are simulated.
1024 devices in a mesh: gx: 64 (over z, core), gy: 16 (over x, y).
Axes of the slice: x: 4, y: 4, z: 32, core: 2. Of those that a mesh axis runs over, the one named last changes fastest.
Arguments:
- density: float32 [256, 128, 128], P('gx', 'gy'), may hold values from 0.9 to 1.1
- velocity: float32 [3, 256, 128, 128], P(None, 'gx', 'gy'), may hold values from -0.625 to 0.625
- fluid_mask: int32 [256, 128, 128], P('gx', 'gy'), may hold values 0 or 1
- unit_of_column: int32 [256, 128], P('gx', 'gy'), may hold values from 0 to 127
- radius_base: float32 [8192], P(('gx', 'gy')), may hold values from 0.5 to 2
Outputs:
- density_out: float32 [256, 128, 128], P('gx', 'gy')
- velocity_out: float32 [3, 256, 128, 128], P(None, 'gx', 'gy')
- radius_out: float32 [8192], P(('gx', 'gy'))
All inputs are finite; a program needn't handle non-finite values. No bound on the sum of `fluid_mask` on one device may be relied on, other than what follows from the above.
Results may differ from a plain program's by a relative error of at most 0.0003.
Values sent between devices are 32-bit elements; how exact they have to be, the bound alone decides.
No kernel may reach another device: no remote copies, remote signals or barrier semaphores. Data moves between devices by JAX's collectives and lax.ppermute only.
A program may use at most 32 MiB of HBM per device.

v0:
```python
import functools

import jax
import jax.numpy as jnp
from jax import lax
from jax.experimental import pallas as pl
from jax.experimental.pallas import tpu as pltpu
from jax.sharding import Mesh
from jax.sharding import PartitionSpec as P


UNIT_DEV = 8
GX_GY = ("gx", "gy_0", "gy_1")
GY = ("gy_0", "gy_1")

LATTICE = (
    (0, 0, 0),
    (1, 0, 0),
    (-1, 0, 0),
    (0, 1, 0),
    (0, -1, 0),
    (0, 0, 1),
    (0, 0, -1),
    (1, 1, 0),
    (-1, -1, 0),
    (1, -1, 0),
    (-1, 1, 0),
    (1, 0, 1),
    (-1, 0, -1),
    (1, 0, -1),
    (-1, 0, 1),
    (0, 1, 1),
    (0, -1, -1),
    (0, 1, -1),
    (0, -1, 1),
)
PAIRS = tuple(range(1, 19, 2))
WEIGHTS = (1.0 / 3.0,) + (1.0 / 18.0,) * 6 + (1.0 / 36.0,) * 12
RELAX_RATE = 1.25
DRIVE_SCALE = 0.002
F32 = jnp.float32

TILE = 8
LANES = 128
PAD = 8
WIDE = 24
MID = 16


def opposite(direction):
    if direction == 0:
        return 0
    return direction + 1 if direction % 2 == 1 else direction - 1


def dot_c(direction, vector):
    total = None
    for c, v in zip(LATTICE[direction], vector):
        if c != 0:
            term = v if c > 0 else -v
            total = term if total is None else total + term
    return total


def moments(f, fluid):
    rho = f[0]
    momentum = [None, None, None]
    for i in PAIRS:
        rho = rho + (f[i] + f[i + 1])
        diff = f[i] - f[i + 1]
        for k in range(3):
            c = LATTICE[i][k]
            if c != 0:
                term = diff if c > 0 else -diff
                momentum[k] = term if momentum[k] is None else momentum[k] + term
    inverse = jnp.where(fluid, 1.0 / rho, 0.0)
    return jnp.where(fluid, rho, 0.0), [m * inverse for m in momentum]


def square(u):
    return u[0] * u[0] + u[1] * u[1] + u[2] * u[2]


def relaxed(f, rho, u, speed_sq, drive):
    rate = 1.0 if f is None else RELAX_RATE
    scaled = rate * rho
    even_base = scaled * (1.0 - 1.5 * speed_sq)
    force = drive * rho
    post = [None] * 19
    rest = WEIGHTS[0] * even_base
    post[0] = rest if f is None else rest + (1.0 - RELAX_RATE) * f[0]
    per_weight = {}
    for w in (WEIGHTS[1], WEIGHTS[7]):
        per_weight[w] = (w * even_base, (4.5 * w) * scaled, (3.0 * w) * scaled, (3.0 * w) * force)
    for i in PAIRS:
        base, quadratic, linear, push = per_weight[WEIGHTS[i]]
        cu = dot_c(i, u)
        even = base + quadratic * (cu * cu)
        odd = linear * cu
        if LATTICE[i][2] > 0:
            odd = odd + push
        elif LATTICE[i][2] < 0:
            odd = odd - push
        post[i] = even + odd
        post[i + 1] = even - odd
        if f is not None:
            post[i] = post[i] + (1.0 - RELAX_RATE) * f[i]
            post[i + 1] = post[i + 1] + (1.0 - RELAX_RATE) * f[i + 1]
    return post


def rolled(x, step):
    if step == 0:
        return x
    return pltpu.roll(x, step % LANES, axis=1)


def pulled(post_ref, column, row, bits):
    f = [post_ref[0, column, pl.ds(row, TILE), :]]
    for i in range(1, 19):
        cx, cy, cz = LATTICE[i]
        source = rolled(post_ref[i, column - cx, pl.ds(row - cy, TILE), :], cz)
        bounced = post_ref[opposite(i), column, pl.ds(row, TILE), :]
        f.append(jnp.where((bits & (1 << i)) != 0, source, bounced))
    return f


def drive_of(radius_row, unit):
    radius = jnp.take_along_axis(radius_row, unit.astype(jnp.int32), axis=1)
    return DRIVE_SCALE * radius * radius


def shear(links, speed_sq):
    return jnp.where(links > 0.0, links * speed_sq, 0.0)


def by_unit(column_values, unit):
    total = jnp.sum(column_values, axis=1, keepdims=True)
    lane = lax.broadcasted_iota(jnp.int32, (TILE, LANES), 1)
    return jnp.where(unit.astype(jnp.int32) == lane, total, 0.0)


def sublane_total(x):
    return jnp.broadcast_to(jnp.sum(x, axis=0, keepdims=True), (TILE, LANES))


def row_pick(rows):
    sub = lax.broadcasted_iota(jnp.int32, (TILE, LANES), 0)
    out = jnp.zeros((TILE, LANES), F32)
    for k, value in enumerate(rows):
        out = jnp.where(sub == k, value, out)
    return out


def every(tile, k):
    return jnp.broadcast_to(tile[k : k + 1, :], (TILE, LANES))


def send_all(ref, tile):
    for j in range(ref.shape[0]):
        ref[j] = tile


def sum_of(ref):
    parts = [ref[j] for j in range(ref.shape[0])]
    while len(parts) > 1:
        parts = [a + b for a, b in zip(parts[::2], parts[1::2])] + (
            [parts[-1]] if len(parts) % 2 else []
        )
    return parts[0]


def gather_kernel(place_ref, density, velocity, mask, unit, radius, out, placed):
    lane = lax.broadcasted_iota(jnp.int32, (TILE, LANES), 1)
    narrow = (TILE, TILE)
    diagonal = lax.broadcasted_iota(jnp.int32, narrow, 0) == lax.broadcasted_iota(jnp.int32, narrow, 1)
    for x in range(4):
        out[0, x] = jnp.where(mask[x] != 0, density[x], 0.0)
        for k in range(3):
            out[1 + k, x] = velocity[k, x]
        units = jnp.broadcast_to(unit[x : x + 1, :].astype(F32), narrow)
        column = jnp.sum(jnp.where(diagonal, units, 0.0), axis=1, keepdims=True)
        out[4, x] = jnp.broadcast_to(column, (TILE, LANES))
    radii = jnp.broadcast_to(radius[...], narrow)
    column = jnp.sum(jnp.where(diagonal, radii, 0.0), axis=1, keepdims=True)
    sub = lax.broadcasted_iota(jnp.int32, (TILE, LANES), 0)
    spread = jnp.where(lane == place_ref[0] * UNIT_DEV + sub, column, 0.0)
    placed[...] = sublane_total(spread)


def rows_kernel(low, own, high, left_out, right_out):
    for half, out in ((0, left_out), (1, right_out)):
        for k in range(5):
            for x in range(2):
                for part, ref in enumerate((low, own, high)):
                    out[k, x, pl.ds(part * TILE, TILE), :] = ref[k, 2 * half + x]


def base_kernel(own, left, right, out):
    sub = lax.broadcasted_iota(jnp.int32, (TILE, LANES), 0)
    tile = jnp.where(sub == 0, own[...], jnp.where(sub == 1, left[...], right[...]))
    send_all(out, jnp.where(sub < 3, tile, 0.0))


def first_kernel(
    edge_ref, halo_l, left, right, halo_r, base_in, f_l, f_r, bits_out, links_out, send, base_out, post, open_
):
    fields = (halo_l, left, right, halo_r)
    base = sum_of(base_in)
    base_out[...] = base
    radius = [every(base, 1), every(base, 0), every(base, 0), every(base, 2)]
    lane = lax.broadcasted_iota(jnp.int32, (TILE, LANES), 1)
    for part in range(4):
        inside = None
        if part == 0:
            inside = edge_ref[0]
        elif part == 3:
            inside = edge_ref[1]
        for x in range(2):
            column = 2 * part + x
            zero = jnp.zeros((TILE, LANES), jnp.int32)
            for k in range(3):
                open_[k, column, pl.ds(0, TILE), :] = zero
                open_[k, column, pl.ds(PAD + WIDE, TILE), :] = zero
            for t in range(WIDE // TILE):
                here = (fields[part][0, x, pl.ds(t * TILE, TILE), :] > 0.0).astype(jnp.int32)
                if inside is not None:
                    here = here * inside
                rows = pl.ds(PAD + t * TILE, TILE)
                open_[0, column, rows, :] = here
                open_[1, column, rows, :] = jnp.where(lane == 0, 0, pltpu.roll(here, 1, axis=1))
                open_[2, column, rows, :] = jnp.where(
                    lane == LANES - 1, 0, pltpu.roll(here, LANES - 1, axis=1)
                )
    for column in range(1, 7):
        part, x = divmod(column, 2)
        for t in range(WIDE // TILE):
            rows = pl.ds(t * TILE, TILE)
            rho = fields[part][0, x, rows, :]
            u = [fields[part][1 + k, x, rows, :] for k in range(3)]
            drive = drive_of(radius[part], fields[part][4, x, rows, :])
            values = relaxed(None, rho, u, square(u), drive)
            for i in range(19):
                post[i, column, pl.ds(PAD + t * TILE, TILE), :] = values[i]
    link_sum = shear_0 = shear_1 = jnp.zeros((TILE, LANES), F32)
    for column in range(1, 7):
        part, x = divmod(column, 2)
        for t in range(WIDE // TILE):
            row = PAD + t * TILE
            rows = pl.ds(t * TILE, TILE)
            bits = jnp.zeros((TILE, LANES), jnp.int32)
            count = jnp.zeros((TILE, LANES), jnp.int32)
            for i in range(1, 19):
                cx, cy, cz = LATTICE[i]
                seen = open_[cz % 3, column - cx, pl.ds(row - cy, TILE), :]
                count = count + seen
                bits = bits | (seen << i)
            bits_out[column - 1, rows, :] = bits
            if part not in (1, 2):
                continue
            f = pulled(post, column, row, bits)
            out = f_l if part == 1 else f_r
            for i in range(19):
                out[i, x, rows, :] = f[i]
            if t != 1:
                links_out[column - 2, rows, :] = jnp.zeros((TILE, LANES), F32)
                continue
            fluid = fields[part][0, x, rows, :] > 0.0
            links = jnp.where(fluid, (18 - count).astype(F32), 0.0)
            links_out[column - 2, rows, :] = links
            unit = fields[part][4, x, rows, :]
            u = [fields[part][1 + k, x, rows, :] for k in range(3)]
            link_sum = link_sum + by_unit(links, unit)
            shear_0 = shear_0 + by_unit(links * square(u), unit)
            _, u = moments(f, fluid)
            shear_1 = shear_1 + by_unit(links * square(u), unit)
    send_all(send, row_pick([sublane_total(s) for s in (shear_0, shear_1, link_sum)]))


def response_kernel(gathered, base, links_in, radius_out, links_out=None):
    totals = sum_of(gathered)
    if links_out is None:
        links = links_in[...]
    else:
        links = every(totals, 2)
        links_out[...] = links
    mean = 100.0 * totals / jnp.maximum(links, 1.0)
    radius_out[...] = every(base[...], 0) * (0.6 + 0.8 * jnp.tanh(mean))


def collide_from(parts, fields, radius, row_in_fields, columns, n_rows, post):
    for column in columns:
        part, x = divmod(column, 2)
        for t in range(n_rows // TILE):
            rows = pl.ds(t * TILE, TILE)
            near = pl.ds(row_in_fields + t * TILE, TILE)
            f = [parts[part][i, x, rows, :] for i in range(19)]
            rho, u = moments(f, fields[part][0, x, near, :] > 0.0)
            drive = drive_of(radius[part], fields[part][4, x, near, :])
            values = relaxed(f, rho, u, square(u), drive)
            for i in range(19):
                post[i, column, pl.ds(PAD + t * TILE, TILE), :] = values[i]


def two_steps_kernel(
    h_l, a, b, h_r, g_hl, g_a, g_b, g_hr, bits_in, links_in, rad, rad_l, rad_r, f_l, f_r, send, post_a, post_b, *, n_rows
):
    parts, fields = (h_l, a, b, h_r), (g_hl, g_a, g_b, g_hr)
    top = (WIDE - n_rows) // 2
    first = [every(r[...], 0) for r in (rad_l, rad, rad, rad_r)]
    second = [every(r[...], 1) for r in (rad_l, rad, rad, rad_r)]
    collide_from(parts, fields, first, top, range(8), n_rows, post_a)
    shear_a = shear_b = jnp.zeros((TILE, LANES), F32)
    skip = (n_rows - MID) // 2
    for column in range(1, 7):
        part, x = divmod(column, 2)
        for t in range(MID // TILE):
            near = pl.ds((WIDE - MID) // 2 + t * TILE, TILE)
            f = pulled(post_a, column, PAD + skip + t * TILE, bits_in[column - 1, near, :])
            rho, u = moments(f, fields[part][0, x, near, :] > 0.0)
            speed_sq = square(u)
            unit = fields[part][4, x, near, :]
            if part in (1, 2):
                shear_a = shear_a + by_unit(shear(links_in[column - 2, near, :], speed_sq), unit)
            values = relaxed(f, rho, u, speed_sq, drive_of(second[part], unit))
            for i in range(19):
                post_b[i, column, pl.ds(PAD + t * TILE, TILE), :] = values[i]
    for column in range(2, 6):
        part, x = divmod(column, 2)
        out = f_l if part == 1 else f_r
        for t in range(MID // TILE):
            near = pl.ds((WIDE - MID) // 2 + t * TILE, TILE)
            f = pulled(post_b, column, PAD + t * TILE, bits_in[column - 1, near, :])
            for i in range(19):
                out[i, x, pl.ds(t * TILE, TILE), :] = f[i]
            _, u = moments(f, fields[part][0, x, near, :] > 0.0)
            shear_b = shear_b + by_unit(
                shear(links_in[column - 2, near, :], square(u)), fields[part][4, x, near, :]
            )
    send_all(send, row_pick([sublane_total(s) for s in (shear_a, shear_b)]))


def last_kernel(
    h_l, a, b, h_r, g_hl, g_a, g_b, g_hr, bits_in, rad, rad_l, rad_r, density, velocity, post
):
    parts, fields = (h_l, a, b, h_r), (g_hl, g_a, g_b, g_hr)
    radius = [every(r[...], 0) for r in (rad_l, rad, rad, rad_r)]
    collide_from(parts, fields, radius, (WIDE - MID) // 2, range(1, 7), MID, post)
    own = pl.ds(TILE, TILE)
    for column in range(2, 6):
        part, x = divmod(column, 2)
        f = pulled(post, column, PAD + (MID - TILE) // 2, bits_in[column - 1, own, :])
        rho, u = moments(f, fields[part][0, x, own, :] > 0.0)
        density[column - 2] = rho
        for k in range(3):
            velocity[k, column - 2] = u[k]


def call(kernel, outs, scratch=(), scalars=0, mib=1, plain_in=False, plain_out=False):
    vmem = pl.BlockSpec(memory_space=pltpu.VMEM)
    smem = pl.BlockSpec(memory_space=pltpu.SMEM)

    def run(*args):
        space = pltpu.HBM if plain_in else pltpu.VMEM
        args = args[:scalars] + tuple(
            pltpu.with_memory_space_constraint(a, space) for a in args[scalars:]
        )
        held = jax.ShapeDtypeStruct if plain_out else pltpu.VMEM
        return pl.pallas_call(
            kernel,
            out_shape=[held(shape, dtype) for shape, dtype in outs],
            in_specs=[smem] * scalars + [vmem] * (len(args) - scalars),
            out_specs=[vmem] * len(outs),
            scratch_shapes=[pltpu.VMEM(shape, dtype) for shape, dtype in scratch],
            compiler_params=pltpu.CompilerParams(vmem_limit_bytes=mib << 20),
        )(*args)

    return run


def step_all(density, velocity, fluid_mask, unit_of_column, radius_base):
    count = lax.axis_size(GY)
    place = lax.axis_index(GY)
    at_x = lax.axis_index("gx")
    edge = jnp.stack([at_x > 0, at_x < lax.axis_size("gx") - 1]).astype(jnp.int32)
    tile = ((TILE, LANES), F32)
    sends = ((count, TILE, LANES), F32)

    def ring(low, high):
        size = lax.axis_size("gx")
        up = [(i, (i + 1) % size) for i in range(size)]
        down = [(target, source) for source, target in up]
        return lax.ppermute(high, "gx", up), lax.ppermute(low, "gx", down)

    def exchange(blocks):
        return lax.all_to_all(blocks, GY, split_axis=0, concat_axis=0, tiled=True)

    own, placed = call(
        gather_kernel, [((5, 4, TILE, LANES), F32), tile], scalars=1, plain_in=True
    )(place.reshape(1), density, velocity, fluid_mask, unit_of_column, radius_base.reshape(1, -1))

    base_l, base_r = ring(placed, placed)
    (base_send,) = call(base_kernel, [sends])(placed, base_l, base_r)
    base_in = exchange(base_send)

    forward = [(i, i + 1) for i in range(count - 1)]
    backward = [(target, source) for source, target in forward]
    low = lax.ppermute(own, GY, forward)
    high = lax.ppermute(own, GY, backward)
    pair = ((5, 2, WIDE, LANES), F32)
    g_l, g_r = call(rows_kernel, [pair, pair])(low, own, high)
    g_hl, g_hr = ring(g_l, g_r)
    fields = (g_hl, g_l, g_r, g_hr)

    def populations(rows):
        return ((19, 2, rows, LANES), F32)

    f_l, f_r, bits, links, send, base = call(
        first_kernel,
        [
            populations(WIDE),
            populations(WIDE),
            ((6, WIDE, LANES), jnp.int32),
            ((4, WIDE, LANES), F32),
            sends,
            tile,
        ],
        [((19, 8, WIDE + 2 * PAD, LANES), F32), ((3, 8, WIDE + 2 * PAD, LANES), jnp.int32)],
        scalars=1,
        mib=6,
    )(edge, *fields, base_in)

    for turn in range(3):
        gathered = exchange(send)
        h_l, h_r = ring(f_l, f_r)
        if turn == 0:
            rad, link_tile = call(response_kernel, [tile, tile])(gathered, base, base)
        else:
            (rad,) = call(response_kernel, [tile])(gathered, base, link_tile)
        rad_l, rad_r = ring(rad, rad)
        parts = (h_l, f_l, f_r, h_r)
        if turn < 2:
            rows = WIDE if turn == 0 else MID
            f_l, f_r, send = call(
                functools.partial(two_steps_kernel, n_rows=rows),
                [populations(MID), populations(MID), sends],
                [
                    ((19, 8, rows + 2 * PAD, LANES), F32),
                    ((19, 8, MID + 2 * PAD, LANES), F32),
                ],
                mib=8,
            )(*parts, *fields, bits, links, rad, rad_l, rad_r)
    density_out, velocity_out = call(
        last_kernel,
        [((4, TILE, LANES), F32), ((3, 4, TILE, LANES), F32)],
        [((19, 8, MID + 2 * PAD, LANES), F32)],
        mib=4,
        plain_out=True,
    )(*parts, *fields, bits, rad, rad_l, rad_r)
    own_radius = lax.dynamic_slice_in_dim(rad[1], place * UNIT_DEV, UNIT_DEV)
    return density_out, velocity_out, own_radius


def solution(mesh):
    finer = Mesh(mesh.devices.reshape(mesh.shape["gx"], 4, -1), ("gx", "gy_0", "gy_1"))
    placed = (P("gx", GY, None), P(None, "gx", GY, None), P("gx", GY, None), P("gx", GY), P(GX_GY))
    return jax.shard_map(
        step_all,
        mesh=finer,
        in_specs=placed,
        out_specs=(P("gx", GY, None), P(None, "gx", GY, None), P(GX_GY)),
        check_vma=False,
    )
```

profile of v0, /device:TPU:2, one launch (start us, length us, event | category | flops | bytes accessed | tf_op | source)
XLA Modules:
  0.0 108.7 jit_solution(5433161437506408774)
XLA Ops:
  0.6 0.9 shard_map.76
  1.5 4.9 %collective-permute-start.1 = (f32[5,4,8,128]{3,2,1,0:T(8,128)S(1)}, f32[5,4,8,128]{3,2,1,0:T(8,128)S(1)}, u32[]{:S(2)}, u32[]{:S(2)}) collective-permute-start(f32[5,4,8,128]{3,2,1,0:T(8,128)S(1)} %get-tuple-element.23.own), channel_id=1, source_target_pairs={{1,0},{2,1},{3,2},{4,3},{5,4},{6,5},{7,6},{8,7},{9,8},{10,9},{11,1... | collective-permute-start | bytes 245768 | tf_op jit(solution)/shard_map/ppermute | solution.py:409
  6.4 1.9 %collective-permute-start = (f32[5,4,8,128]{3,2,1,0:T(8,128)S(1)}, f32[5,4,8,128]{3,2,1,0:T(8,128)S(1)}, u32[]{:S(2)}, u32[]{:S(2)}) collective-permute-start(f32[5,4,8,128]{3,2,1,0:T(8,128)S(1)} %get-tuple-element.23.own), channel_id=1, source_target_pairs={{0,1},{1,2},{2,3},{3,4},{4,5},{5,6},{6,7},{7,8},{8,9},{9,10},{10,1... | collective-permute-start | bytes 245768 | tf_op jit(solution)/shard_map/ppermute | solution.py:408
  8.5 6.4 %collective-permute-done.low = f32[5,4,8,128]{3,2,1,0:T(8,128)S(1)} collective-permute-done((f32[5,4,8,128]{3,2,1,0:T(8,128)S(1)}, f32[5,4,8,128]{3,2,1,0:T(8,128)S(1)}, u32[]{:S(2)}, u32[]{:S(2)}) %collective-permute-start) | collective-permute-done | bytes 81952 | tf_op jit(solution)/shard_map/ppermute | solution.py:408
  14.9 14.8 %collective-permute-start.3 = (f32[5,2,24,128]{3,2,1,0:T(8,128)S(1)}, f32[5,2,24,128]{3,2,1,0:T(8,128)S(1)}, u32[]{:S(2)}, u32[]{:S(2)}) collective-permute-start(f32[5,2,24,128]{3,2,1,0:T(8,128)S(1)} %get-tuple-element.25.left.g_a), channel_id=1, source_target_pairs={{16,0},{32,16},{48,32},{64,48},{80,64},{96,80},{112,96},{128,112},... | collective-permute-start | bytes 368648 | tf_op jit(solution)/shard_map/ppermute | solution.py:393
  29.7 2.1 %collective-permute-start.5 = (f32[8,128]{1,0:T(8,128)S(1)}, f32[8,128]{1,0:T(8,128)S(1)}, u32[]{:S(2)}, u32[]{:S(2)}) collective-permute-start(f32[8,128]{1,0:T(8,128)S(1)} %get-tuple-element.26.own), channel_id=1, source_target_pairs={{16,0},{32,16},{48,32},{64,48},{80,64},{96,80},{112,96},{128,112},... | collective-permute-start | bytes 12296 | tf_op jit(solution)/shard_map/ppermute | solution.py:393
  31.8 1.3 %collective-permute-done.5.right = f32[8,128]{1,0:T(8,128)S(1)} collective-permute-done((f32[8,128]{1,0:T(8,128)S(1)}, f32[8,128]{1,0:T(8,128)S(1)}, u32[]{:S(2)}, u32[]{:S(2)}) %collective-permute-start.5) | collective-permute-done | bytes 4128 | tf_op jit(solution)/shard_map/ppermute | solution.py:393
  33.1 2.9 %collective-permute-done.4.left = f32[8,128]{1,0:T(8,128)S(1)} collective-permute-done((f32[8,128]{1,0:T(8,128)S(1)}, f32[8,128]{1,0:T(8,128)S(1)}, u32[]{:S(2)}, u32[]{:S(2)}) %collective-permute-start.4) | collective-permute-done | bytes 4128 | tf_op jit(solution)/shard_map/ppermute | solution.py:393
  36.7 4.9 %all-to-all-start = ((f32[16,8,128]{2,1,0:T(8,128)}), f32[16,8,128]{2,1,0:T(8,128)S(1)}, u32[]{:S(2)}, u32[]{:S(2)}) async-start(f32[16,8,128]{2,1,0:T(8,128)} %shard_map.78), calls=%async_computation | async-start | bytes 131072 | tf_op jit(solution)/shard_map/all_to_all | solution.py:396
  41.6 6.2 %all-to-all-done.base_in = f32[16,8,128]{2,1,0:T(8,128)S(1)} async-done(((f32[16,8,128]{2,1,0:T(8,128)}), f32[16,8,128]{2,1,0:T(8,128)S(1)}, u32[]{:S(2)}, u32[]{:S(2)}) %all-to-all-start) | async-done | bytes 65568 | tf_op jit(solution)/shard_map/all_to_all | solution.py:396
  47.8 1.2 %shard_map.79 = (f32[19,2,24,128]{3,2,1,0:T(8,128)S(1)}, f32[19,2,24,128]{3,2,1,0:T(8,128)S(1)}, s32[6,24,128]{2,1,0:T(8,128)S(1)}, f32[4,24,128]{2,1,0:T(8,128)...) custom-call(s32[2]{0:T(128)S(1)} %add_convert_fusion.edge_ref, ...), custom_call_target="tpu_custom_call" | custom-call | tf_op jit(solution)/shard_map/pallas_call | solution.py:369
  49.1 2.9 %collective-permute-start.7 = (f32[19,2,24,128]{3,2,1,0:T(8,128)S(1)}, f32[19,2,24,128]{3,2,1,0:T(8,128)S(1)}, u32[]{:S(2)}, u32[]{:S(2)}) collective-permute-start(f32[19,2,24,128]{3,2,1,0:T(8,128)S(1)} %get-tuple-element.28.a), channel_id=1, source_target_pairs={{16,0},{32,16},{48,32},{64,48},{80,64},{96,80},{112,96},{128,112},... | collective-permute-start | bytes 1400840 | tf_op jit(solution)/shard_map/ppermute | solution.py:393
  52.0 10.9 %all_to_all.20.gathered = f32[16,8,128]{2,1,0:T(8,128)S(1)} all-to-all(f32[16,8,128]{2,1,0:T(8,128)S(1)} %get-tuple-element.31), channel_id=1, replica_groups=mesh['gx'=64,'gy_0'=4,'gy_1'=4] {'gy_0','gy_1'}, dimensions={0} | all-to-all | bytes 131072 | tf_op jit(solution)/shard_map/all_to_all | solution.py:396
  64.3 2.9 %collective-permute-done.8.rad_l = f32[8,128]{1,0:T(8,128)S(1)} collective-permute-done((f32[8,128]{1,0:T(8,128)S(1)}, f32[8,128]{1,0:T(8,128)S(1)}, u32[]{:S(2)}, u32[]{:S(2)}) %collective-permute-start.8) | collective-permute-done | bytes 4128 | tf_op jit(solution)/shard_map/ppermute | solution.py:393
  67.2 1.7 %shard_map.81 = (f32[19,2,16,128]{3,2,1,0:T(8,128)S(1)}, f32[19,2,16,128]{3,2,1,0:T(8,128)S(1)}, f32[16,8,128]{2,1,0:T(8,128)S(1)}) custom-call(f32[19,2,24,128]{3,2,1,0:T(8,128)S(1)} %collective-permute-done.6.h_l, f32[19,2,24,128]{3,2,1,0:T(8,128)S(1)} %get-tuple-element.28.a, f32[19,2,24,128]{3,2,1,0:T(8,128)S(1)} %get-tuple-element.27.b, ...), custom_call_target="tpu_custom_call" | custom-call | tf_op jit(solution)/shard_map/pallas_call | solution.py:369
  69.0 2.9 %collective-permute-start.11 = (f32[19,2,16,128]{3,2,1,0:T(8,128)S(1)}, f32[19,2,16,128]{3,2,1,0:T(8,128)S(1)}, u32[]{:S(2)}, u32[]{:S(2)}) collective-permute-start(f32[19,2,16,128]{3,2,1,0:T(8,128)S(1)} %get-tuple-element.35.a), channel_id=1, source_target_pairs={{16,0},{32,16},{48,32},{64,48},{80,64},{96,80},{112,96},{128,112},... | collective-permute-start | bytes 933896 | tf_op jit(solution)/shard_map/ppermute | solution.py:393
  71.9 10.9 %all_to_all.21.gathered = f32[16,8,128]{2,1,0:T(8,128)S(1)} all-to-all(f32[16,8,128]{2,1,0:T(8,128)S(1)} %get-tuple-element.36), channel_id=1, replica_groups=mesh['gx'=64,'gy_0'=4,'gy_1'=4] {'gy_0','gy_1'}, dimensions={0} | all-to-all | bytes 131072 | tf_op jit(solution)/shard_map/all_to_all | solution.py:396
  84.2 2.9 %collective-permute-done.12.rad_l = f32[8,128]{1,0:T(8,128)S(1)} collective-permute-done((f32[8,128]{1,0:T(8,128)S(1)}, f32[8,128]{1,0:T(8,128)S(1)}, u32[]{:S(2)}, u32[]{:S(2)}) %collective-permute-start.12) | collective-permute-done | bytes 4128 | tf_op jit(solution)/shard_map/ppermute | solution.py:393
  87.1 2.1 %shard_map.83 = (f32[19,2,16,128]{3,2,1,0:T(8,128)S(1)}, f32[19,2,16,128]{3,2,1,0:T(8,128)S(1)}, f32[16,8,128]{2,1,0:T(8,128)}) custom-call(f32[19,2,16,128]{3,2,1,0:T(8,128)S(1)} %collective-permute-done.10.h_l, f32[19,2,16,128]{3,2,1,0:T(8,128)S(1)} %get-tuple-element.35.a, f32[19,2,16,128]{3,2,1,0:T(8,128)S(1)} %get-tuple-element.34.b, ...), custom_call_target="tpu_custom_call" | custom-call | tf_op jit(solution)/shard_map/pallas_call | solution.py:369
  89.2 3.0 %collective-permute-start.15 = (f32[19,2,16,128]{3,2,1,0:T(8,128)S(1)}, f32[19,2,16,128]{3,2,1,0:T(8,128)S(1)}, u32[]{:S(2)}, u32[]{:S(2)}) collective-permute-start(f32[19,2,16,128]{3,2,1,0:T(8,128)S(1)} %get-tuple-element.39.a), channel_id=1, source_target_pairs={{16,0},{32,16},{48,32},{64,48},{80,64},{96,80},{112,96},{128,112},... | collective-permute-start | bytes 933896 | tf_op jit(solution)/shard_map/ppermute | solution.py:393
  92.2 4.8 %all-to-all-start.3 = ((f32[16,8,128]{2,1,0:T(8,128)}), f32[16,8,128]{2,1,0:T(8,128)S(1)}, u32[]{:S(2)}, u32[]{:S(2)}) async-start(f32[16,8,128]{2,1,0:T(8,128)} %get-tuple-element.40), calls=%async_computation.3 | async-start | bytes 131072 | tf_op jit(solution)/shard_map/all_to_all | solution.py:396
  97.0 6.3 %all-to-all-done.3.gathered = f32[16,8,128]{2,1,0:T(8,128)S(1)} async-done(((f32[16,8,128]{2,1,0:T(8,128)}), f32[16,8,128]{2,1,0:T(8,128)S(1)}, u32[]{:S(2)}, u32[]{:S(2)}) %all-to-all-start.3) | async-done | bytes 65568 | tf_op jit(solution)/shard_map/all_to_all | solution.py:396
  104.7 2.9 %collective-permute-done.16.rad_l = f32[8,128]{1,0:T(8,128)S(1)} collective-permute-done((f32[8,128]{1,0:T(8,128)S(1)}, f32[8,128]{1,0:T(8,128)S(1)}, u32[]{:S(2)}, u32[]{:S(2)}) %collective-permute-start.16) | collective-permute-done | bytes 4128 | tf_op jit(solution)/shard_map/ppermute | solution.py:393
  107.6 1.1 shard_map.85
  (31 shorter events, 5.0 us)
Async XLA Ops:
  1.5 6.9 %collective-permute-start.1 = (f32[5,4,8,128]{3,2,1,0:T(8,128)S(1)}, f32[5,4,8,128]{3,2,1,0:T(8,128)S(1)}, u32[]{:S(2)}, u32[]{:S(2)}) collective-permute-start(f32[5,4,8,128]{3,2,1,0:T(8,128)S(1)} %get-tuple-element.23.own), channel_id=1, source_target_pairs={{1,0},{2,1},{3,2},{4,3},{5,4},{6,5},{7,6},{8,7},{9,8},{10,9},{11,1... | collective-permute-start | bytes 245768 | tf_op jit(solution)/shard_map/ppermute | solution.py:409
  6.4 8.4 %collective-permute-start = (f32[5,4,8,128]{3,2,1,0:T(8,128)S(1)}, f32[5,4,8,128]{3,2,1,0:T(8,128)S(1)}, u32[]{:S(2)}, u32[]{:S(2)}) collective-permute-start(f32[5,4,8,128]{3,2,1,0:T(8,128)S(1)} %get-tuple-element.23.own), channel_id=1, source_target_pairs={{0,1},{1,2},{2,3},{3,4},{4,5},{5,6},{6,7},{7,8},{8,9},{9,10},{10,1... | collective-permute-start | bytes 245768 | tf_op jit(solution)/shard_map/ppermute | solution.py:408
  14.9 32.9 %collective-permute-start.2 = (f32[5,2,24,128]{3,2,1,0:T(8,128)S(1)}, f32[5,2,24,128]{3,2,1,0:T(8,128)S(1)}, u32[]{:S(2)}, u32[]{:S(2)}) collective-permute-start(f32[5,2,24,128]{3,2,1,0:T(8,128)S(1)} %get-tuple-element.24.right.g_b), channel_id=1, source_target_pairs={{0,16},{16,32},{32,48},{48,64},{64,80},{80,96},{96,112},{112,128},... | collective-permute-start | bytes 368648 | tf_op jit(solution)/shard_map/ppermute | solution.py:393
  14.9 32.9 %collective-permute-start.3 = (f32[5,2,24,128]{3,2,1,0:T(8,128)S(1)}, f32[5,2,24,128]{3,2,1,0:T(8,128)S(1)}, u32[]{:S(2)}, u32[]{:S(2)}) collective-permute-start(f32[5,2,24,128]{3,2,1,0:T(8,128)S(1)} %get-tuple-element.25.left.g_a), channel_id=1, source_target_pairs={{16,0},{32,16},{48,32},{64,48},{80,64},{96,80},{112,96},{128,112},... | collective-permute-start | bytes 368648 | tf_op jit(solution)/shard_map/ppermute | solution.py:393
  29.7 3.4 %collective-permute-start.5 = (f32[8,128]{1,0:T(8,128)S(1)}, f32[8,128]{1,0:T(8,128)S(1)}, u32[]{:S(2)}, u32[]{:S(2)}) collective-permute-start(f32[8,128]{1,0:T(8,128)S(1)} %get-tuple-element.26.own), channel_id=1, source_target_pairs={{16,0},{32,16},{48,32},{64,48},{80,64},{96,80},{112,96},{128,112},... | collective-permute-start | bytes 12296 | tf_op jit(solution)/shard_map/ppermute | solution.py:393
  31.8 4.2 %collective-permute-start.4 = (f32[8,128]{1,0:T(8,128)S(1)}, f32[8,128]{1,0:T(8,128)S(1)}, u32[]{:S(2)}, u32[]{:S(2)}) collective-permute-start(f32[8,128]{1,0:T(8,128)S(1)} %get-tuple-element.26.own), channel_id=1, source_target_pairs={{0,16},{16,32},{32,48},{48,64},{64,80},{80,96},{96,112},{112,128},... | collective-permute-start | bytes 12296 | tf_op jit(solution)/shard_map/ppermute | solution.py:393
  36.7 11.1 %all-to-all-start = ((f32[16,8,128]{2,1,0:T(8,128)}), f32[16,8,128]{2,1,0:T(8,128)S(1)}, u32[]{:S(2)}, u32[]{:S(2)}) async-start(f32[16,8,128]{2,1,0:T(8,128)} %shard_map.78), calls=%async_computation | async-start | bytes 131072 | tf_op jit(solution)/shard_map/all_to_all | solution.py:396
  49.1 18.1 %collective-permute-start.6 = (f32[19,2,24,128]{3,2,1,0:T(8,128)S(1)}, f32[19,2,24,128]{3,2,1,0:T(8,128)S(1)}, u32[]{:S(2)}, u32[]{:S(2)}) collective-permute-start(f32[19,2,24,128]{3,2,1,0:T(8,128)S(1)} %get-tuple-element.27.b), channel_id=1, source_target_pairs={{0,16},{16,32},{32,48},{48,64},{64,80},{80,96},{96,112},{112,128},... | collective-permute-start | bytes 1400840 | tf_op jit(solution)/shard_map/ppermute | solution.py:393
  49.1 18.1 %collective-permute-start.7 = (f32[19,2,24,128]{3,2,1,0:T(8,128)S(1)}, f32[19,2,24,128]{3,2,1,0:T(8,128)S(1)}, u32[]{:S(2)}, u32[]{:S(2)}) collective-permute-start(f32[19,2,24,128]{3,2,1,0:T(8,128)S(1)} %get-tuple-element.28.a), channel_id=1, source_target_pairs={{16,0},{32,16},{48,32},{64,48},{80,64},{96,80},{112,96},{128,112},... | collective-permute-start | bytes 1400840 | tf_op jit(solution)/shard_map/ppermute | solution.py:393
  62.9 1.3 %collective-permute-start.9 = (f32[8,128]{1,0:T(8,128)S(1)}, f32[8,128]{1,0:T(8,128)S(1)}, u32[]{:S(2)}, u32[]{:S(2)}) collective-permute-start(f32[8,128]{1,0:T(8,128)S(1)} %get-tuple-element.33.rad), channel_id=1, source_target_pairs={{16,0},{32,16},{48,32},{64,48},{80,64},{96,80},{112,96},{128,112},... | collective-permute-start | bytes 12296 | tf_op jit(solution)/shard_map/ppermute | solution.py:393
  63.0 4.3 %collective-permute-start.8 = (f32[8,128]{1,0:T(8,128)S(1)}, f32[8,128]{1,0:T(8,128)S(1)}, u32[]{:S(2)}, u32[]{:S(2)}) collective-permute-start(f32[8,128]{1,0:T(8,128)S(1)} %get-tuple-element.33.rad), channel_id=1, source_target_pairs={{0,16},{16,32},{32,48},{48,64},{64,80},{80,96},{96,112},{112,128},... | collective-permute-start | bytes 12296 | tf_op jit(solution)/shard_map/ppermute | solution.py:393
  69.0 18.1 %collective-permute-start.10 = (f32[19,2,16,128]{3,2,1,0:T(8,128)S(1)}, f32[19,2,16,128]{3,2,1,0:T(8,128)S(1)}, u32[]{:S(2)}, u32[]{:S(2)}) collective-permute-start(f32[19,2,16,128]{3,2,1,0:T(8,128)S(1)} %get-tuple-element.34.b), channel_id=1, source_target_pairs={{0,16},{16,32},{32,48},{48,64},{64,80},{80,96},{96,112},{112,128},... | collective-permute-start | bytes 933896 | tf_op jit(solution)/shard_map/ppermute | solution.py:393
  69.0 18.1 %collective-permute-start.11 = (f32[19,2,16,128]{3,2,1,0:T(8,128)S(1)}, f32[19,2,16,128]{3,2,1,0:T(8,128)S(1)}, u32[]{:S(2)}, u32[]{:S(2)}) collective-permute-start(f32[19,2,16,128]{3,2,1,0:T(8,128)S(1)} %get-tuple-element.35.a), channel_id=1, source_target_pairs={{16,0},{32,16},{48,32},{64,48},{80,64},{96,80},{112,96},{128,112},... | collective-permute-start | bytes 933896 | tf_op jit(solution)/shard_map/ppermute | solution.py:393
  82.8 1.3 %collective-permute-start.13 = (f32[8,128]{1,0:T(8,128)S(1)}, f32[8,128]{1,0:T(8,128)S(1)}, u32[]{:S(2)}, u32[]{:S(2)}) collective-permute-start(f32[8,128]{1,0:T(8,128)S(1)} %shard_map.82.rad), channel_id=1, source_target_pairs={{16,0},{32,16},{48,32},{64,48},{80,64},{96,80},{112,96},{128,112},... | collective-permute-start | bytes 12296 | tf_op jit(solution)/shard_map/ppermute | solution.py:393
  82.8 4.3 %collective-permute-start.12 = (f32[8,128]{1,0:T(8,128)S(1)}, f32[8,128]{1,0:T(8,128)S(1)}, u32[]{:S(2)}, u32[]{:S(2)}) collective-permute-start(f32[8,128]{1,0:T(8,128)S(1)} %shard_map.82.rad), channel_id=1, source_target_pairs={{0,16},{16,32},{32,48},{48,64},{64,80},{80,96},{96,112},{112,128},... | collective-permute-start | bytes 12296 | tf_op jit(solution)/shard_map/ppermute | solution.py:393
  89.2 18.4 %collective-permute-start.14 = (f32[19,2,16,128]{3,2,1,0:T(8,128)S(1)}, f32[19,2,16,128]{3,2,1,0:T(8,128)S(1)}, u32[]{:S(2)}, u32[]{:S(2)}) collective-permute-start(f32[19,2,16,128]{3,2,1,0:T(8,128)S(1)} %get-tuple-element.38.b), channel_id=1, source_target_pairs={{0,16},{16,32},{32,48},{48,64},{64,80},{80,96},{96,112},{112,128},... | collective-permute-start | bytes 933896 | tf_op jit(solution)/shard_map/ppermute | solution.py:393
  89.2 18.4 %collective-permute-start.15 = (f32[19,2,16,128]{3,2,1,0:T(8,128)S(1)}, f32[19,2,16,128]{3,2,1,0:T(8,128)S(1)}, u32[]{:S(2)}, u32[]{:S(2)}) collective-permute-start(f32[19,2,16,128]{3,2,1,0:T(8,128)S(1)} %get-tuple-element.39.a), channel_id=1, source_target_pairs={{16,0},{32,16},{48,32},{64,48},{80,64},{96,80},{112,96},{128,112},... | collective-permute-start | bytes 933896 | tf_op jit(solution)/shard_map/ppermute | solution.py:393
  92.2 11.1 %all-to-all-start.3 = ((f32[16,8,128]{2,1,0:T(8,128)}), f32[16,8,128]{2,1,0:T(8,128)S(1)}, u32[]{:S(2)}, u32[]{:S(2)}) async-start(f32[16,8,128]{2,1,0:T(8,128)} %get-tuple-element.40), calls=%async_computation.3 | async-start | bytes 131072 | tf_op jit(solution)/shard_map/all_to_all | solution.py:396
  103.3 1.3 %collective-permute-start.17 = (f32[8,128]{1,0:T(8,128)S(1)}, f32[8,128]{1,0:T(8,128)S(1)}, u32[]{:S(2)}, u32[]{:S(2)}) collective-permute-start(f32[8,128]{1,0:T(8,128)S(1)} %shard_map.84.rad), channel_id=1, source_target_pairs={{16,0},{32,16},{48,32},{64,48},{80,64},{96,80},{112,96},{128,112},... | collective-permute-start | bytes 12296 | tf_op jit(solution)/shard_map/ppermute | solution.py:393
  103.4 4.3 %collective-permute-start.16 = (f32[8,128]{1,0:T(8,128)S(1)}, f32[8,128]{1,0:T(8,128)S(1)}, u32[]{:S(2)}, u32[]{:S(2)}) collective-permute-start(f32[8,128]{1,0:T(8,128)S(1)} %shard_map.84.rad), channel_id=1, source_target_pairs={{0,16},{16,32},{32,48},{48,64},{64,80},{80,96},{96,112},{112,128},... | collective-permute-start | bytes 12296 | tf_op jit(solution)/shard_map/ppermute | solution.py:393
where the time goes:
time: 109 us
  starting transfers between devices  43.9 us (40%)
  waiting for transfers between devices  33.9 us (31%)
  blocking collectives  21.8 us (20%)
  Pallas kernels  7.72 us (7%)
    ppermute x16, starting transfers between devices, ring(): return (lax.ppermute(high, 'gx', up), lax.ppermute(low, 'gx', down))  27.3 us
    all_to_all x2, blocking collectives, exchange(): return lax.all_to_all(blocks, GY, split_axis=0, concat_axis=0, tiled=True)  21.8 us
    ppermute x16, waiting for transfers between devices, ring(): return (lax.ppermute(high, 'gx', up), lax.ppermute(low, 'gx', down))  15 us
    all_to_all x2, waiting for transfers between devices, exchange(): return lax.all_to_all(blocks, GY, split_axis=0, concat_axis=0, tiled=True)  12.5 us
    all_to_all x2, starting transfers between devices, exchange(): return lax.all_to_all(blocks, GY, split_axis=0, concat_axis=0, tiled=True)  9.71 us
    pallas_call x10, Pallas kernels, run(): pl.pallas_call(kernel, out_shape=[held(shape, dtype) for shape, dtype in...  7.72 us
    ppermute x1, waiting for transfers between devices, step_all(): low = lax.ppermute(own, GY, forward)  6.41 us
    ppermute x1, starting transfers between devices, step_all(): high = lax.ppermute(own, GY, backward)  4.88 us
  transfers between devices with their start and end apart: 20, of which 12 were waited for; matrix products, arithmetic and copies ran while one was open for 1% of the time, Pallas kernels for 1%

commit v1 on v0

--- a/solution.py
+++ b/solution.py
@@ -45,6 +45,9 @@
 PAD = 8
 WIDE = 24
 MID = 16
+BASE_ROW = 5 * 2 * WIDE
+TOWARD = {side: tuple(i for i in range(19) if LATTICE[i][0] == side) for side in (-1, 1)}
+FAR = 9
 
 
 def opposite(direction):
@@ -109,6 +112,47 @@
     return post
 
 
+def relaxed_some(directions, f, rho, u, drive):
+    scaled = RELAX_RATE * rho
+    base = scaled * (1.0 - 1.5 * square(u))
+    force = drive * rho
+    post = []
+    for i, population in zip(directions, f):
+        cu = dot_c(i, u)
+        value = base + scaled * (4.5 * (cu * cu) + 3.0 * cu)
+        if LATTICE[i][2] != 0:
+            value = value + (3.0 * LATTICE[i][2]) * force
+        post.append(WEIGHTS[i] * value + (1.0 - RELAX_RATE) * population)
+    return post
+
+
+def field(ref, k, x, row):
+    return ref[pl.ds((2 * k + x) * WIDE + row, TILE), :]
+
+
+def put_all(out, rows, f):
+    for i in range(19):
+        out[i, rows, :] = f[i]
+
+
+def put_far(out, first, rows, side, f, rho, u):
+    values = [f[i] for i in TOWARD[side]] + [rho] + list(u)
+    for n, value in enumerate(values):
+        out[first + n, rows, :] = value
+
+
+def collide_far(halo, first, side, field_ref, x, row_in_fields, radius, column, n_rows, post):
+    for t in range(n_rows // TILE):
+        rows = pl.ds(t * TILE, TILE)
+        f = [halo[first + n, rows, :] for n in range(5)]
+        rho = halo[first + 5, rows, :]
+        u = [halo[first + 6 + k, rows, :] for k in range(3)]
+        drive = drive_of(radius, field(field_ref, 4, x, row_in_fields + t * TILE))
+        values = relaxed_some(TOWARD[side], f, rho, u, drive)
+        for i, value in zip(TOWARD[side], values):
+            post[i, column, pl.ds(PAD + t * TILE, TILE), :] = value
+
+
 def rolled(x, step):
     if step == 0:
         return x
@@ -170,7 +214,7 @@
     return parts[0]
 
 
-def gather_kernel(place_ref, density, velocity, mask, unit, radius, out, placed):
+def gather_kernel(place_ref, density, velocity, mask, unit, radius, out, send):
     lane = lax.broadcasted_iota(jnp.int32, (TILE, LANES), 1)
     narrow = (TILE, TILE)
     diagonal = lax.broadcasted_iota(jnp.int32, narrow, 0) == lax.broadcasted_iota(jnp.int32, narrow, 1)
@@ -185,30 +229,26 @@
     column = jnp.sum(jnp.where(diagonal, radii, 0.0), axis=1, keepdims=True)
     sub = lax.broadcasted_iota(jnp.int32, (TILE, LANES), 0)
     spread = jnp.where(lane == place_ref[0] * UNIT_DEV + sub, column, 0.0)
-    placed[...] = sublane_total(spread)
-
-
-def rows_kernel(low, own, high, left_out, right_out):
+    send_all(send, sublane_total(spread))
+
+
+def rows_kernel(low, own, high, base_in, left_out, right_out):
+    base = sum_of(base_in)
     for half, out in ((0, left_out), (1, right_out)):
         for k in range(5):
             for x in range(2):
                 for part, ref in enumerate((low, own, high)):
-                    out[k, x, pl.ds(part * TILE, TILE), :] = ref[k, 2 * half + x]
-
-
-def base_kernel(own, left, right, out):
-    sub = lax.broadcasted_iota(jnp.int32, (TILE, LANES), 0)
-    tile = jnp.where(sub == 0, own[...], jnp.where(sub == 1, left[...], right[...]))
-    send_all(out, jnp.where(sub < 3, tile, 0.0))
+                    row = (2 * k + x) * WIDE + part * TILE
+                    out[pl.ds(row, TILE), :] = ref[k, 2 * half + x]
+        out[pl.ds(BASE_ROW, TILE), :] = base
 
 
 def first_kernel(
-    edge_ref, halo_l, left, right, halo_r, base_in, f_l, f_r, bits_out, links_out, send, base_out, post, open_
+    edge_ref, halo_l, left, right, halo_r, f_l, f_r, send_l, send_r, bits_out, links_out, send, base_out, post, open_
 ):
     fields = (halo_l, left, right, halo_r)
-    base = sum_of(base_in)
-    base_out[...] = base
-    radius = [every(base, 1), every(base, 0), every(base, 0), every(base, 2)]
+    radius = [ref[pl.ds(BASE_ROW, TILE), :] for ref in fields]
+    base_out[...] = radius[1]
     lane = lax.broadcasted_iota(jnp.int32, (TILE, LANES), 1)
     for part in range(4):
         inside = None
@@ -223,7 +263,7 @@
                 open_[k, column, pl.ds(0, TILE), :] = zero
                 open_[k, column, pl.ds(PAD + WIDE, TILE), :] = zero
             for t in range(WIDE // TILE):
-                here = (fields[part][0, x, pl.ds(t * TILE, TILE), :] > 0.0).astype(jnp.int32)
+                here = (field(fields[part], 0, x, t * TILE) > 0.0).astype(jnp.int32)
                 if inside is not None:
                     here = here * inside
                 rows = pl.ds(PAD + t * TILE, TILE)
@@ -235,10 +275,9 @@
     for column in range(1, 7):
         part, x = divmod(column, 2)
         for t in range(WIDE // TILE):
-            rows = pl.ds(t * TILE, TILE)
-            rho = fields[part][0, x, rows, :]
-            u = [fields[part][1 + k, x, rows, :] for k in range(3)]
-            drive = drive_of(radius[part], fields[part][4, x, rows, :])
+            rho = field(fields[part], 0, x, t * TILE)
+            u = [field(fields[part], 1 + k, x, t * TILE) for k in range(3)]
+            drive = drive_of(radius[part], field(fields[part], 4, x, t * TILE))
             values = relaxed(None, rho, u, square(u), drive)
             for i in range(19):
                 post[i, column, pl.ds(PAD + t * TILE, TILE), :] = values[i]
@@ -262,17 +301,26 @@
             out = f_l if part == 1 else f_r
             for i in range(19):
                 out[i, x, rows, :] = f[i]
+            fluid = field(fields[part], 0, x, t * TILE) > 0.0
+            if t == 1 or column in (3, 4):
+                rho, u = moments(f, fluid)
+            if column == 2:
+                put_all(send_l, rows, f)
+            elif column == 3:
+                put_far(send_l, 19, rows, -1, f, rho, u)
+            elif column == 4:
+                put_far(send_r, 19, rows, 1, f, rho, u)
+            else:
+                put_all(send_r, rows, f)
             if t != 1:
                 links_out[column - 2, rows, :] = jnp.zeros((TILE, LANES), F32)
                 continue
-            fluid = fields[part][0, x, rows, :] > 0.0
             links = jnp.where(fluid, (18 - count).astype(F32), 0.0)
             links_out[column - 2, rows, :] = links
-            unit = fields[part][4, x, rows, :]
-            u = [fields[part][1 + k, x, rows, :] for k in range(3)]
+            unit = field(fields[part], 4, x, t * TILE)
+            start = [field(fields[part], 1 + k, x, t * TILE) for k in range(3)]
             link_sum = link_sum + by_unit(links, unit)
-            shear_0 = shear_0 + by_unit(links * square(u), unit)
-            _, u = moments(f, fluid)
+            shear_0 = shear_0 + by_unit(links * square(start), unit)
             shear_1 = shear_1 + by_unit(links * square(u), unit)
     send_all(send, row_pick([sublane_total(s) for s in (shear_0, shear_1, link_sum)]))
 
@@ -288,38 +336,53 @@
     radius_out[...] = every(base[...], 0) * (0.6 + 0.8 * jnp.tanh(mean))
 
 
-def collide_from(parts, fields, radius, row_in_fields, columns, n_rows, post):
-    for column in columns:
-        part, x = divmod(column, 2)
-        for t in range(n_rows // TILE):
-            rows = pl.ds(t * TILE, TILE)
-            near = pl.ds(row_in_fields + t * TILE, TILE)
-            f = [parts[part][i, x, rows, :] for i in range(19)]
-            rho, u = moments(f, fields[part][0, x, near, :] > 0.0)
-            drive = drive_of(radius[part], fields[part][4, x, near, :])
-            values = relaxed(f, rho, u, square(u), drive)
-            for i in range(19):
-                post[i, column, pl.ds(PAD + t * TILE, TILE), :] = values[i]
+def collide_all(populations, column, fields, radius, row_in_fields, n_rows, post):
+    part, x = divmod(column, 2)
+    for t in range(n_rows // TILE):
+        rows = pl.ds(t * TILE, TILE)
+        near = row_in_fields + t * TILE
+        f = [populations(i, rows) for i in range(19)]
+        rho, u = moments(f, field(fields[part], 0, x, near) > 0.0)
+        drive = drive_of(radius[part], field(fields[part], 4, x, near))
+        values = relaxed(f, rho, u, square(u), drive)
+        for i in range(19):
+            post[i, column, pl.ds(PAD + t * TILE, TILE), :] = values[i]
+
+
+def in_pair(ref, x):
+    return lambda i, rows: ref[i, x, rows, :]
+
+
+def in_halo(ref):
+    return lambda i, rows: ref[i, rows, :]
 
 
 def two_steps_kernel(
-    h_l, a, b, h_r, g_hl, g_a, g_b, g_hr, bits_in, links_in, rad, rad_l, rad_r, f_l, f_r, send, post_a, post_b, *, n_rows
+    h_l, a, b, h_r, g_hl, g_a, g_b, g_hr, bits_in, links_in, rad, rad_l, rad_r,
+    f_l, f_r, send_l, send_r, send, post_a, post_b, *, n_rows, last_halo,
 ):
-    parts, fields = (h_l, a, b, h_r), (g_hl, g_a, g_b, g_hr)
+    fields = (g_hl, g_a, g_b, g_hr)
     top = (WIDE - n_rows) // 2
     first = [every(r[...], 0) for r in (rad_l, rad, rad, rad_r)]
     second = [every(r[...], 1) for r in (rad_l, rad, rad, rad_r)]
-    collide_from(parts, fields, first, top, range(8), n_rows, post_a)
+    for column in range(2, 6):
+        source = in_pair(a if column < 4 else b, column % 2)
+        collide_all(source, column, fields, first, top, n_rows, post_a)
+    collide_all(in_halo(h_l), 1, fields, first, top, n_rows, post_a)
+    collide_all(in_halo(h_r), 6, fields, first, top, n_rows, post_a)
+    collide_far(h_l, 19, 1, g_hl, 0, top, first[0], 0, n_rows, post_a)
+    collide_far(h_r, 19, -1, g_hr, 1, top, first[3], 7, n_rows, post_a)
     shear_a = shear_b = jnp.zeros((TILE, LANES), F32)
     skip = (n_rows - MID) // 2
     for column in range(1, 7):
         part, x = divmod(column, 2)
         for t in range(MID // TILE):
-            near = pl.ds((WIDE - MID) // 2 + t * TILE, TILE)
+            row = (WIDE - MID) // 2 + t * TILE
+            near = pl.ds(row, TILE)
             f = pulled(post_a, column, PAD + skip + t * TILE, bits_in[column - 1, near, :])
-            rho, u = moments(f, fields[part][0, x, near, :] > 0.0)
+            rho, u = moments(f, field(fields[part], 0, x, row) > 0.0)
             speed_sq = square(u)
-            unit = fields[part][4, x, near, :]
+            unit = field(fields[part], 4, x, row)
             if part in (1, 2):
                 shear_a = shear_a + by_unit(shear(links_in[column - 2, near, :], speed_sq), unit)
             values = relaxed(f, rho, u, speed_sq, drive_of(second[part], unit))
@@ -329,13 +392,28 @@
         part, x = divmod(column, 2)
         out = f_l if part == 1 else f_r
         for t in range(MID // TILE):
-            near = pl.ds((WIDE - MID) // 2 + t * TILE, TILE)
+            row = (WIDE - MID) // 2 + t * TILE
+            near = pl.ds(row, TILE)
+            rows = pl.ds(t * TILE, TILE)
             f = pulled(post_b, column, PAD + t * TILE, bits_in[column - 1, near, :])
             for i in range(19):
-                out[i, x, pl.ds(t * TILE, TILE), :] = f[i]
-            _, u = moments(f, fields[part][0, x, near, :] > 0.0)
+                out[i, x, rows, :] = f[i]
+            rho, u = moments(f, field(fields[part], 0, x, row) > 0.0)
+            if last_halo:
+                if column == 2:
+                    put_far(send_l, 0, rows, -1, f, rho, u)
+                elif column == 5:
+                    put_far(send_r, 0, rows, 1, f, rho, u)
+            elif column == 2:
+                put_all(send_l, rows, f)
+            elif column == 3:
+                put_far(send_l, 19, rows, -1, f, rho, u)
+            elif column == 4:
+                put_far(send_r, 19, rows, 1, f, rho, u)
+            else:
+                put_all(send_r, rows, f)
             shear_b = shear_b + by_unit(
-                shear(links_in[column - 2, near, :], square(u)), fields[part][4, x, near, :]
+                shear(links_in[column - 2, near, :], square(u)), field(fields[part], 4, x, row)
             )
     send_all(send, row_pick([sublane_total(s) for s in (shear_a, shear_b)]))
 
@@ -343,14 +421,19 @@
 def last_kernel(
     h_l, a, b, h_r, g_hl, g_a, g_b, g_hr, bits_in, rad, rad_l, rad_r, density, velocity, post
 ):
-    parts, fields = (h_l, a, b, h_r), (g_hl, g_a, g_b, g_hr)
+    fields = (g_hl, g_a, g_b, g_hr)
     radius = [every(r[...], 0) for r in (rad_l, rad, rad, rad_r)]
-    collide_from(parts, fields, radius, (WIDE - MID) // 2, range(1, 7), MID, post)
+    top = (WIDE - MID) // 2
+    for column in range(2, 6):
+        source = in_pair(a if column < 4 else b, column % 2)
+        collide_all(source, column, fields, radius, top, MID, post)
+    collide_far(h_l, 0, 1, g_hl, 1, top, radius[0], 1, MID, post)
+    collide_far(h_r, 0, -1, g_hr, 0, top, radius[3], 6, MID, post)
     own = pl.ds(TILE, TILE)
     for column in range(2, 6):
         part, x = divmod(column, 2)
         f = pulled(post, column, PAD + (MID - TILE) // 2, bits_in[column - 1, own, :])
-        rho, u = moments(f, fields[part][0, x, own, :] > 0.0)
+        rho, u = moments(f, field(fields[part], 0, x, TILE) > 0.0)
         density[column - 2] = rho
         for k in range(3):
             velocity[k, column - 2] = u[k]
@@ -395,31 +478,31 @@
     def exchange(blocks):
         return lax.all_to_all(blocks, GY, split_axis=0, concat_axis=0, tiled=True)
 
-    own, placed = call(
-        gather_kernel, [((5, 4, TILE, LANES), F32), tile], scalars=1, plain_in=True
+    own, base_send = call(
+        gather_kernel, [((5, 4, TILE, LANES), F32), sends], scalars=1, plain_in=True
     )(place.reshape(1), density, velocity, fluid_mask, unit_of_column, radius_base.reshape(1, -1))
-
-    base_l, base_r = ring(placed, placed)
-    (base_send,) = call(base_kernel, [sends])(placed, base_l, base_r)
     base_in = exchange(base_send)
 
     forward = [(i, i + 1) for i in range(count - 1)]
     backward = [(target, source) for source, target in forward]
     low = lax.ppermute(own, GY, forward)
     high = lax.ppermute(own, GY, backward)
-    pair = ((5, 2, WIDE, LANES), F32)
-    g_l, g_r = call(rows_kernel, [pair, pair])(low, own, high)
+    pair = ((BASE_ROW + TILE, LANES), F32)
+    g_l, g_r = call(rows_kernel, [pair, pair])(low, own, high, base_in)
     g_hl, g_hr = ring(g_l, g_r)
     fields = (g_hl, g_l, g_r, g_hr)
 
     def populations(rows):
-        return ((19, 2, rows, LANES), F32)
-
-    f_l, f_r, bits, links, send, base = call(
+        return [((19, 2, rows, LANES), F32)] * 2
+
+    def halos(rows, last=False):
+        return [((FAR if last else 19 + FAR, rows, LANES), F32)] * 2
+
+    f_l, f_r, send_l, send_r, bits, links, send, base = call(
         first_kernel,
         [
-            populations(WIDE),
-            populations(WIDE),
+            *populations(WIDE),
+            *halos(WIDE),
             ((6, WIDE, LANES), jnp.int32),
             ((4, WIDE, LANES), F32),
             sends,
@@ -428,11 +511,11 @@
         [((19, 8, WIDE + 2 * PAD, LANES), F32), ((3, 8, WIDE + 2 * PAD, LANES), jnp.int32)],
         scalars=1,
         mib=6,
-    )(edge, *fields, base_in)
+    )(edge, *fields)
 
     for turn in range(3):
         gathered = exchange(send)
-        h_l, h_r = ring(f_l, f_r)
+        h_l, h_r = ring(send_l, send_r)
         if turn == 0:
             rad, link_tile = call(response_kernel, [tile, tile])(gathered, base, base)
         else:
@@ -441,9 +524,9 @@
         parts = (h_l, f_l, f_r, h_r)
         if turn < 2:
             rows = WIDE if turn == 0 else MID
-            f_l, f_r, send = call(
-                functools.partial(two_steps_kernel, n_rows=rows),
-                [populations(MID), populations(MID), sends],
+            f_l, f_r, send_l, send_r, send = call(
+                functools.partial(two_steps_kernel, n_rows=rows, last_halo=turn == 1),
+                [*populations(MID), *halos(MID, last=turn == 1), sends],
                 [
                     ((19, 8, rows + 2 * PAD, LANES), F32),
                     ((19, 8, MID + 2 * PAD, LANES), F32),

time: 109 us -> 98.2 us (0.901)
  blocking collectives: 21.8 us -> 43 us
  waiting for transfers between devices: 33.9 us -> 16.6 us
  starting transfers between devices: 43.9 us -> 29.9 us
    all_to_all x2 -> x3, blocking collectives: 21.8 us -> 43 us  [exchange(): return lax.all_to_all(blocks, GY, split_axis=0, concat_axis=0, tiled=True)]
    all_to_all x2 -> x1, waiting for transfers between devices: 12.5 us -> 3.33 us  [exchange(): return lax.all_to_all(blocks, GY, split_axis=0, concat_axis=0, tiled=True)]
    ppermute x16 -> x14, starting transfers between devices: 27.3 us -> 18.3 us  [ring(): return (lax.ppermute(high, 'gx', up), lax.ppermute(low, 'gx', down))]
    ppermute x1, waiting for transfers between devices: 6.41 us -> 0.01 us  [step_all(): low = lax.ppermute(own, GY, forward)]
    all_to_all x2 -> x1, starting transfers between devices: 9.71 us -> 4.83 us  [exchange(): return lax.all_to_all(blocks, GY, split_axis=0, concat_axis=0, tiled=True)]
    ppermute x16 -> x14, waiting for transfers between devices: 15 us -> 13.2 us  [ring(): return (lax.ppermute(high, 'gx', up), lax.ppermute(low, 'gx', down))]
    pallas_call x10 -> x9, Pallas kernels: 7.72 us -> 7 us  [run(): pl.pallas_call(kernel, out_shape=[held(shape, dtype) for shape, dtype in...]
  transfers between devices with their start and end apart: 20 -> 17, of which waited for: 12 -> 8; matrix products, arithmetic and copies ran while one was open for 1% -> 1% of each run, Pallas kernels for 1% -> 0%
where the time goes in v1:
time: 98.2 us; the launch traced here: 97.9 us
  blocking collectives  43 us (44%)
  starting transfers between devices  29.9 us (30%)
  waiting for transfers between devices  16.6 us (17%)
  Pallas kernels  7 us (7%)
    all_to_all x3, blocking collectives, exchange(): return lax.all_to_all(blocks, GY, split_axis=0, concat_axis=0, tiled=True)  43 us
    ppermute x14, starting transfers between devices, ring(): return (lax.ppermute(high, 'gx', up), lax.ppermute(low, 'gx', down))  18.3 us
    ppermute x14, waiting for transfers between devices, ring(): return (lax.ppermute(high, 'gx', up), lax.ppermute(low, 'gx', down))  13.2 us
    pallas_call x9, Pallas kernels, run(): pl.pallas_call(kernel, out_shape=[held(shape, dtype) for shape, dtype in...  7 us
    ppermute x1, starting transfers between devices, step_all(): high = lax.ppermute(own, GY, backward)  4.89 us
    all_to_all x1, starting transfers between devices, exchange(): return lax.all_to_all(blocks, GY, split_axis=0, concat_axis=0, tiled=True)  4.83 us
    all_to_all x1, waiting for transfers between devices, exchange(): return lax.all_to_all(blocks, GY, split_axis=0, concat_axis=0, tiled=True)  3.33 us
  transfers between devices with their start and end apart: 17, of which 8 were waited for; matrix products, arithmetic and copies ran while one was open for 1% of the time, Pallas kernels for 0%

profile of v1, /device:TPU:2, one launch (start us, length us, event | category | flops | bytes accessed | tf_op | source)
XLA Modules:
  0.0 97.9 jit_solution(9277749845186329626)
XLA Ops:
  0.6 0.9 shard_map.76
  1.5 4.9 %collective-permute-start.1 = (f32[5,4,8,128]{3,2,1,0:T(8,128)S(1)}, f32[5,4,8,128]{3,2,1,0:T(8,128)S(1)}, u32[]{:S(2)}, u32[]{:S(2)}) collective-permute-start(f32[5,4,8,128]{3,2,1,0:T(8,128)S(1)} %get-tuple-element.29.own), channel_id=1, source_target_pairs={{1,0},{2,1},{3,2},{4,3},{5,4},{6,5},{7,6},{8,7},{9,8},{10,9},{11,1... | collective-permute-start | bytes 245768 | tf_op jit(solution)/shard_map/ppermute | solution.py:489
  6.4 1.9 %collective-permute-start = (f32[5,4,8,128]{3,2,1,0:T(8,128)S(1)}, f32[5,4,8,128]{3,2,1,0:T(8,128)S(1)}, u32[]{:S(2)}, u32[]{:S(2)}) collective-permute-start(f32[5,4,8,128]{3,2,1,0:T(8,128)S(1)} %get-tuple-element.29.own), channel_id=1, source_target_pairs={{0,1},{1,2},{2,3},{3,4},{4,5},{5,6},{6,7},{7,8},{8,9},{9,10},{10,1... | collective-permute-start | bytes 245768 | tf_op jit(solution)/shard_map/ppermute | solution.py:488
  8.4 20.9 %all_to_all.20.base_in = f32[16,8,128]{2,1,0:T(8,128)S(1)} all-to-all(f32[16,8,128]{2,1,0:T(8,128)S(1)} %get-tuple-element.30), channel_id=1, replica_groups=mesh['gx'=64,'gy_0'=4,'gy_1'=4] {'gy_0','gy_1'}, dimensions={0} | all-to-all | bytes 131072 | tf_op jit(solution)/shard_map/all_to_all | solution.py:479
  29.4 7.8 %collective-permute-start.3 = (f32[248,128]{1,0:T(8,128)S(1)}, f32[248,128]{1,0:T(8,128)S(1)}, u32[]{:S(2)}, u32[]{:S(2)}) collective-permute-start(f32[248,128]{1,0:T(8,128)S(1)} %get-tuple-element.32.left.g_a), channel_id=1, source_target_pairs={{16,0},{32,16},{48,32},{64,48},{80,64},{96,80},{112,96},{128,112},... | collective-permute-start | bytes 380936 | tf_op jit(solution)/shard_map/ppermute | solution.py:476
  37.2 2.5 %collective-permute-done.2.halo_l.g_hl = f32[248,128]{1,0:T(8,128)S(1)} collective-permute-done((f32[248,128]{1,0:T(8,128)S(1)}, f32[248,128]{1,0:T(8,128)S(1)}, u32[]{:S(2)}, u32[]{:S(2)}) %collective-permute-start.2) | collective-permute-done | bytes 127008 | tf_op jit(solution)/shard_map/ppermute | solution.py:476
  39.7 1.3 %shard_map.78 = (f32[19,2,24,128]{3,2,1,0:T(8,128)S(1)}, f32[19,2,24,128]{3,2,1,0:T(8,128)S(1)}, f32[28,24,128]{2,1,0:T(8,128)S(1)}, f32[28,24,128]{2,1,0:T(8,12...) custom-call(s32[2]{0:T(128)S(1)} %add_convert_fusion.edge_ref, ...), custom_call_target="tpu_custom_call" | custom-call | tf_op jit(solution)/shard_map/pallas_call | solution.py:452
  41.0 3.0 %collective-permute-start.5 = (f32[28,24,128]{2,1,0:T(8,128)S(1)}, f32[28,24,128]{2,1,0:T(8,128)S(1)}, u32[]{:S(2)}, u32[]{:S(2)}) collective-permute-start(f32[28,24,128]{2,1,0:T(8,128)S(1)} %get-tuple-element.36), channel_id=1, source_target_pairs={{16,0},{32,16},{48,32},{64,48},{80,64},{96,80},{112,96},{128,112},... | collective-permute-start | bytes 1032200 | tf_op jit(solution)/shard_map/ppermute | solution.py:476
  44.0 11.2 %all_to_all.21.gathered = f32[16,8,128]{2,1,0:T(8,128)S(1)} all-to-all(f32[16,8,128]{2,1,0:T(8,128)S(1)} %get-tuple-element.39), channel_id=1, replica_groups=mesh['gx'=64,'gy_0'=4,'gy_1'=4] {'gy_0','gy_1'}, dimensions={0} | all-to-all | bytes 131072 | tf_op jit(solution)/shard_map/all_to_all | solution.py:479
  55.2 0.5 collective-permute-start.6
  55.7 0.8 collective-permute-done.7.rad_r
  56.6 2.9 %collective-permute-done.6.rad_l = f32[8,128]{1,0:T(8,128)S(1)} collective-permute-done((f32[8,128]{1,0:T(8,128)S(1)}, f32[8,128]{1,0:T(8,128)S(1)}, u32[]{:S(2)}, u32[]{:S(2)}) %collective-permute-start.6) | collective-permute-done | bytes 4128 | tf_op jit(solution)/shard_map/ppermute | solution.py:476
  59.5 1.7 %shard_map.80 = (f32[19,2,16,128]{3,2,1,0:T(8,128)S(1)}, f32[19,2,16,128]{3,2,1,0:T(8,128)S(1)}, f32[28,16,128]{2,1,0:T(8,128)S(1)}, f32[28,16,128]{2,1,0:T(8,128)S(1)}, f32[16,8,128]{2,1,0:T(8,128)S(1)}) custom-call(f32[28,24,128]{2,1,0:T(8,128)S(1)} %collective-permute-done.4.h_l, f32[19,2,24,128]{3,2,1,0:T(8,128)S(1)} %get-tuple-element.34.a, ...), custom_call_target="tpu_custom_call" | custom-call | tf_op jit(solution)/shard_map/pallas_call | solution.py:452
  61.2 2.9 %collective-permute-start.9 = (f32[28,16,128]{2,1,0:T(8,128)S(1)}, f32[28,16,128]{2,1,0:T(8,128)S(1)}, u32[]{:S(2)}, u32[]{:S(2)}) collective-permute-start(f32[28,16,128]{2,1,0:T(8,128)S(1)} %get-tuple-element.45), channel_id=1, source_target_pairs={{16,0},{32,16},{48,32},{64,48},{80,64},{96,80},{112,96},{128,112},... | collective-permute-start | bytes 688136 | tf_op jit(solution)/shard_map/ppermute | solution.py:476
  64.1 10.9 %all_to_all.22.gathered = f32[16,8,128]{2,1,0:T(8,128)S(1)} all-to-all(f32[16,8,128]{2,1,0:T(8,128)S(1)} %get-tuple-element.46), channel_id=1, replica_groups=mesh['gx'=64,'gy_0'=4,'gy_1'=4] {'gy_0','gy_1'}, dimensions={0} | all-to-all | bytes 131072 | tf_op jit(solution)/shard_map/all_to_all | solution.py:479
  75.5 0.8 collective-permute-done.11.rad_r
  76.4 2.9 %collective-permute-done.10.rad_l = f32[8,128]{1,0:T(8,128)S(1)} collective-permute-done((f32[8,128]{1,0:T(8,128)S(1)}, f32[8,128]{1,0:T(8,128)S(1)}, u32[]{:S(2)}, u32[]{:S(2)}) %collective-permute-start.10) | collective-permute-done | bytes 4128 | tf_op jit(solution)/shard_map/ppermute | solution.py:476
  79.3 2.1 %shard_map.82 = (f32[19,2,16,128]{3,2,1,0:T(8,128)S(1)}, f32[19,2,16,128]{3,2,1,0:T(8,128)S(1)}, f32[9,16,128]{2,1,0:T(8,128)S(1)}, f32[9,16,128]{2,1,0:T(8,128)S(1)}, f32[16,8,128]{2,1,0:T(8,128)}) custom-call(f32[28,16,128]{2,1,0:T(8,128)S(1)} %collective-permute-done.8.h_l, f32[19,2,16,128]{3,2,1,0:T(8,128)S(1)} %get-tuple-element.43.a, ...), custom_call_target="tpu_custom_call" | custom-call | tf_op jit(solution)/shard_map/pallas_call | solution.py:452
  81.4 4.8 %all-to-all-start.3 = ((f32[16,8,128]{2,1,0:T(8,128)}), f32[16,8,128]{2,1,0:T(8,128)S(1)}, u32[]{:S(2)}, u32[]{:S(2)}) async-start(f32[16,8,128]{2,1,0:T(8,128)} %get-tuple-element.52), calls=%async_computation.3 | async-start | bytes 131072 | tf_op jit(solution)/shard_map/all_to_all | solution.py:479
  86.2 2.9 %collective-permute-start.13 = (f32[9,16,128]{2,1,0:T(8,128)S(1)}, f32[9,16,128]{2,1,0:T(8,128)S(1)}, u32[]{:S(2)}, u32[]{:S(2)}) collective-permute-start(f32[9,16,128]{2,1,0:T(8,128)S(1)} %get-tuple-element.51), channel_id=1, source_target_pairs={{16,0},{32,16},{48,32},{64,48},{80,64},{96,80},{112,96},{128,112},... | collective-permute-start | bytes 221192 | tf_op jit(solution)/shard_map/ppermute | solution.py:476
  89.2 3.3 %all-to-all-done.3.gathered = f32[16,8,128]{2,1,0:T(8,128)S(1)} async-done(((f32[16,8,128]{2,1,0:T(8,128)}), f32[16,8,128]{2,1,0:T(8,128)S(1)}, u32[]{:S(2)}, u32[]{:S(2)}) %all-to-all-start.3) | async-done | bytes 65568 | tf_op jit(solution)/shard_map/all_to_all | solution.py:479
  93.1 0.6 dynamic-slice_bitcast_fusion
  93.9 2.9 %collective-permute-done.14.rad_l = f32[8,128]{1,0:T(8,128)S(1)} collective-permute-done((f32[8,128]{1,0:T(8,128)S(1)}, f32[8,128]{1,0:T(8,128)S(1)}, u32[]{:S(2)}, u32[]{:S(2)}) %collective-permute-start.14) | collective-permute-done | bytes 4128 | tf_op jit(solution)/shard_map/ppermute | solution.py:476
  96.8 1.0 %shard_map.84 = (f32[4,8,128]{2,1,0:T(8,128)}, f32[3,4,8,128]{3,2,1,0:T(8,128)}) custom-call(f32[9,16,128]{2,1,0:T(8,128)S(1)} %collective-permute-done.12.h_l, f32[19,2,16,128]{3,2,1,0:T(8,128)S(1)} %get-tuple-element.49.a, f32[19,2,16,128]{3,2,1,0:T(8,128)S(1)} %get-tuple-element.50.b, f32[9,16,128]{2,1,0:T(8,128)S(1)} %collective-permute-done.13.h_r, ...), custom_call_target="tpu_custom_call" | custom-call | tf_op jit(solution)/shard_map/pallas_call | solution.py:452
  (25 shorter events, 1.5 us)
Async XLA Ops:
  1.5 27.8 %collective-permute-start.1 = (f32[5,4,8,128]{3,2,1,0:T(8,128)S(1)}, f32[5,4,8,128]{3,2,1,0:T(8,128)S(1)}, u32[]{:S(2)}, u32[]{:S(2)}) collective-permute-start(f32[5,4,8,128]{3,2,1,0:T(8,128)S(1)} %get-tuple-element.29.own), channel_id=1, source_target_pairs={{1,0},{2,1},{3,2},{4,3},{5,4},{6,5},{7,6},{8,7},{9,8},{10,9},{11,1... | collective-permute-start | bytes 245768 | tf_op jit(solution)/shard_map/ppermute | solution.py:489
  6.4 22.9 %collective-permute-start = (f32[5,4,8,128]{3,2,1,0:T(8,128)S(1)}, f32[5,4,8,128]{3,2,1,0:T(8,128)S(1)}, u32[]{:S(2)}, u32[]{:S(2)}) collective-permute-start(f32[5,4,8,128]{3,2,1,0:T(8,128)S(1)} %get-tuple-element.29.own), channel_id=1, source_target_pairs={{0,1},{1,2},{2,3},{3,4},{4,5},{5,6},{6,7},{7,8},{8,9},{9,10},{10,1... | collective-permute-start | bytes 245768 | tf_op jit(solution)/shard_map/ppermute | solution.py:488
  29.3 10.4 %collective-permute-start.2 = (f32[248,128]{1,0:T(8,128)S(1)}, f32[248,128]{1,0:T(8,128)S(1)}, u32[]{:S(2)}, u32[]{:S(2)}) collective-permute-start(f32[248,128]{1,0:T(8,128)S(1)} %get-tuple-element.31.right.g_b), channel_id=1, source_target_pairs={{0,16},{16,32},{32,48},{48,64},{64,80},{80,96},{96,112},{112,128},... | collective-permute-start | bytes 380936 | tf_op jit(solution)/shard_map/ppermute | solution.py:476
  29.4 10.4 %collective-permute-start.3 = (f32[248,128]{1,0:T(8,128)S(1)}, f32[248,128]{1,0:T(8,128)S(1)}, u32[]{:S(2)}, u32[]{:S(2)}) collective-permute-start(f32[248,128]{1,0:T(8,128)S(1)} %get-tuple-element.32.left.g_a), channel_id=1, source_target_pairs={{16,0},{32,16},{48,32},{64,48},{80,64},{96,80},{112,96},{128,112},... | collective-permute-start | bytes 380936 | tf_op jit(solution)/shard_map/ppermute | solution.py:476
  41.0 18.5 %collective-permute-start.4 = (f32[28,24,128]{2,1,0:T(8,128)S(1)}, f32[28,24,128]{2,1,0:T(8,128)S(1)}, u32[]{:S(2)}, u32[]{:S(2)}) collective-permute-start(f32[28,24,128]{2,1,0:T(8,128)S(1)} %get-tuple-element.33), channel_id=1, source_target_pairs={{0,16},{16,32},{32,48},{48,64},{64,80},{80,96},{96,112},{112,128},... | collective-permute-start | bytes 1032200 | tf_op jit(solution)/shard_map/ppermute | solution.py:476
  41.0 18.5 %collective-permute-start.5 = (f32[28,24,128]{2,1,0:T(8,128)S(1)}, f32[28,24,128]{2,1,0:T(8,128)S(1)}, u32[]{:S(2)}, u32[]{:S(2)}) collective-permute-start(f32[28,24,128]{2,1,0:T(8,128)S(1)} %get-tuple-element.36), channel_id=1, source_target_pairs={{16,0},{32,16},{48,32},{64,48},{80,64},{96,80},{112,96},{128,112},... | collective-permute-start | bytes 1032200 | tf_op jit(solution)/shard_map/ppermute | solution.py:476
  55.2 1.3 %collective-permute-start.7 = (f32[8,128]{1,0:T(8,128)S(1)}, f32[8,128]{1,0:T(8,128)S(1)}, u32[]{:S(2)}, u32[]{:S(2)}) collective-permute-start(f32[8,128]{1,0:T(8,128)S(1)} %get-tuple-element.41.rad), channel_id=1, source_target_pairs={{16,0},{32,16},{48,32},{64,48},{80,64},{96,80},{112,96},{128,112},... | collective-permute-start | bytes 12296 | tf_op jit(solution)/shard_map/ppermute | solution.py:476
  55.2 4.3 %collective-permute-start.6 = (f32[8,128]{1,0:T(8,128)S(1)}, f32[8,128]{1,0:T(8,128)S(1)}, u32[]{:S(2)}, u32[]{:S(2)}) collective-permute-start(f32[8,128]{1,0:T(8,128)S(1)} %get-tuple-element.41.rad), channel_id=1, source_target_pairs={{0,16},{16,32},{32,48},{48,64},{64,80},{80,96},{96,112},{112,128},... | collective-permute-start | bytes 12296 | tf_op jit(solution)/shard_map/ppermute | solution.py:476
  61.2 18.1 %collective-permute-start.8 = (f32[28,16,128]{2,1,0:T(8,128)S(1)}, f32[28,16,128]{2,1,0:T(8,128)S(1)}, u32[]{:S(2)}, u32[]{:S(2)}) collective-permute-start(f32[28,16,128]{2,1,0:T(8,128)S(1)} %get-tuple-element.42), channel_id=1, source_target_pairs={{0,16},{16,32},{32,48},{48,64},{64,80},{80,96},{96,112},{112,128},... | collective-permute-start | bytes 688136 | tf_op jit(solution)/shard_map/ppermute | solution.py:476
  61.2 18.1 %collective-permute-start.9 = (f32[28,16,128]{2,1,0:T(8,128)S(1)}, f32[28,16,128]{2,1,0:T(8,128)S(1)}, u32[]{:S(2)}, u32[]{:S(2)}) collective-permute-start(f32[28,16,128]{2,1,0:T(8,128)S(1)} %get-tuple-element.45), channel_id=1, source_target_pairs={{16,0},{32,16},{48,32},{64,48},{80,64},{96,80},{112,96},{128,112},... | collective-permute-start | bytes 688136 | tf_op jit(solution)/shard_map/ppermute | solution.py:476
  75.0 1.3 %collective-permute-start.11 = (f32[8,128]{1,0:T(8,128)S(1)}, f32[8,128]{1,0:T(8,128)S(1)}, u32[]{:S(2)}, u32[]{:S(2)}) collective-permute-start(f32[8,128]{1,0:T(8,128)S(1)} %shard_map.81.rad), channel_id=1, source_target_pairs={{16,0},{32,16},{48,32},{64,48},{80,64},{96,80},{112,96},{128,112},... | collective-permute-start | bytes 12296 | tf_op jit(solution)/shard_map/ppermute | solution.py:476
  75.0 4.3 %collective-permute-start.10 = (f32[8,128]{1,0:T(8,128)S(1)}, f32[8,128]{1,0:T(8,128)S(1)}, u32[]{:S(2)}, u32[]{:S(2)}) collective-permute-start(f32[8,128]{1,0:T(8,128)S(1)} %shard_map.81.rad), channel_id=1, source_target_pairs={{0,16},{16,32},{32,48},{48,64},{64,80},{80,96},{96,112},{112,128},... | collective-permute-start | bytes 12296 | tf_op jit(solution)/shard_map/ppermute | solution.py:476
  81.4 11.1 %all-to-all-start.3 = ((f32[16,8,128]{2,1,0:T(8,128)}), f32[16,8,128]{2,1,0:T(8,128)S(1)}, u32[]{:S(2)}, u32[]{:S(2)}) async-start(f32[16,8,128]{2,1,0:T(8,128)} %get-tuple-element.52), calls=%async_computation.3 | async-start | bytes 131072 | tf_op jit(solution)/shard_map/all_to_all | solution.py:479
  86.2 10.6 %collective-permute-start.12 = (f32[9,16,128]{2,1,0:T(8,128)S(1)}, f32[9,16,128]{2,1,0:T(8,128)S(1)}, u32[]{:S(2)}, u32[]{:S(2)}) collective-permute-start(f32[9,16,128]{2,1,0:T(8,128)S(1)} %get-tuple-element.48), channel_id=1, source_target_pairs={{0,16},{16,32},{32,48},{48,64},{64,80},{80,96},{96,112},{112,128},... | collective-permute-start | bytes 221192 | tf_op jit(solution)/shard_map/ppermute | solution.py:476
  86.2 10.6 %collective-permute-start.13 = (f32[9,16,128]{2,1,0:T(8,128)S(1)}, f32[9,16,128]{2,1,0:T(8,128)S(1)}, u32[]{:S(2)}, u32[]{:S(2)}) collective-permute-start(f32[9,16,128]{2,1,0:T(8,128)S(1)} %get-tuple-element.51), channel_id=1, source_target_pairs={{16,0},{32,16},{48,32},{64,48},{80,64},{96,80},{112,96},{128,112},... | collective-permute-start | bytes 221192 | tf_op jit(solution)/shard_map/ppermute | solution.py:476
  92.6 1.3 %collective-permute-start.15 = (f32[8,128]{1,0:T(8,128)S(1)}, f32[8,128]{1,0:T(8,128)S(1)}, u32[]{:S(2)}, u32[]{:S(2)}) collective-permute-start(f32[8,128]{1,0:T(8,128)S(1)} %shard_map.83.rad), channel_id=1, source_target_pairs={{16,0},{32,16},{48,32},{64,48},{80,64},{96,80},{112,96},{128,112},... | collective-permute-start | bytes 12296 | tf_op jit(solution)/shard_map/ppermute | solution.py:476
  92.6 4.3 %collective-permute-start.14 = (f32[8,128]{1,0:T(8,128)S(1)}, f32[8,128]{1,0:T(8,128)S(1)}, u32[]{:S(2)}, u32[]{:S(2)}) collective-permute-start(f32[8,128]{1,0:T(8,128)S(1)} %shard_map.83.rad), channel_id=1, source_target_pairs={{0,16},{16,32},{32,48},{48,64},{64,80},{80,96},{96,112},{112,128},... | collective-permute-start | bytes 12296 | tf_op jit(solution)/shard_map/ppermute | solution.py:476

commit v2 on v1

--- a/solution.py
+++ b/solution.py
@@ -141,7 +141,7 @@
         out[first + n, rows, :] = value
 
 
-def collide_far(halo, first, side, field_ref, x, row_in_fields, radius, column, n_rows, post):
+def collide_far(halo, first, side, field_ref, x, row_in_fields, radius, n_rows, post, slot):
     for t in range(n_rows // TILE):
         rows = pl.ds(t * TILE, TILE)
         f = [halo[first + n, rows, :] for n in range(5)]
@@ -150,7 +150,7 @@
         drive = drive_of(radius, field(field_ref, 4, x, row_in_fields + t * TILE))
         values = relaxed_some(TOWARD[side], f, rho, u, drive)
         for i, value in zip(TOWARD[side], values):
-            post[i, column, pl.ds(PAD + t * TILE, TILE), :] = value
+            post[i, slot, pl.ds(PAD + t * TILE, TILE), :] = value
 
 
 def rolled(x, step):
@@ -159,12 +159,16 @@
     return pltpu.roll(x, step % LANES, axis=1)
 
 
-def pulled(post_ref, column, row, bits):
-    f = [post_ref[0, column, pl.ds(row, TILE), :]]
+def pulled(held, column, row, bits):
+    def load(i, at_column, at_row):
+        ref, slot = held[at_column]
+        return ref[i, slot, pl.ds(at_row, TILE), :]
+
+    f = [load(0, column, row)]
     for i in range(1, 19):
         cx, cy, cz = LATTICE[i]
-        source = rolled(post_ref[i, column - cx, pl.ds(row - cy, TILE), :], cz)
-        bounced = post_ref[opposite(i), column, pl.ds(row, TILE), :]
+        source = rolled(load(i, column - cx, row - cy), cz)
+        bounced = load(opposite(i), column, row)
         f.append(jnp.where((bits & (1 << i)) != 0, source, bounced))
     return f
 
@@ -214,22 +218,34 @@
     return parts[0]
 
 
-def gather_kernel(place_ref, density, velocity, mask, unit, radius, out, send):
+def gather_kernel(
+    place_ref, density, velocity, mask, unit, radius, out, send, density_v, velocity_v, mask_v, unit_v, radius_v, send_v, sems
+):
+    pairs = ((radius, radius_v), (density, density_v), (velocity, velocity_v), (mask, mask_v), (unit, unit_v))
+    loads = [pltpu.make_async_copy(a, b, sems.at[n]) for n, (a, b) in enumerate(pairs)]
+    for load in loads:
+        load.start()
     lane = lax.broadcasted_iota(jnp.int32, (TILE, LANES), 1)
     narrow = (TILE, TILE)
     diagonal = lax.broadcasted_iota(jnp.int32, narrow, 0) == lax.broadcasted_iota(jnp.int32, narrow, 1)
-    for x in range(4):
-        out[0, x] = jnp.where(mask[x] != 0, density[x], 0.0)
-        for k in range(3):
-            out[1 + k, x] = velocity[k, x]
-        units = jnp.broadcast_to(unit[x : x + 1, :].astype(F32), narrow)
-        column = jnp.sum(jnp.where(diagonal, units, 0.0), axis=1, keepdims=True)
-        out[4, x] = jnp.broadcast_to(column, (TILE, LANES))
-    radii = jnp.broadcast_to(radius[...], narrow)
+    loads[0].wait()
+    radii = jnp.broadcast_to(radius_v[...], narrow)
     column = jnp.sum(jnp.where(diagonal, radii, 0.0), axis=1, keepdims=True)
     sub = lax.broadcasted_iota(jnp.int32, (TILE, LANES), 0)
     spread = jnp.where(lane == place_ref[0] * UNIT_DEV + sub, column, 0.0)
-    send_all(send, sublane_total(spread))
+    send_all(send_v, sublane_total(spread))
+    store = pltpu.make_async_copy(send_v, send, sems.at[5])
+    store.start()
+    for load in loads[1:]:
+        load.wait()
+    for x in range(4):
+        out[0, x] = jnp.where(mask_v[x] != 0, density_v[x], 0.0)
+        for k in range(3):
+            out[1 + k, x] = velocity_v[k, x]
+        units = jnp.broadcast_to(unit_v[x : x + 1, :].astype(F32), narrow)
+        column = jnp.sum(jnp.where(diagonal, units, 0.0), axis=1, keepdims=True)
+        out[4, x] = jnp.broadcast_to(column, (TILE, LANES))
+    store.wait()
 
 
 def rows_kernel(low, own, high, base_in, left_out, right_out):
@@ -243,44 +259,54 @@
         out[pl.ds(BASE_ROW, TILE), :] = base
 
 
+def mark_open(open_, slot, column_fields, x, inside):
+    lane = lax.broadcasted_iota(jnp.int32, (TILE, LANES), 1)
+    zero = jnp.zeros((TILE, LANES), jnp.int32)
+    for k in range(3):
+        open_[k, slot, pl.ds(0, TILE), :] = zero
+        open_[k, slot, pl.ds(PAD + WIDE, TILE), :] = zero
+    for t in range(WIDE // TILE):
+        here = (field(column_fields, 0, x, t * TILE) > 0.0).astype(jnp.int32)
+        if inside is not None:
+            here = here * inside
+        rows = pl.ds(PAD + t * TILE, TILE)
+        open_[0, slot, rows, :] = here
+        open_[1, slot, rows, :] = jnp.where(lane == 0, 0, pltpu.roll(here, 1, axis=1))
+        open_[2, slot, rows, :] = jnp.where(lane == LANES - 1, 0, pltpu.roll(here, LANES - 1, axis=1))
+
+
+def start_column(post, slot, column_fields, x, radius, directions):
+    for t in range(WIDE // TILE):
+        rho = field(column_fields, 0, x, t * TILE)
+        u = [field(column_fields, 1 + k, x, t * TILE) for k in range(3)]
+        drive = drive_of(radius, field(column_fields, 4, x, t * TILE))
+        values = relaxed(None, rho, u, square(u), drive)
+        for i in directions:
+            post[i, slot, pl.ds(PAD + t * TILE, TILE), :] = values[i]
+
+
+def first_own_kernel(left, right, post, open_):
+    for column in range(4):
+        part, x = divmod(column, 2)
+        ref = (left, right)[part]
+        start_column(post, column, ref, x, ref[pl.ds(BASE_ROW, TILE), :], range(19))
+        mark_open(open_, column, ref, x, None)
+
+
 def first_kernel(
-    edge_ref, halo_l, left, right, halo_r, f_l, f_r, send_l, send_r, bits_out, links_out, send, base_out, post, open_
+    edge_ref, halo_l, left, right, halo_r, post_own, open_own,
+    f_l, f_r, send_l, send_r, bits_out, links_out, send, base_out, post_halo, open_halo,
 ):
     fields = (halo_l, left, right, halo_r)
-    radius = [ref[pl.ds(BASE_ROW, TILE), :] for ref in fields]
-    base_out[...] = radius[1]
-    lane = lax.broadcasted_iota(jnp.int32, (TILE, LANES), 1)
-    for part in range(4):
-        inside = None
-        if part == 0:
-            inside = edge_ref[0]
-        elif part == 3:
-            inside = edge_ref[1]
-        for x in range(2):
-            column = 2 * part + x
-            zero = jnp.zeros((TILE, LANES), jnp.int32)
-            for k in range(3):
-                open_[k, column, pl.ds(0, TILE), :] = zero
-                open_[k, column, pl.ds(PAD + WIDE, TILE), :] = zero
-            for t in range(WIDE // TILE):
-                here = (field(fields[part], 0, x, t * TILE) > 0.0).astype(jnp.int32)
-                if inside is not None:
-                    here = here * inside
-                rows = pl.ds(PAD + t * TILE, TILE)
-                open_[0, column, rows, :] = here
-                open_[1, column, rows, :] = jnp.where(lane == 0, 0, pltpu.roll(here, 1, axis=1))
-                open_[2, column, rows, :] = jnp.where(
-                    lane == LANES - 1, 0, pltpu.roll(here, LANES - 1, axis=1)
-                )
-    for column in range(1, 7):
-        part, x = divmod(column, 2)
-        for t in range(WIDE // TILE):
-            rho = field(fields[part], 0, x, t * TILE)
-            u = [field(fields[part], 1 + k, x, t * TILE) for k in range(3)]
-            drive = drive_of(radius[part], field(fields[part], 4, x, t * TILE))
-            values = relaxed(None, rho, u, square(u), drive)
-            for i in range(19):
-                post[i, column, pl.ds(PAD + t * TILE, TILE), :] = values[i]
+    base_out[...] = left[pl.ds(BASE_ROW, TILE), :]
+    post = {1: (post_halo, 0), 6: (post_halo, 1)} | {2 + k: (post_own, k) for k in range(4)}
+    open_ = {0: (open_halo, 0), 1: (open_halo, 1), 6: (open_halo, 2), 7: (open_halo, 3)}
+    open_ |= {2 + k: (open_own, k) for k in range(4)}
+    for x in range(2):
+        mark_open(open_halo, x, halo_l, x, edge_ref[0])
+        mark_open(open_halo, 2 + x, halo_r, x, edge_ref[1])
+    start_column(post_halo, 0, halo_l, 1, halo_l[pl.ds(BASE_ROW, TILE), :], TOWARD[1])
+    start_column(post_halo, 1, halo_r, 0, halo_r[pl.ds(BASE_ROW, TILE), :], TOWARD[-1])
     link_sum = shear_0 = shear_1 = jnp.zeros((TILE, LANES), F32)
     for column in range(1, 7):
         part, x = divmod(column, 2)
@@ -291,7 +317,8 @@
             count = jnp.zeros((TILE, LANES), jnp.int32)
             for i in range(1, 19):
                 cx, cy, cz = LATTICE[i]
-                seen = open_[cz % 3, column - cx, pl.ds(row - cy, TILE), :]
+                ref, slot = open_[column - cx]
+                seen = ref[cz % 3, slot, pl.ds(row - cy, TILE), :]
                 count = count + seen
                 bits = bits | (seen << i)
             bits_out[column - 1, rows, :] = bits
@@ -336,17 +363,16 @@
     radius_out[...] = every(base[...], 0) * (0.6 + 0.8 * jnp.tanh(mean))
 
 
-def collide_all(populations, column, fields, radius, row_in_fields, n_rows, post):
-    part, x = divmod(column, 2)
+def collide_all(populations, field_ref, x, radius, row_in_fields, n_rows, post, slot):
     for t in range(n_rows // TILE):
         rows = pl.ds(t * TILE, TILE)
         near = row_in_fields + t * TILE
         f = [populations(i, rows) for i in range(19)]
-        rho, u = moments(f, field(fields[part], 0, x, near) > 0.0)
-        drive = drive_of(radius[part], field(fields[part], 4, x, near))
+        rho, u = moments(f, field(field_ref, 0, x, near) > 0.0)
+        drive = drive_of(radius, field(field_ref, 4, x, near))
         values = relaxed(f, rho, u, square(u), drive)
         for i in range(19):
-            post[i, column, pl.ds(PAD + t * TILE, TILE), :] = values[i]
+            post[i, slot, pl.ds(PAD + t * TILE, TILE), :] = values[i]
 
 
 def in_pair(ref, x):
@@ -357,37 +383,69 @@
     return lambda i, rows: ref[i, rows, :]
 
 
+def own_kernel(a, b, g_a, g_b, rad, post, *, n_rows, row):
+    radius = every(rad[...], row)
+    for column in range(4):
+        part, x = divmod(column, 2)
+        collide_all(
+            in_pair((a, b)[part], x), (g_a, g_b)[part], x, radius, (WIDE - n_rows) // 2, n_rows, post, column
+        )
+
+
+def advance(held, column, field_ref, x, links, bits_in, radius, skip, side, post, slot):
+    sums = jnp.zeros((TILE, LANES), F32)
+    for t in range(MID // TILE):
+        row = (WIDE - MID) // 2 + t * TILE
+        near = pl.ds(row, TILE)
+        rows = pl.ds(PAD + t * TILE, TILE)
+        f = pulled(held, column, PAD + skip + t * TILE, bits_in[column - 1, near, :])
+        rho, u = moments(f, field(field_ref, 0, x, row) > 0.0)
+        unit = field(field_ref, 4, x, row)
+        drive = drive_of(radius, unit)
+        if side is not None:
+            chosen = TOWARD[side]
+            values = relaxed_some(chosen, [f[i] for i in chosen], rho, u, drive)
+        else:
+            chosen = range(19)
+            speed_sq = square(u)
+            sums = sums + by_unit(shear(links[column - 2, near, :], speed_sq), unit)
+            values = relaxed(f, rho, u, speed_sq, drive)
+        for i, value in zip(chosen, values):
+            post[i, slot, rows, :] = value
+    return sums
+
+
+def two_own_kernel(a, b, g_a, g_b, bits_in, links_in, rad, post_a, post_b, shear_out, *, n_rows):
+    own_kernel(a, b, g_a, g_b, rad, post_a, n_rows=n_rows, row=0)
+    held = {2 + k: (post_a, k) for k in range(4)}
+    second = every(rad[...], 1)
+    skip = (n_rows - MID) // 2
+    shear_out[...] = advance(
+        held, 3, g_a, 1, links_in, bits_in, second, skip, None, post_b, 0
+    ) + advance(held, 4, g_b, 0, links_in, bits_in, second, skip, None, post_b, 1)
+
+
 def two_steps_kernel(
-    h_l, a, b, h_r, g_hl, g_a, g_b, g_hr, bits_in, links_in, rad, rad_l, rad_r,
+    h_l, h_r, g_hl, g_a, g_b, g_hr, bits_in, links_in, rad, rad_l, rad_r, own_a, own_b, shear_in,
     f_l, f_r, send_l, send_r, send, post_a, post_b, *, n_rows, last_halo,
 ):
     fields = (g_hl, g_a, g_b, g_hr)
     top = (WIDE - n_rows) // 2
-    first = [every(r[...], 0) for r in (rad_l, rad, rad, rad_r)]
-    second = [every(r[...], 1) for r in (rad_l, rad, rad, rad_r)]
-    for column in range(2, 6):
-        source = in_pair(a if column < 4 else b, column % 2)
-        collide_all(source, column, fields, first, top, n_rows, post_a)
-    collide_all(in_halo(h_l), 1, fields, first, top, n_rows, post_a)
-    collide_all(in_halo(h_r), 6, fields, first, top, n_rows, post_a)
-    collide_far(h_l, 19, 1, g_hl, 0, top, first[0], 0, n_rows, post_a)
-    collide_far(h_r, 19, -1, g_hr, 1, top, first[3], 7, n_rows, post_a)
-    shear_a = shear_b = jnp.zeros((TILE, LANES), F32)
     skip = (n_rows - MID) // 2
-    for column in range(1, 7):
-        part, x = divmod(column, 2)
-        for t in range(MID // TILE):
-            row = (WIDE - MID) // 2 + t * TILE
-            near = pl.ds(row, TILE)
-            f = pulled(post_a, column, PAD + skip + t * TILE, bits_in[column - 1, near, :])
-            rho, u = moments(f, field(fields[part], 0, x, row) > 0.0)
-            speed_sq = square(u)
-            unit = field(fields[part], 4, x, row)
-            if part in (1, 2):
-                shear_a = shear_a + by_unit(shear(links_in[column - 2, near, :], speed_sq), unit)
-            values = relaxed(f, rho, u, speed_sq, drive_of(second[part], unit))
-            for i in range(19):
-                post_b[i, column, pl.ds(PAD + t * TILE, TILE), :] = values[i]
+    collide_all(in_halo(h_l), g_hl, 1, every(rad_l[...], 0), top, n_rows, post_a, 1)
+    collide_all(in_halo(h_r), g_hr, 0, every(rad_r[...], 0), top, n_rows, post_a, 2)
+    collide_far(h_l, 19, 1, g_hl, 0, top, every(rad_l[...], 0), n_rows, post_a, 0)
+    collide_far(h_r, 19, -1, g_hr, 1, top, every(rad_r[...], 0), n_rows, post_a, 3)
+    held = {0: (post_a, 0), 1: (post_a, 1), 6: (post_a, 2), 7: (post_a, 3)}
+    held |= {2 + k: (own_a, k) for k in range(4)}
+    own = every(rad[...], 1)
+    shear_a = shear_in[...]
+    shear_b = jnp.zeros((TILE, LANES), F32)
+    advance(held, 1, g_hl, 1, links_in, bits_in, every(rad_l[...], 1), skip, 1, post_b, 0)
+    advance(held, 6, g_hr, 0, links_in, bits_in, every(rad_r[...], 1), skip, -1, post_b, 3)
+    shear_a += advance(held, 2, g_a, 0, links_in, bits_in, own, skip, None, post_b, 1)
+    shear_a += advance(held, 5, g_b, 1, links_in, bits_in, own, skip, None, post_b, 2)
+    held = {1: (post_b, 0), 2: (post_b, 1), 3: (own_b, 0), 4: (own_b, 1), 5: (post_b, 2), 6: (post_b, 3)}
     for column in range(2, 6):
         part, x = divmod(column, 2)
         out = f_l if part == 1 else f_r
@@ -395,7 +453,7 @@
             row = (WIDE - MID) // 2 + t * TILE
             near = pl.ds(row, TILE)
             rows = pl.ds(t * TILE, TILE)
-            f = pulled(post_b, column, PAD + t * TILE, bits_in[column - 1, near, :])
+            f = pulled(held, column, PAD + t * TILE, bits_in[column - 1, near, :])
             for i in range(19):
                 out[i, x, rows, :] = f[i]
             rho, u = moments(f, field(fields[part], 0, x, row) > 0.0)
@@ -418,35 +476,29 @@
     send_all(send, row_pick([sublane_total(s) for s in (shear_a, shear_b)]))
 
 
-def last_kernel(
-    h_l, a, b, h_r, g_hl, g_a, g_b, g_hr, bits_in, rad, rad_l, rad_r, density, velocity, post
-):
+def last_kernel(h_l, h_r, g_hl, g_a, g_b, g_hr, bits_in, rad_l, rad_r, own_post, density, velocity, post):
     fields = (g_hl, g_a, g_b, g_hr)
-    radius = [every(r[...], 0) for r in (rad_l, rad, rad, rad_r)]
     top = (WIDE - MID) // 2
-    for column in range(2, 6):
-        source = in_pair(a if column < 4 else b, column % 2)
-        collide_all(source, column, fields, radius, top, MID, post)
-    collide_far(h_l, 0, 1, g_hl, 1, top, radius[0], 1, MID, post)
-    collide_far(h_r, 0, -1, g_hr, 0, top, radius[3], 6, MID, post)
+    collide_far(h_l, 0, 1, g_hl, 1, top, every(rad_l[...], 0), MID, post, 0)
+    collide_far(h_r, 0, -1, g_hr, 0, top, every(rad_r[...], 0), MID, post, 1)
+    held = {1: (post, 0), 6: (post, 1)} | {2 + k: (own_post, k) for k in range(4)}
     own = pl.ds(TILE, TILE)
     for column in range(2, 6):
         part, x = divmod(column, 2)
-        f = pulled(post, column, PAD + (MID - TILE) // 2, bits_in[column - 1, own, :])
+        f = pulled(held, column, PAD + (MID - TILE) // 2, bits_in[column - 1, own, :])
         rho, u = moments(f, field(fields[part], 0, x, TILE) > 0.0)
         density[column - 2] = rho
         for k in range(3):
             velocity[k, column - 2] = u[k]
 
 
-def call(kernel, outs, scratch=(), scalars=0, mib=1, plain_in=False, plain_out=False):
+def call(kernel, outs, scratch=(), scalars=0, mib=1, plain_out=False):
     vmem = pl.BlockSpec(memory_space=pltpu.VMEM)
     smem = pl.BlockSpec(memory_space=pltpu.SMEM)
 
     def run(*args):
-        space = pltpu.HBM if plain_in else pltpu.VMEM
         args = args[:scalars] + tuple(
-            pltpu.with_memory_space_constraint(a, space) for a in args[scalars:]
+            pltpu.with_memory_space_constraint(a, pltpu.VMEM) for a in args[scalars:]
         )
         held = jax.ShapeDtypeStruct if plain_out else pltpu.VMEM
         return pl.pallas_call(
@@ -478,9 +530,17 @@
     def exchange(blocks):
         return lax.all_to_all(blocks, GY, split_axis=0, concat_axis=0, tiled=True)
 
-    own, base_send = call(
-        gather_kernel, [((5, 4, TILE, LANES), F32), sends], scalars=1, plain_in=True
-    )(place.reshape(1), density, velocity, fluid_mask, unit_of_column, radius_base.reshape(1, -1))
+    arrays = (density, velocity, fluid_mask, unit_of_column, radius_base.reshape(1, -1))
+    anywhere = pl.BlockSpec(memory_space=pl.ANY)
+    own, base_send = pl.pallas_call(
+        gather_kernel,
+        out_shape=[pltpu.VMEM((5, 4, TILE, LANES), F32), jax.ShapeDtypeStruct(*sends)],
+        in_specs=[pl.BlockSpec(memory_space=pltpu.SMEM)] + [anywhere] * 5,
+        out_specs=[pl.BlockSpec(memory_space=pltpu.VMEM), anywhere],
+        scratch_shapes=[pltpu.VMEM(a.shape, a.dtype) for a in arrays]
+        + [pltpu.VMEM(*sends), pltpu.SemaphoreType.DMA((6,))],
+        compiler_params=pltpu.CompilerParams(vmem_limit_bytes=1 << 20),
+    )(place.reshape(1), *(pltpu.with_memory_space_constraint(a, pltpu.HBM) for a in arrays))
     base_in = exchange(base_send)
 
     forward = [(i, i + 1) for i in range(count - 1)]
@@ -491,6 +551,14 @@
     g_l, g_r = call(rows_kernel, [pair, pair])(low, own, high, base_in)
     g_hl, g_hr = ring(g_l, g_r)
     fields = (g_hl, g_l, g_r, g_hr)
+
+    def posts(columns, rows):
+        return ((19, columns, rows + 2 * PAD, LANES), F32)
+
+    def opens(columns):
+        return ((3, columns, WIDE + 2 * PAD, LANES), jnp.int32)
+
+    post_own, open_own = call(first_own_kernel, [posts(4, WIDE), opens(4)])(g_l, g_r)
 
     def populations(rows):
         return [((19, 2, rows, LANES), F32)] * 2
@@ -508,10 +576,10 @@
             sends,
             tile,
         ],
-        [((19, 8, WIDE + 2 * PAD, LANES), F32), ((3, 8, WIDE + 2 * PAD, LANES), jnp.int32)],
+        [posts(2, WIDE), opens(4)],
         scalars=1,
-        mib=6,
-    )(edge, *fields)
+        mib=3,
+    )(edge, *fields, post_own, open_own)
 
     for turn in range(3):
         gathered = exchange(send)
@@ -521,25 +589,27 @@
         else:
             (rad,) = call(response_kernel, [tile])(gathered, base, link_tile)
         rad_l, rad_r = ring(rad, rad)
-        parts = (h_l, f_l, f_r, h_r)
         if turn < 2:
             rows = WIDE if turn == 0 else MID
+            own_part = call(
+                functools.partial(two_own_kernel, n_rows=rows), [posts(4, rows), posts(2, MID), tile]
+            )(f_l, f_r, g_l, g_r, bits, links, rad)
             f_l, f_r, send_l, send_r, send = call(
                 functools.partial(two_steps_kernel, n_rows=rows, last_halo=turn == 1),
                 [*populations(MID), *halos(MID, last=turn == 1), sends],
-                [
-                    ((19, 8, rows + 2 * PAD, LANES), F32),
-                    ((19, 8, MID + 2 * PAD, LANES), F32),
-                ],
-                mib=8,
-            )(*parts, *fields, bits, links, rad, rad_l, rad_r)
+                [posts(4, rows), posts(4, MID)],
+                mib=4,
+            )(h_l, h_r, *fields, bits, links, rad, rad_l, rad_r, *own_part)
+    (own_post,) = call(functools.partial(own_kernel, n_rows=MID, row=0), [posts(4, MID)])(
+        f_l, f_r, g_l, g_r, rad
+    )
     density_out, velocity_out = call(
         last_kernel,
         [((4, TILE, LANES), F32), ((3, 4, TILE, LANES), F32)],
-        [((19, 8, MID + 2 * PAD, LANES), F32)],
-        mib=4,
+        [posts(2, MID)],
+        mib=2,
         plain_out=True,
-    )(*parts, *fields, bits, rad, rad_l, rad_r)
+    )(h_l, h_r, *fields, bits, rad_l, rad_r, own_post)
     own_radius = lax.dynamic_slice_in_dim(rad[1], place * UNIT_DEV, UNIT_DEV)
     return density_out, velocity_out, own_radius
 

time: 98.2 us -> 96.4 us (0.982)
  waiting for transfers between devices: 16.6 us -> 15.1 us
    ppermute x14, waiting for transfers between devices: 13.2 us -> 11.7 us  [ring(): return (lax.ppermute(high, 'gx', up), lax.ppermute(low, 'gx', down))]
    pallas_call x9 -> x12, Pallas kernels: 7 us -> 5.61 us  [run(): pl.pallas_call(kernel, out_shape=[held(shape, dtype) for shape, dtype in...]
  transfers between devices with their start and end apart: 17 -> 17, of which waited for: 8 -> 7; matrix products, arithmetic and copies ran while one was open for 1% -> 1% of each run, Pallas kernels for 0% -> 2%
where the time goes in v2:
time: 96.4 us; the launch traced here: 96 us
  blocking collectives  43 us (45%)
  starting transfers between devices  29.9 us (31%)
  waiting for transfers between devices  15.1 us (16%)
  Pallas kernels  6.59 us (7%)
    all_to_all x3, blocking collectives, exchange(): return lax.all_to_all(blocks, GY, split_axis=0, concat_axis=0, tiled=True)  43 us
    ppermute x14, starting transfers between devices, ring(): return (lax.ppermute(high, 'gx', up), lax.ppermute(low, 'gx', down))  18.3 us
    ppermute x14, waiting for transfers between devices, ring(): return (lax.ppermute(high, 'gx', up), lax.ppermute(low, 'gx', down))  11.7 us
    pallas_call x12, Pallas kernels, run(): pl.pallas_call(kernel, out_shape=[held(shape, dtype) for shape, dtype in...  5.61 us
    ppermute x1, starting transfers between devices, step_all(): high = lax.ppermute(own, GY, backward)  4.89 us
    all_to_all x1, starting transfers between devices, exchange(): return lax.all_to_all(blocks, GY, split_axis=0, concat_axis=0, tiled=True)  4.83 us
    all_to_all x1, waiting for transfers between devices, exchange(): return lax.all_to_all(blocks, GY, split_axis=0, concat_axis=0, tiled=True)  3.33 us
  transfers between devices with their start and end apart: 17, of which 7 were waited for; matrix products, arithmetic and copies ran while one was open for 1% of the time, Pallas kernels for 2%

profile of v2, /device:TPU:2, one launch (start us, length us, event | category | flops | bytes accessed | tf_op | source)
XLA Modules:
  0.0 96.0 jit_solution(17911514226532787748)
XLA Ops:
  0.6 1.0 %shard_map.76 = (f32[5,4,8,128]{3,2,1,0:T(8,128)S(1)}, f32[16,8,128]{2,1,0:T(8,128)S(1)}) custom-call(s32[1]{0:T(128)} %bitcast.2.place_ref, f32[4,8,128]{2,1,0:T(8,128)} %density.1, f32[3,4,8,128]{3,2,1,0:T(8,128)} %velocity.1, s32[4,8,128]{2,1,0:T(8,128)} %mask.1, s32[4,8]{1,0:T(4,128)} %unit.1, f32[1,8]{1,0:T(1,128)} %bitcast.6), custom_call_target="tpu_custom_call" | custom-call | tf_op jit(solution)/shard_map/pallas_call | solution.py:535
  1.6 4.9 %collective-permute-start.1 = (f32[5,4,8,128]{3,2,1,0:T(8,128)S(1)}, f32[5,4,8,128]{3,2,1,0:T(8,128)S(1)}, u32[]{:S(2)}, u32[]{:S(2)}) collective-permute-start(f32[5,4,8,128]{3,2,1,0:T(8,128)S(1)} %get-tuple-element.37.own), channel_id=1, source_target_pairs={{1,0},{2,1},{3,2},{4,3},{5,4},{6,5},{7,6},{8,7},{9,8},{10,9},{11,1... | collective-permute-start | bytes 245768 | tf_op jit(solution)/shard_map/ppermute | solution.py:549
  6.5 1.9 %collective-permute-start = (f32[5,4,8,128]{3,2,1,0:T(8,128)S(1)}, f32[5,4,8,128]{3,2,1,0:T(8,128)S(1)}, u32[]{:S(2)}, u32[]{:S(2)}) collective-permute-start(f32[5,4,8,128]{3,2,1,0:T(8,128)S(1)} %get-tuple-element.37.own), channel_id=1, source_target_pairs={{0,1},{1,2},{2,3},{3,4},{4,5},{5,6},{6,7},{7,8},{8,9},{9,10},{10,1... | collective-permute-start | bytes 245768 | tf_op jit(solution)/shard_map/ppermute | solution.py:548
  8.5 20.9 %all_to_all.20.base_in = f32[16,8,128]{2,1,0:T(8,128)S(1)} all-to-all(f32[16,8,128]{2,1,0:T(8,128)S(1)} %get-tuple-element.38), channel_id=1, replica_groups=mesh['gx'=64,'gy_0'=4,'gy_1'=4] {'gy_0','gy_1'}, dimensions={0} | all-to-all | bytes 131072 | tf_op jit(solution)/shard_map/all_to_all | solution.py:531
  29.4 7.8 %collective-permute-start.3 = (f32[248,128]{1,0:T(8,128)S(1)}, f32[248,128]{1,0:T(8,128)S(1)}, u32[]{:S(2)}, u32[]{:S(2)}) collective-permute-start(f32[248,128]{1,0:T(8,128)S(1)} %get-tuple-element.40.left.g_a), channel_id=1, source_target_pairs={{16,0},{32,16},{48,32},{64,48},{80,64},{96,80},{112,96},{128,112},... | collective-permute-start | bytes 380936 | tf_op jit(solution)/shard_map/ppermute | solution.py:528
  37.5 2.3 %collective-permute-done.2.halo_l.g_hl = f32[248,128]{1,0:T(8,128)S(1)} collective-permute-done((f32[248,128]{1,0:T(8,128)S(1)}, f32[248,128]{1,0:T(8,128)S(1)}, u32[]{:S(2)}, u32[]{:S(2)}) %collective-permute-start.2) | collective-permute-done | bytes 127008 | tf_op jit(solution)/shard_map/ppermute | solution.py:528
  39.8 1.1 %shard_map.79 = (f32[19,2,24,128]{3,2,1,0:T(8,128)S(1)}, f32[19,2,24,128]{3,2,1,0:T(8,128)S(1)}, f32[28,24,128]{2,1,0:T(8,128)S(1)}, f32[28,24,128]{2,1,0:T(8,12...) custom-call(s32[2]{0:T(128)S(1)} %add_convert_fusion.edge_ref, ...), custom_call_target="tpu_custom_call" | custom-call | tf_op jit(solution)/shard_map/pallas_call | solution.py:504
  40.9 3.0 %collective-permute-start.5 = (f32[28,24,128]{2,1,0:T(8,128)S(1)}, f32[28,24,128]{2,1,0:T(8,128)S(1)}, u32[]{:S(2)}, u32[]{:S(2)}) collective-permute-start(f32[28,24,128]{2,1,0:T(8,128)S(1)} %get-tuple-element.44), channel_id=1, source_target_pairs={{16,0},{32,16},{48,32},{64,48},{80,64},{96,80},{112,96},{128,112},... | collective-permute-start | bytes 1032200 | tf_op jit(solution)/shard_map/ppermute | solution.py:528
  43.9 11.2 %all_to_all.21.gathered = f32[16,8,128]{2,1,0:T(8,128)S(1)} all-to-all(f32[16,8,128]{2,1,0:T(8,128)S(1)} %get-tuple-element.47), channel_id=1, replica_groups=mesh['gx'=64,'gy_0'=4,'gy_1'=4] {'gy_0','gy_1'}, dimensions={0} | all-to-all | bytes 131072 | tf_op jit(solution)/shard_map/all_to_all | solution.py:531
  55.1 0.5 collective-permute-start.6
  55.6 0.6 shard_map.81
  56.5 2.9 %collective-permute-done.6.rad_l = f32[8,128]{1,0:T(8,128)S(1)} collective-permute-done((f32[8,128]{1,0:T(8,128)S(1)}, f32[8,128]{1,0:T(8,128)S(1)}, u32[]{:S(2)}, u32[]{:S(2)}) %collective-permute-start.6) | collective-permute-done | bytes 4128 | tf_op jit(solution)/shard_map/ppermute | solution.py:528
  59.4 0.8 shard_map.82
  60.2 2.9 %collective-permute-start.9 = (f32[28,16,128]{2,1,0:T(8,128)S(1)}, f32[28,16,128]{2,1,0:T(8,128)S(1)}, u32[]{:S(2)}, u32[]{:S(2)}) collective-permute-start(f32[28,16,128]{2,1,0:T(8,128)S(1)} %get-tuple-element.56), channel_id=1, source_target_pairs={{16,0},{32,16},{48,32},{64,48},{80,64},{96,80},{112,96},{128,112},... | collective-permute-start | bytes 688136 | tf_op jit(solution)/shard_map/ppermute | solution.py:528
  63.2 10.9 %all_to_all.22.gathered = f32[16,8,128]{2,1,0:T(8,128)S(1)} all-to-all(f32[16,8,128]{2,1,0:T(8,128)S(1)} %get-tuple-element.57), channel_id=1, replica_groups=mesh['gx'=64,'gy_0'=4,'gy_1'=4] {'gy_0','gy_1'}, dimensions={0} | all-to-all | bytes 131072 | tf_op jit(solution)/shard_map/all_to_all | solution.py:531
  74.1 0.5 collective-permute-start.10
  75.4 2.9 %collective-permute-done.10.rad_l = f32[8,128]{1,0:T(8,128)S(1)} collective-permute-done((f32[8,128]{1,0:T(8,128)S(1)}, f32[8,128]{1,0:T(8,128)S(1)}, u32[]{:S(2)}, u32[]{:S(2)}) %collective-permute-start.10) | collective-permute-done | bytes 4128 | tf_op jit(solution)/shard_map/ppermute | solution.py:528
  78.4 1.4 %shard_map.85 = (f32[19,2,16,128]{3,2,1,0:T(8,128)S(1)}, f32[19,2,16,128]{3,2,1,0:T(8,128)S(1)}, f32[9,16,128]{2,1,0:T(8,128)S(1)}, f32[9,16,128]{2,1,0:T(8,128)S(1)}, f32[16,8,128]{2,1,0:T(8,128)}) custom-call(f32[28,16,128]{2,1,0:T(8,128)S(1)} %collective-permute-done.8.h_l, f32[28,16,128]{2,1,0:T(8,128)S(1)} %collective-permute-done.9.h_r, ...), custom_call_target="tpu_custom_call" | custom-call | tf_op jit(solution)/shard_map/pallas_call | solution.py:504
  79.7 4.8 %all-to-all-start.3 = ((f32[16,8,128]{2,1,0:T(8,128)}), f32[16,8,128]{2,1,0:T(8,128)S(1)}, u32[]{:S(2)}, u32[]{:S(2)}) async-start(f32[16,8,128]{2,1,0:T(8,128)} %get-tuple-element.66), calls=%async_computation.3 | async-start | bytes 131072 | tf_op jit(solution)/shard_map/all_to_all | solution.py:531
  84.6 2.9 %collective-permute-start.13 = (f32[9,16,128]{2,1,0:T(8,128)S(1)}, f32[9,16,128]{2,1,0:T(8,128)S(1)}, u32[]{:S(2)}, u32[]{:S(2)}) collective-permute-start(f32[9,16,128]{2,1,0:T(8,128)S(1)} %get-tuple-element.65), channel_id=1, source_target_pairs={{16,0},{32,16},{48,32},{64,48},{80,64},{96,80},{112,96},{128,112},... | collective-permute-start | bytes 221192 | tf_op jit(solution)/shard_map/ppermute | solution.py:528
  87.5 3.3 %all-to-all-done.3.gathered = f32[16,8,128]{2,1,0:T(8,128)S(1)} async-done(((f32[16,8,128]{2,1,0:T(8,128)}), f32[16,8,128]{2,1,0:T(8,128)S(1)}, u32[]{:S(2)}, u32[]{:S(2)}) %all-to-all-start.3) | async-done | bytes 65568 | tf_op jit(solution)/shard_map/all_to_all | solution.py:531
  91.4 0.6 dynamic-slice_bitcast_fusion
  92.2 2.9 %collective-permute-done.14.rad_l = f32[8,128]{1,0:T(8,128)S(1)} collective-permute-done((f32[8,128]{1,0:T(8,128)S(1)}, f32[8,128]{1,0:T(8,128)S(1)}, u32[]{:S(2)}, u32[]{:S(2)}) %collective-permute-start.14) | collective-permute-done | bytes 4128 | tf_op jit(solution)/shard_map/ppermute | solution.py:528
  95.2 0.8 shard_map.88
  (29 shorter events, 2.2 us)
Async XLA Ops:
  1.6 27.8 %collective-permute-start.1 = (f32[5,4,8,128]{3,2,1,0:T(8,128)S(1)}, f32[5,4,8,128]{3,2,1,0:T(8,128)S(1)}, u32[]{:S(2)}, u32[]{:S(2)}) collective-permute-start(f32[5,4,8,128]{3,2,1,0:T(8,128)S(1)} %get-tuple-element.37.own), channel_id=1, source_target_pairs={{1,0},{2,1},{3,2},{4,3},{5,4},{6,5},{7,6},{8,7},{9,8},{10,9},{11,1... | collective-permute-start | bytes 245768 | tf_op jit(solution)/shard_map/ppermute | solution.py:549
  6.5 22.9 %collective-permute-start = (f32[5,4,8,128]{3,2,1,0:T(8,128)S(1)}, f32[5,4,8,128]{3,2,1,0:T(8,128)S(1)}, u32[]{:S(2)}, u32[]{:S(2)}) collective-permute-start(f32[5,4,8,128]{3,2,1,0:T(8,128)S(1)} %get-tuple-element.37.own), channel_id=1, source_target_pairs={{0,1},{1,2},{2,3},{3,4},{4,5},{5,6},{6,7},{7,8},{8,9},{9,10},{10,1... | collective-permute-start | bytes 245768 | tf_op jit(solution)/shard_map/ppermute | solution.py:548
  29.4 10.4 %collective-permute-start.2 = (f32[248,128]{1,0:T(8,128)S(1)}, f32[248,128]{1,0:T(8,128)S(1)}, u32[]{:S(2)}, u32[]{:S(2)}) collective-permute-start(f32[248,128]{1,0:T(8,128)S(1)} %get-tuple-element.39.right.g_b), channel_id=1, source_target_pairs={{0,16},{16,32},{32,48},{48,64},{64,80},{80,96},{96,112},{112,128},... | collective-permute-start | bytes 380936 | tf_op jit(solution)/shard_map/ppermute | solution.py:528
  29.4 10.4 %collective-permute-start.3 = (f32[248,128]{1,0:T(8,128)S(1)}, f32[248,128]{1,0:T(8,128)S(1)}, u32[]{:S(2)}, u32[]{:S(2)}) collective-permute-start(f32[248,128]{1,0:T(8,128)S(1)} %get-tuple-element.40.left.g_a), channel_id=1, source_target_pairs={{16,0},{32,16},{48,32},{64,48},{80,64},{96,80},{112,96},{128,112},... | collective-permute-start | bytes 380936 | tf_op jit(solution)/shard_map/ppermute | solution.py:528
  40.9 18.5 %collective-permute-start.4 = (f32[28,24,128]{2,1,0:T(8,128)S(1)}, f32[28,24,128]{2,1,0:T(8,128)S(1)}, u32[]{:S(2)}, u32[]{:S(2)}) collective-permute-start(f32[28,24,128]{2,1,0:T(8,128)S(1)} %get-tuple-element.43), channel_id=1, source_target_pairs={{0,16},{16,32},{32,48},{48,64},{64,80},{80,96},{96,112},{112,128},... | collective-permute-start | bytes 1032200 | tf_op jit(solution)/shard_map/ppermute | solution.py:528
  40.9 18.5 %collective-permute-start.5 = (f32[28,24,128]{2,1,0:T(8,128)S(1)}, f32[28,24,128]{2,1,0:T(8,128)S(1)}, u32[]{:S(2)}, u32[]{:S(2)}) collective-permute-start(f32[28,24,128]{2,1,0:T(8,128)S(1)} %get-tuple-element.44), channel_id=1, source_target_pairs={{16,0},{32,16},{48,32},{64,48},{80,64},{96,80},{112,96},{128,112},... | collective-permute-start | bytes 1032200 | tf_op jit(solution)/shard_map/ppermute | solution.py:528
  55.1 1.3 %collective-permute-start.7 = (f32[8,128]{1,0:T(8,128)S(1)}, f32[8,128]{1,0:T(8,128)S(1)}, u32[]{:S(2)}, u32[]{:S(2)}) collective-permute-start(f32[8,128]{1,0:T(8,128)S(1)} %get-tuple-element.49.rad), channel_id=1, source_target_pairs={{16,0},{32,16},{48,32},{64,48},{80,64},{96,80},{112,96},{128,112},... | collective-permute-start | bytes 12296 | tf_op jit(solution)/shard_map/ppermute | solution.py:528
  55.1 4.3 %collective-permute-start.6 = (f32[8,128]{1,0:T(8,128)S(1)}, f32[8,128]{1,0:T(8,128)S(1)}, u32[]{:S(2)}, u32[]{:S(2)}) collective-permute-start(f32[8,128]{1,0:T(8,128)S(1)} %get-tuple-element.49.rad), channel_id=1, source_target_pairs={{0,16},{16,32},{32,48},{48,64},{64,80},{80,96},{96,112},{112,128},... | collective-permute-start | bytes 12296 | tf_op jit(solution)/shard_map/ppermute | solution.py:528
  60.2 18.1 %collective-permute-start.8 = (f32[28,16,128]{2,1,0:T(8,128)S(1)}, f32[28,16,128]{2,1,0:T(8,128)S(1)}, u32[]{:S(2)}, u32[]{:S(2)}) collective-permute-start(f32[28,16,128]{2,1,0:T(8,128)S(1)} %get-tuple-element.55), channel_id=1, source_target_pairs={{0,16},{16,32},{32,48},{48,64},{64,80},{80,96},{96,112},{112,128},... | collective-permute-start | bytes 688136 | tf_op jit(solution)/shard_map/ppermute | solution.py:528
  60.2 18.1 %collective-permute-start.9 = (f32[28,16,128]{2,1,0:T(8,128)S(1)}, f32[28,16,128]{2,1,0:T(8,128)S(1)}, u32[]{:S(2)}, u32[]{:S(2)}) collective-permute-start(f32[28,16,128]{2,1,0:T(8,128)S(1)} %get-tuple-element.56), channel_id=1, source_target_pairs={{16,0},{32,16},{48,32},{64,48},{80,64},{96,80},{112,96},{128,112},... | collective-permute-start | bytes 688136 | tf_op jit(solution)/shard_map/ppermute | solution.py:528
  74.1 1.3 %collective-permute-start.11 = (f32[8,128]{1,0:T(8,128)S(1)}, f32[8,128]{1,0:T(8,128)S(1)}, u32[]{:S(2)}, u32[]{:S(2)}) collective-permute-start(f32[8,128]{1,0:T(8,128)S(1)} %shard_map.83.rad), channel_id=1, source_target_pairs={{16,0},{32,16},{48,32},{64,48},{80,64},{96,80},{112,96},{128,112},... | collective-permute-start | bytes 12296 | tf_op jit(solution)/shard_map/ppermute | solution.py:528
  74.1 4.3 %collective-permute-start.10 = (f32[8,128]{1,0:T(8,128)S(1)}, f32[8,128]{1,0:T(8,128)S(1)}, u32[]{:S(2)}, u32[]{:S(2)}) collective-permute-start(f32[8,128]{1,0:T(8,128)S(1)} %shard_map.83.rad), channel_id=1, source_target_pairs={{0,16},{16,32},{32,48},{48,64},{64,80},{80,96},{96,112},{112,128},... | collective-permute-start | bytes 12296 | tf_op jit(solution)/shard_map/ppermute | solution.py:528
  79.7 11.1 %all-to-all-start.3 = ((f32[16,8,128]{2,1,0:T(8,128)}), f32[16,8,128]{2,1,0:T(8,128)S(1)}, u32[]{:S(2)}, u32[]{:S(2)}) async-start(f32[16,8,128]{2,1,0:T(8,128)} %get-tuple-element.66), calls=%async_computation.3 | async-start | bytes 131072 | tf_op jit(solution)/shard_map/all_to_all | solution.py:531
  84.6 10.6 %collective-permute-start.12 = (f32[9,16,128]{2,1,0:T(8,128)S(1)}, f32[9,16,128]{2,1,0:T(8,128)S(1)}, u32[]{:S(2)}, u32[]{:S(2)}) collective-permute-start(f32[9,16,128]{2,1,0:T(8,128)S(1)} %get-tuple-element.64), channel_id=1, source_target_pairs={{0,16},{16,32},{32,48},{48,64},{64,80},{80,96},{96,112},{112,128},... | collective-permute-start | bytes 221192 | tf_op jit(solution)/shard_map/ppermute | solution.py:528
  84.6 10.6 %collective-permute-start.13 = (f32[9,16,128]{2,1,0:T(8,128)S(1)}, f32[9,16,128]{2,1,0:T(8,128)S(1)}, u32[]{:S(2)}, u32[]{:S(2)}) collective-permute-start(f32[9,16,128]{2,1,0:T(8,128)S(1)} %get-tuple-element.65), channel_id=1, source_target_pairs={{16,0},{32,16},{48,32},{64,48},{80,64},{96,80},{112,96},{128,112},... | collective-permute-start | bytes 221192 | tf_op jit(solution)/shard_map/ppermute | solution.py:528
  90.9 1.3 %collective-permute-start.15 = (f32[8,128]{1,0:T(8,128)S(1)}, f32[8,128]{1,0:T(8,128)S(1)}, u32[]{:S(2)}, u32[]{:S(2)}) collective-permute-start(f32[8,128]{1,0:T(8,128)S(1)} %shard_map.86.rad), channel_id=1, source_target_pairs={{16,0},{32,16},{48,32},{64,48},{80,64},{96,80},{112,96},{128,112},... | collective-permute-start | bytes 12296 | tf_op jit(solution)/shard_map/ppermute | solution.py:528
  90.9 4.3 %collective-permute-start.14 = (f32[8,128]{1,0:T(8,128)S(1)}, f32[8,128]{1,0:T(8,128)S(1)}, u32[]{:S(2)}, u32[]{:S(2)}) collective-permute-start(f32[8,128]{1,0:T(8,128)S(1)} %shard_map.86.rad), channel_id=1, source_target_pairs={{0,16},{16,32},{32,48},{48,64},{64,80},{80,96},{96,112},{112,128},... | collective-permute-start | bytes 12296 | tf_op jit(solution)/shard_map/ppermute | solution.py:528

commit v3 on v2

--- a/solution.py
+++ b/solution.py
@@ -45,7 +45,9 @@
 PAD = 8
 WIDE = 24
 MID = 16
-BASE_ROW = 5 * 2 * WIDE
+OWN_PLANES = {(k, x): 2 * k + x for k in range(5) for x in range(2)}
+NEAR_FAR = {(k, 0): k for k in range(5)} | {(0, 1): 5, (4, 1): 6}
+LEFT_PLANES = {(k, 1 - x): plane for (k, x), plane in NEAR_FAR.items()}
 TOWARD = {side: tuple(i for i in range(19) if LATTICE[i][0] == side) for side in (-1, 1)}
 FAR = 9
 
@@ -126,8 +128,18 @@
     return post
 
 
-def field(ref, k, x, row):
-    return ref[pl.ds((2 * k + x) * WIDE + row, TILE), :]
+def field(held, k, x, row):
+    ref, planes = held
+    return ref[pl.ds(planes[k, x] * WIDE + row, TILE), :]
+
+
+def base_of(held):
+    ref, planes = held
+    return ref[pl.ds(len(planes) * WIDE, TILE), :]
+
+
+def fields_of(halo_l, left, right, halo_r):
+    return ((halo_l, LEFT_PLANES), (left, OWN_PLANES), (right, OWN_PLANES), (halo_r, NEAR_FAR))
 
 
 def put_all(out, rows, f):
@@ -248,15 +260,20 @@
     store.wait()
 
 
-def rows_kernel(low, own, high, base_in, left_out, right_out):
+def rows_kernel(low, own, high, base_in, left_out, right_out, left_send, right_send):
     base = sum_of(base_in)
-    for half, out in ((0, left_out), (1, right_out)):
-        for k in range(5):
-            for x in range(2):
-                for part, ref in enumerate((low, own, high)):
-                    row = (2 * k + x) * WIDE + part * TILE
-                    out[pl.ds(row, TILE), :] = ref[k, 2 * half + x]
-        out[pl.ds(BASE_ROW, TILE), :] = base
+    for half, out, send, planes in (
+        (0, left_out, left_send, NEAR_FAR),
+        (1, right_out, right_send, LEFT_PLANES),
+    ):
+        for (k, x), plane in OWN_PLANES.items():
+            for part, ref in enumerate((low, own, high)):
+                value = ref[k, 2 * half + x]
+                out[pl.ds(plane * WIDE + part * TILE, TILE), :] = value
+                if (k, x) in planes:
+                    send[pl.ds(planes[k, x] * WIDE + part * TILE, TILE), :] = value
+        out[pl.ds(len(OWN_PLANES) * WIDE, TILE), :] = base
+        send[pl.ds(len(planes) * WIDE, TILE), :] = base
 
 
 def mark_open(open_, slot, column_fields, x, inside):
@@ -285,71 +302,87 @@
             post[i, slot, pl.ds(PAD + t * TILE, TILE), :] = values[i]
 
 
-def first_own_kernel(left, right, post, open_):
+def stream_first(post, open_, column, held, x, f_out, send_near, send_far, side, links_out):
+    sums = None
+    bits_of = []
+    for t in range(WIDE // TILE):
+        row = PAD + t * TILE
+        rows = pl.ds(t * TILE, TILE)
+        bits, count = open_bits(open_, column, row)
+        bits_of.append(bits)
+        f = pulled(post, column, row, bits)
+        put_all(f_out.at[:, x], rows, f)
+        fluid = field(held, 0, x, t * TILE) > 0.0
+        if t == 1 or send_far is not None:
+            rho, u = moments(f, fluid)
+        if send_far is not None:
+            put_far(send_far, 19, rows, side, f, rho, u)
+        else:
+            put_all(send_near, rows, f)
+        if t != 1:
+            links_out[column - 2, rows, :] = jnp.zeros((TILE, LANES), F32)
+            continue
+        links = jnp.where(fluid, (18 - count).astype(F32), 0.0)
+        links_out[column - 2, rows, :] = links
+        unit = field(held, 4, x, t * TILE)
+        start = [field(held, 1 + k, x, t * TILE) for k in range(3)]
+        sums = [by_unit(v, unit) for v in (links * square(start), links * square(u), links)]
+    return bits_of, sums
+
+
+def open_bits(open_, column, row):
+    bits = count = jnp.zeros((TILE, LANES), jnp.int32)
+    for i in range(1, 19):
+        cx, cy, cz = LATTICE[i]
+        ref, slot = open_[column - cx]
+        seen = ref[cz % 3, slot, pl.ds(row - cy, TILE), :]
+        count = count + seen
+        bits = bits | (seen << i)
+    return bits, count
+
+
+def put_bits(bits_out, column, bits_of):
+    for t, bits in enumerate(bits_of):
+        bits_out[column - 1, pl.ds(t * TILE, TILE), :] = bits
+
+
+def first_own_kernel(left, right, post, open_, f_l, f_r, send_l, send_r, bits_out, links_out, sums_out):
+    pairs = ((left, OWN_PLANES), (right, OWN_PLANES))
     for column in range(4):
         part, x = divmod(column, 2)
-        ref = (left, right)[part]
-        start_column(post, column, ref, x, ref[pl.ds(BASE_ROW, TILE), :], range(19))
-        mark_open(open_, column, ref, x, None)
+        start_column(post, column, pairs[part], x, base_of(pairs[part]), range(19))
+        mark_open(open_, column, pairs[part], x, None)
+    held = {2 + k: (post, k) for k in range(4)}
+    seen = {2 + k: (open_, k) for k in range(4)}
+    bits, sums_a = stream_first(held, seen, 3, pairs[0], 1, f_l, None, send_l, -1, links_out)
+    put_bits(bits_out, 3, bits)
+    bits, sums_b = stream_first(held, seen, 4, pairs[1], 0, f_r, None, send_r, 1, links_out)
+    put_bits(bits_out, 4, bits)
+    for k in range(3):
+        sums_out[k] = sums_a[k] + sums_b[k]
 
 
 def first_kernel(
-    edge_ref, halo_l, left, right, halo_r, post_own, open_own,
-    f_l, f_r, send_l, send_r, bits_out, links_out, send, base_out, post_halo, open_halo,
+    edge_ref, halo_l, left, right, halo_r, post_own, open_own, sums_in, *rest
 ):
-    fields = (halo_l, left, right, halo_r)
-    base_out[...] = left[pl.ds(BASE_ROW, TILE), :]
+    f_l, f_r, send_l, send_r, bits_out, links_out, send, base_out, post_halo, open_halo = rest[6:]
+    fields = fields_of(halo_l, left, right, halo_r)
+    base_out[...] = base_of(fields[1])
     post = {1: (post_halo, 0), 6: (post_halo, 1)} | {2 + k: (post_own, k) for k in range(4)}
     open_ = {0: (open_halo, 0), 1: (open_halo, 1), 6: (open_halo, 2), 7: (open_halo, 3)}
     open_ |= {2 + k: (open_own, k) for k in range(4)}
     for x in range(2):
-        mark_open(open_halo, x, halo_l, x, edge_ref[0])
-        mark_open(open_halo, 2 + x, halo_r, x, edge_ref[1])
-    start_column(post_halo, 0, halo_l, 1, halo_l[pl.ds(BASE_ROW, TILE), :], TOWARD[1])
-    start_column(post_halo, 1, halo_r, 0, halo_r[pl.ds(BASE_ROW, TILE), :], TOWARD[-1])
-    link_sum = shear_0 = shear_1 = jnp.zeros((TILE, LANES), F32)
-    for column in range(1, 7):
-        part, x = divmod(column, 2)
-        for t in range(WIDE // TILE):
-            row = PAD + t * TILE
-            rows = pl.ds(t * TILE, TILE)
-            bits = jnp.zeros((TILE, LANES), jnp.int32)
-            count = jnp.zeros((TILE, LANES), jnp.int32)
-            for i in range(1, 19):
-                cx, cy, cz = LATTICE[i]
-                ref, slot = open_[column - cx]
-                seen = ref[cz % 3, slot, pl.ds(row - cy, TILE), :]
-                count = count + seen
-                bits = bits | (seen << i)
-            bits_out[column - 1, rows, :] = bits
-            if part not in (1, 2):
-                continue
-            f = pulled(post, column, row, bits)
-            out = f_l if part == 1 else f_r
-            for i in range(19):
-                out[i, x, rows, :] = f[i]
-            fluid = field(fields[part], 0, x, t * TILE) > 0.0
-            if t == 1 or column in (3, 4):
-                rho, u = moments(f, fluid)
-            if column == 2:
-                put_all(send_l, rows, f)
-            elif column == 3:
-                put_far(send_l, 19, rows, -1, f, rho, u)
-            elif column == 4:
-                put_far(send_r, 19, rows, 1, f, rho, u)
-            else:
-                put_all(send_r, rows, f)
-            if t != 1:
-                links_out[column - 2, rows, :] = jnp.zeros((TILE, LANES), F32)
-                continue
-            links = jnp.where(fluid, (18 - count).astype(F32), 0.0)
-            links_out[column - 2, rows, :] = links
-            unit = field(fields[part], 4, x, t * TILE)
-            start = [field(fields[part], 1 + k, x, t * TILE) for k in range(3)]
-            link_sum = link_sum + by_unit(links, unit)
-            shear_0 = shear_0 + by_unit(links * square(start), unit)
-            shear_1 = shear_1 + by_unit(links * square(u), unit)
-    send_all(send, row_pick([sublane_total(s) for s in (shear_0, shear_1, link_sum)]))
+        mark_open(open_halo, x, fields[0], x, edge_ref[0])
+        mark_open(open_halo, 2 + x, fields[3], x, edge_ref[1])
+    start_column(post_halo, 0, fields[0], 1, base_of(fields[0]), TOWARD[1])
+    start_column(post_halo, 1, fields[3], 0, base_of(fields[3]), TOWARD[-1])
+    for column in (1, 6):
+        put_bits(bits_out, column, [open_bits(open_, column, PAD + t * TILE)[0] for t in range(WIDE // TILE)])
+    bits, sums_a = stream_first(post, open_, 2, fields[1], 0, f_l, send_l, None, None, links_out)
+    put_bits(bits_out, 2, bits)
+    bits, sums_b = stream_first(post, open_, 5, fields[2], 1, f_r, send_r, None, None, links_out)
+    put_bits(bits_out, 5, bits)
+    send_all(send, row_pick([sublane_total(sums_in[k] + sums_a[k] + sums_b[k]) for k in range(3)]))
 
 
 def response_kernel(gathered, base, links_in, radius_out, links_out=None):
@@ -388,7 +421,7 @@
     for column in range(4):
         part, x = divmod(column, 2)
         collide_all(
-            in_pair((a, b)[part], x), (g_a, g_b)[part], x, radius, (WIDE - n_rows) // 2, n_rows, post, column
+            in_pair((a, b)[part], x), ((g_a, g_b)[part], OWN_PLANES), x, radius, (WIDE - n_rows) // 2, n_rows, post, column
         )
 
 
@@ -421,15 +454,15 @@
     second = every(rad[...], 1)
     skip = (n_rows - MID) // 2
     shear_out[...] = advance(
-        held, 3, g_a, 1, links_in, bits_in, second, skip, None, post_b, 0
-    ) + advance(held, 4, g_b, 0, links_in, bits_in, second, skip, None, post_b, 1)
+        held, 3, (g_a, OWN_PLANES), 1, links_in, bits_in, second, skip, None, post_b, 0
+    ) + advance(held, 4, (g_b, OWN_PLANES), 0, links_in, bits_in, second, skip, None, post_b, 1)
 
 
 def two_steps_kernel(
     h_l, h_r, g_hl, g_a, g_b, g_hr, bits_in, links_in, rad, rad_l, rad_r, own_a, own_b, shear_in,
     f_l, f_r, send_l, send_r, send, post_a, post_b, *, n_rows, last_halo,
 ):
-    fields = (g_hl, g_a, g_b, g_hr)
+    fields = g_hl, g_a, g_b, g_hr = fields_of(g_hl, g_a, g_b, g_hr)
     top = (WIDE - n_rows) // 2
     skip = (n_rows - MID) // 2
     collide_all(in_halo(h_l), g_hl, 1, every(rad_l[...], 0), top, n_rows, post_a, 1)
@@ -477,7 +510,7 @@
 
 
 def last_kernel(h_l, h_r, g_hl, g_a, g_b, g_hr, bits_in, rad_l, rad_r, own_post, density, velocity, post):
-    fields = (g_hl, g_a, g_b, g_hr)
+    fields = g_hl, g_a, g_b, g_hr = fields_of(g_hl, g_a, g_b, g_hr)
     top = (WIDE - MID) // 2
     collide_far(h_l, 0, 1, g_hl, 1, top, every(rad_l[...], 0), MID, post, 0)
     collide_far(h_r, 0, -1, g_hr, 0, top, every(rad_r[...], 0), MID, post, 1)
@@ -492,7 +525,7 @@
             velocity[k, column - 2] = u[k]
 
 
-def call(kernel, outs, scratch=(), scalars=0, mib=1, plain_out=False):
+def call(kernel, outs, scratch=(), scalars=0, mib=1, plain_out=False, aliases=()):
     vmem = pl.BlockSpec(memory_space=pltpu.VMEM)
     smem = pl.BlockSpec(memory_space=pltpu.SMEM)
 
@@ -507,6 +540,7 @@
             in_specs=[smem] * scalars + [vmem] * (len(args) - scalars),
             out_specs=[vmem] * len(outs),
             scratch_shapes=[pltpu.VMEM(shape, dtype) for shape, dtype in scratch],
+            input_output_aliases=dict(aliases),
             compiler_params=pltpu.CompilerParams(vmem_limit_bytes=mib << 20),
         )(*args)
 
@@ -525,7 +559,9 @@
         size = lax.axis_size("gx")
         up = [(i, (i + 1) % size) for i in range(size)]
         down = [(target, source) for source, target in up]
-        return lax.ppermute(high, "gx", up), lax.ppermute(low, "gx", down)
+        before = lax.ppermute(high, "gx", up)
+        after = lax.ppermute(low, "gx", down)
+        return before, after
 
     def exchange(blocks):
         return lax.all_to_all(blocks, GY, split_axis=0, concat_axis=0, tiled=True)
@@ -547,9 +583,10 @@
     backward = [(target, source) for source, target in forward]
     low = lax.ppermute(own, GY, forward)
     high = lax.ppermute(own, GY, backward)
-    pair = ((BASE_ROW + TILE, LANES), F32)
-    g_l, g_r = call(rows_kernel, [pair, pair])(low, own, high, base_in)
-    g_hl, g_hr = ring(g_l, g_r)
+    pair = ((len(OWN_PLANES) * WIDE + TILE, LANES), F32)
+    near_far = ((len(NEAR_FAR) * WIDE + TILE, LANES), F32)
+    g_l, g_r, go_l, go_r = call(rows_kernel, [pair, pair, near_far, near_far])(low, own, high, base_in)
+    g_hl, g_hr = ring(go_l, go_r)
     fields = (g_hl, g_l, g_r, g_hr)
 
     def posts(columns, rows):
@@ -558,28 +595,29 @@
     def opens(columns):
         return ((3, columns, WIDE + 2 * PAD, LANES), jnp.int32)
 
-    post_own, open_own = call(first_own_kernel, [posts(4, WIDE), opens(4)])(g_l, g_r)
-
     def populations(rows):
         return [((19, 2, rows, LANES), F32)] * 2
 
     def halos(rows, last=False):
         return [((FAR if last else 19 + FAR, rows, LANES), F32)] * 2
 
+    shared = [
+        *populations(WIDE),
+        *halos(WIDE),
+        ((6, WIDE, LANES), jnp.int32),
+        ((4, WIDE, LANES), F32),
+    ]
+    post_own, open_own, *begun, sums = call(
+        first_own_kernel, [posts(4, WIDE), opens(4), *shared, ((3, TILE, LANES), F32)]
+    )(g_l, g_r)
     f_l, f_r, send_l, send_r, bits, links, send, base = call(
         first_kernel,
-        [
-            *populations(WIDE),
-            *halos(WIDE),
-            ((6, WIDE, LANES), jnp.int32),
-            ((4, WIDE, LANES), F32),
-            sends,
-            tile,
-        ],
+        [*shared, sends, tile],
         [posts(2, WIDE), opens(4)],
         scalars=1,
         mib=3,
-    )(edge, *fields, post_own, open_own)
+        aliases=[(8 + k, k) for k in range(6)],
+    )(edge, *fields, post_own, open_own, sums, *begun)
 
     for turn in range(3):
         gathered = exchange(send)

time: 96.4 us -> 96.4 us (level)
  blocking collectives: 43 us -> 22 us
  starting transfers between devices: 29.9 us -> 44.7 us
  waiting for transfers between devices: 15.1 us -> 20.8 us
    all_to_all x3 -> x2, blocking collectives: 43 us -> 22 us  [exchange(): return lax.all_to_all(blocks, GY, split_axis=0, concat_axis=0, tiled=True)]
    all_to_all x1 -> x2, starting transfers between devices: 4.83 us -> 20.3 us  [exchange(): return lax.all_to_all(blocks, GY, split_axis=0, concat_axis=0, tiled=True)]
    all_to_all x1 -> x2, waiting for transfers between devices: 3.33 us -> 9.66 us  [exchange(): return lax.all_to_all(blocks, GY, split_axis=0, concat_axis=0, tiled=True)]
  transfers between devices with their start and end apart: 17 -> 18, of which waited for: 7 -> 8; matrix products, arithmetic and copies ran while one was open for 1% -> 1% of each run, Pallas kernels for 2% -> 2%
where the time goes in v3:
time: 96.4 us; the launch traced here: 96 us
  starting transfers between devices  44.7 us (46%)
  blocking collectives  22 us (23%)
  waiting for transfers between devices  20.8 us (22%)
  Pallas kernels  7 us (7%)
    all_to_all x2, blocking collectives, exchange(): return lax.all_to_all(blocks, GY, split_axis=0, concat_axis=0, tiled=True)  22 us
    all_to_all x2, starting transfers between devices, exchange(): return lax.all_to_all(blocks, GY, split_axis=0, concat_axis=0, tiled=True)  20.3 us
    ppermute x7, starting transfers between devices, ring(): after = lax.ppermute(low, 'gx', down)  16 us
    ppermute x7, waiting for transfers between devices, ring(): before = lax.ppermute(high, 'gx', up)  10.5 us
    all_to_all x2, waiting for transfers between devices, exchange(): return lax.all_to_all(blocks, GY, split_axis=0, concat_axis=0, tiled=True)  9.66 us
    pallas_call x12, Pallas kernels, run(): pl.pallas_call(kernel, out_shape=[held(shape, dtype) for shape, dtype in...  5.59 us
    ppermute x1, starting transfers between devices, step_all(): high = lax.ppermute(own, GY, backward)  4.89 us
  transfers between devices with their start and end apart: 18, of which 8 were waited for; matrix products, arithmetic and copies ran while one was open for 1% of the time, Pallas kernels for 2%

profile of v3, /device:TPU:2, one launch (start us, length us, event | category | flops | bytes accessed | tf_op | source)
XLA Modules:
  0.0 96.0 jit_solution(1632322737089469238)
XLA Ops:
  0.6 1.4 %shard_map.76 = (f32[5,4,8,128]{3,2,1,0:T(8,128)S(1)}, f32[16,8,128]{2,1,0:T(8,128)}) custom-call(s32[1]{0:T(128)} %bitcast.2.place_ref, f32[4,8,128]{2,1,0:T(8,128)} %density.1, f32[3,4,8,128]{3,2,1,0:T(8,128)} %velocity.1, s32[4,8,128]{2,1,0:T(8,128)} %mask.1, s32[4,8]{1,0:T(4,128)} %unit.1, f32[1,8]{1,0:T(1,128)} %bitcast.6), custom_call_target="tpu_custom_call" | custom-call | tf_op jit(solution)/shard_map/pallas_call | solution.py:571
  2.1 4.9 %collective-permute-start.1 = (f32[5,4,8,128]{3,2,1,0:T(8,128)S(1)}, f32[5,4,8,128]{3,2,1,0:T(8,128)S(1)}, u32[]{:S(2)}, u32[]{:S(2)}) collective-permute-start(f32[5,4,8,128]{3,2,1,0:T(8,128)S(1)} %get-tuple-element.46.own), channel_id=1, source_target_pairs={{1,0},{2,1},{3,2},{4,3},{5,4},{6,5},{7,6},{8,7},{9,8},{10,9},{11,1... | collective-permute-start | bytes 245768 | tf_op jit(solution)/shard_map/ppermute | solution.py:585
  7.0 1.9 %collective-permute-start = (f32[5,4,8,128]{3,2,1,0:T(8,128)S(1)}, f32[5,4,8,128]{3,2,1,0:T(8,128)S(1)}, u32[]{:S(2)}, u32[]{:S(2)}) collective-permute-start(f32[5,4,8,128]{3,2,1,0:T(8,128)S(1)} %get-tuple-element.46.own), channel_id=1, source_target_pairs={{0,1},{1,2},{2,3},{3,4},{4,5},{5,6},{6,7},{7,8},{8,9},{9,10},{10,1... | collective-permute-start | bytes 245768 | tf_op jit(solution)/shard_map/ppermute | solution.py:584
  8.9 15.5 %all-to-all-start = ((f32[16,8,128]{2,1,0:T(8,128)}), f32[16,8,128]{2,1,0:T(8,128)S(1)}, u32[]{:S(2)}, u32[]{:S(2)}) async-start(f32[16,8,128]{2,1,0:T(8,128)} %get-tuple-element.47), calls=%async_computation | async-start | bytes 131072 | tf_op jit(solution)/shard_map/all_to_all | solution.py:567
  24.4 6.3 %all-to-all-done.base_in = f32[16,8,128]{2,1,0:T(8,128)S(1)} async-done(((f32[16,8,128]{2,1,0:T(8,128)}), f32[16,8,128]{2,1,0:T(8,128)S(1)}, u32[]{:S(2)}, u32[]{:S(2)}) %all-to-all-start) | async-done | bytes 65568 | tf_op jit(solution)/shard_map/all_to_all | solution.py:567
  30.8 7.1 %collective-permute-start.3 = (f32[176,128]{1,0:T(8,128)S(1)}, f32[176,128]{1,0:T(8,128)S(1)}, u32[]{:S(2)}, u32[]{:S(2)}) collective-permute-start(f32[176,128]{1,0:T(8,128)S(1)} %get-tuple-element.51), channel_id=1, source_target_pairs={{16,0},{32,16},{48,32},{64,48},{80,64},{96,80},{112,96},{128,112},... | collective-permute-start | bytes 270344 | tf_op jit(solution)/shard_map/ppermute | solution.py:563
  38.3 1.7 %collective-permute-done.2.halo_l.g_hl = f32[176,128]{1,0:T(8,128)S(1)} collective-permute-done((f32[176,128]{1,0:T(8,128)S(1)}, f32[176,128]{1,0:T(8,128)S(1)}, u32[]{:S(2)}, u32[]{:S(2)}) %collective-permute-start.2) | collective-permute-done | bytes 90144 | tf_op jit(solution)/shard_map/ppermute | solution.py:562
  40.1 0.9 shard_map.79
  41.0 3.0 %collective-permute-start.5 = (f32[28,24,128]{2,1,0:T(8,128)S(1)}, f32[28,24,128]{2,1,0:T(8,128)S(1)}, u32[]{:S(2)}, u32[]{:S(2)}) collective-permute-start(f32[28,24,128]{2,1,0:T(8,128)S(1)} %get-tuple-element.62), channel_id=1, source_target_pairs={{16,0},{32,16},{48,32},{64,48},{80,64},{96,80},{112,96},{128,112},... | collective-permute-start | bytes 1032200 | tf_op jit(solution)/shard_map/ppermute | solution.py:563
  44.0 11.2 %all_to_all.20.gathered = f32[16,8,128]{2,1,0:T(8,128)S(1)} all-to-all(f32[16,8,128]{2,1,0:T(8,128)S(1)} %get-tuple-element.65), channel_id=1, replica_groups=mesh['gx'=64,'gy_0'=4,'gy_1'=4] {'gy_0','gy_1'}, dimensions={0} | all-to-all | bytes 131072 | tf_op jit(solution)/shard_map/all_to_all | solution.py:567
  55.2 0.5 collective-permute-start.6
  55.7 0.6 shard_map.81
  56.5 2.9 %collective-permute-done.6.rad_l = f32[8,128]{1,0:T(8,128)S(1)} collective-permute-done((f32[8,128]{1,0:T(8,128)S(1)}, f32[8,128]{1,0:T(8,128)S(1)}, u32[]{:S(2)}, u32[]{:S(2)}) %collective-permute-start.6) | collective-permute-done | bytes 4128 | tf_op jit(solution)/shard_map/ppermute | solution.py:562
  59.5 0.8 shard_map.82
  60.3 2.9 %collective-permute-start.9 = (f32[28,16,128]{2,1,0:T(8,128)S(1)}, f32[28,16,128]{2,1,0:T(8,128)S(1)}, u32[]{:S(2)}, u32[]{:S(2)}) collective-permute-start(f32[28,16,128]{2,1,0:T(8,128)S(1)} %get-tuple-element.74), channel_id=1, source_target_pairs={{16,0},{32,16},{48,32},{64,48},{80,64},{96,80},{112,96},{128,112},... | collective-permute-start | bytes 688136 | tf_op jit(solution)/shard_map/ppermute | solution.py:563
  63.2 10.9 %all_to_all.21.gathered = f32[16,8,128]{2,1,0:T(8,128)S(1)} all-to-all(f32[16,8,128]{2,1,0:T(8,128)S(1)} %get-tuple-element.75), channel_id=1, replica_groups=mesh['gx'=64,'gy_0'=4,'gy_1'=4] {'gy_0','gy_1'}, dimensions={0} | all-to-all | bytes 131072 | tf_op jit(solution)/shard_map/all_to_all | solution.py:567
  75.5 2.9 %collective-permute-done.10.rad_l = f32[8,128]{1,0:T(8,128)S(1)} collective-permute-done((f32[8,128]{1,0:T(8,128)S(1)}, f32[8,128]{1,0:T(8,128)S(1)}, u32[]{:S(2)}, u32[]{:S(2)}) %collective-permute-start.10) | collective-permute-done | bytes 4128 | tf_op jit(solution)/shard_map/ppermute | solution.py:562
  78.4 1.4 %shard_map.85 = (f32[19,2,16,128]{3,2,1,0:T(8,128)S(1)}, f32[19,2,16,128]{3,2,1,0:T(8,128)S(1)}, f32[9,16,128]{2,1,0:T(8,128)S(1)}, f32[9,16,128]{2,1,0:T(8,128)S(1)}, f32[16,8,128]{2,1,0:T(8,128)}) custom-call(f32[28,16,128]{2,1,0:T(8,128)S(1)} %collective-permute-done.8.h_l, f32[28,16,128]{2,1,0:T(8,128)S(1)} %collective-permute-done.9.h_r, ...), custom_call_target="tpu_custom_call" | custom-call | tf_op jit(solution)/shard_map/pallas_call | solution.py:537
  79.8 4.8 %all-to-all-start.3 = ((f32[16,8,128]{2,1,0:T(8,128)}), f32[16,8,128]{2,1,0:T(8,128)S(1)}, u32[]{:S(2)}, u32[]{:S(2)}) async-start(f32[16,8,128]{2,1,0:T(8,128)} %get-tuple-element.84), calls=%async_computation.3 | async-start | bytes 131072 | tf_op jit(solution)/shard_map/all_to_all | solution.py:567
  84.6 2.9 %collective-permute-start.13 = (f32[9,16,128]{2,1,0:T(8,128)S(1)}, f32[9,16,128]{2,1,0:T(8,128)S(1)}, u32[]{:S(2)}, u32[]{:S(2)}) collective-permute-start(f32[9,16,128]{2,1,0:T(8,128)S(1)} %get-tuple-element.83), channel_id=1, source_target_pairs={{16,0},{32,16},{48,32},{64,48},{80,64},{96,80},{112,96},{128,112},... | collective-permute-start | bytes 221192 | tf_op jit(solution)/shard_map/ppermute | solution.py:563
  87.6 3.3 %all-to-all-done.3.gathered = f32[16,8,128]{2,1,0:T(8,128)S(1)} async-done(((f32[16,8,128]{2,1,0:T(8,128)}), f32[16,8,128]{2,1,0:T(8,128)S(1)}, u32[]{:S(2)}, u32[]{:S(2)}) %all-to-all-start.3) | async-done | bytes 65568 | tf_op jit(solution)/shard_map/all_to_all | solution.py:567
  91.5 0.6 dynamic-slice_bitcast_fusion
  92.3 2.9 %collective-permute-done.14.rad_l = f32[8,128]{1,0:T(8,128)S(1)} collective-permute-done((f32[8,128]{1,0:T(8,128)S(1)}, f32[8,128]{1,0:T(8,128)S(1)}, u32[]{:S(2)}, u32[]{:S(2)}) %collective-permute-start.14) | collective-permute-done | bytes 4128 | tf_op jit(solution)/shard_map/ppermute | solution.py:562
  95.2 0.8 shard_map.88
  (30 shorter events, 2.9 us)
Async XLA Ops:
  2.1 28.7 %collective-permute-start.1 = (f32[5,4,8,128]{3,2,1,0:T(8,128)S(1)}, f32[5,4,8,128]{3,2,1,0:T(8,128)S(1)}, u32[]{:S(2)}, u32[]{:S(2)}) collective-permute-start(f32[5,4,8,128]{3,2,1,0:T(8,128)S(1)} %get-tuple-element.46.own), channel_id=1, source_target_pairs={{1,0},{2,1},{3,2},{4,3},{5,4},{6,5},{7,6},{8,7},{9,8},{10,9},{11,1... | collective-permute-start | bytes 245768 | tf_op jit(solution)/shard_map/ppermute | solution.py:585
  7.0 23.8 %collective-permute-start = (f32[5,4,8,128]{3,2,1,0:T(8,128)S(1)}, f32[5,4,8,128]{3,2,1,0:T(8,128)S(1)}, u32[]{:S(2)}, u32[]{:S(2)}) collective-permute-start(f32[5,4,8,128]{3,2,1,0:T(8,128)S(1)} %get-tuple-element.46.own), channel_id=1, source_target_pairs={{0,1},{1,2},{2,3},{3,4},{4,5},{5,6},{6,7},{7,8},{8,9},{9,10},{10,1... | collective-permute-start | bytes 245768 | tf_op jit(solution)/shard_map/ppermute | solution.py:584
  8.9 21.8 %all-to-all-start = ((f32[16,8,128]{2,1,0:T(8,128)}), f32[16,8,128]{2,1,0:T(8,128)S(1)}, u32[]{:S(2)}, u32[]{:S(2)}) async-start(f32[16,8,128]{2,1,0:T(8,128)} %get-tuple-element.47), calls=%async_computation | async-start | bytes 131072 | tf_op jit(solution)/shard_map/all_to_all | solution.py:567
  30.7 9.3 %collective-permute-start.2 = (f32[176,128]{1,0:T(8,128)S(1)}, f32[176,128]{1,0:T(8,128)S(1)}, u32[]{:S(2)}, u32[]{:S(2)}) collective-permute-start(f32[176,128]{1,0:T(8,128)S(1)} %get-tuple-element.48), channel_id=1, source_target_pairs={{0,16},{16,32},{32,48},{48,64},{64,80},{80,96},{96,112},{112,128},... | collective-permute-start | bytes 270344 | tf_op jit(solution)/shard_map/ppermute | solution.py:562
  30.8 9.3 %collective-permute-start.3 = (f32[176,128]{1,0:T(8,128)S(1)}, f32[176,128]{1,0:T(8,128)S(1)}, u32[]{:S(2)}, u32[]{:S(2)}) collective-permute-start(f32[176,128]{1,0:T(8,128)S(1)} %get-tuple-element.51), channel_id=1, source_target_pairs={{16,0},{32,16},{48,32},{64,48},{80,64},{96,80},{112,96},{128,112},... | collective-permute-start | bytes 270344 | tf_op jit(solution)/shard_map/ppermute | solution.py:563
  41.0 18.5 %collective-permute-start.4 = (f32[28,24,128]{2,1,0:T(8,128)S(1)}, f32[28,24,128]{2,1,0:T(8,128)S(1)}, u32[]{:S(2)}, u32[]{:S(2)}) collective-permute-start(f32[28,24,128]{2,1,0:T(8,128)S(1)} %get-tuple-element.61), channel_id=1, source_target_pairs={{0,16},{16,32},{32,48},{48,64},{64,80},{80,96},{96,112},{112,128},... | collective-permute-start | bytes 1032200 | tf_op jit(solution)/shard_map/ppermute | solution.py:562
  41.0 18.5 %collective-permute-start.5 = (f32[28,24,128]{2,1,0:T(8,128)S(1)}, f32[28,24,128]{2,1,0:T(8,128)S(1)}, u32[]{:S(2)}, u32[]{:S(2)}) collective-permute-start(f32[28,24,128]{2,1,0:T(8,128)S(1)} %get-tuple-element.62), channel_id=1, source_target_pairs={{16,0},{32,16},{48,32},{64,48},{80,64},{96,80},{112,96},{128,112},... | collective-permute-start | bytes 1032200 | tf_op jit(solution)/shard_map/ppermute | solution.py:563
  55.2 1.3 %collective-permute-start.7 = (f32[8,128]{1,0:T(8,128)S(1)}, f32[8,128]{1,0:T(8,128)S(1)}, u32[]{:S(2)}, u32[]{:S(2)}) collective-permute-start(f32[8,128]{1,0:T(8,128)S(1)} %get-tuple-element.67.rad), channel_id=1, source_target_pairs={{16,0},{32,16},{48,32},{64,48},{80,64},{96,80},{112,96},{128,112},... | collective-permute-start | bytes 12296 | tf_op jit(solution)/shard_map/ppermute | solution.py:563
  55.2 4.3 %collective-permute-start.6 = (f32[8,128]{1,0:T(8,128)S(1)}, f32[8,128]{1,0:T(8,128)S(1)}, u32[]{:S(2)}, u32[]{:S(2)}) collective-permute-start(f32[8,128]{1,0:T(8,128)S(1)} %get-tuple-element.67.rad), channel_id=1, source_target_pairs={{0,16},{16,32},{32,48},{48,64},{64,80},{80,96},{96,112},{112,128},... | collective-permute-start | bytes 12296 | tf_op jit(solution)/shard_map/ppermute | solution.py:562
  60.3 18.1 %collective-permute-start.8 = (f32[28,16,128]{2,1,0:T(8,128)S(1)}, f32[28,16,128]{2,1,0:T(8,128)S(1)}, u32[]{:S(2)}, u32[]{:S(2)}) collective-permute-start(f32[28,16,128]{2,1,0:T(8,128)S(1)} %get-tuple-element.73), channel_id=1, source_target_pairs={{0,16},{16,32},{32,48},{48,64},{64,80},{80,96},{96,112},{112,128},... | collective-permute-start | bytes 688136 | tf_op jit(solution)/shard_map/ppermute | solution.py:562
  60.3 18.1 %collective-permute-start.9 = (f32[28,16,128]{2,1,0:T(8,128)S(1)}, f32[28,16,128]{2,1,0:T(8,128)S(1)}, u32[]{:S(2)}, u32[]{:S(2)}) collective-permute-start(f32[28,16,128]{2,1,0:T(8,128)S(1)} %get-tuple-element.74), channel_id=1, source_target_pairs={{16,0},{32,16},{48,32},{64,48},{80,64},{96,80},{112,96},{128,112},... | collective-permute-start | bytes 688136 | tf_op jit(solution)/shard_map/ppermute | solution.py:563
  74.1 1.3 %collective-permute-start.11 = (f32[8,128]{1,0:T(8,128)S(1)}, f32[8,128]{1,0:T(8,128)S(1)}, u32[]{:S(2)}, u32[]{:S(2)}) collective-permute-start(f32[8,128]{1,0:T(8,128)S(1)} %shard_map.83.rad), channel_id=1, source_target_pairs={{16,0},{32,16},{48,32},{64,48},{80,64},{96,80},{112,96},{128,112},... | collective-permute-start | bytes 12296 | tf_op jit(solution)/shard_map/ppermute | solution.py:563
  74.2 4.3 %collective-permute-start.10 = (f32[8,128]{1,0:T(8,128)S(1)}, f32[8,128]{1,0:T(8,128)S(1)}, u32[]{:S(2)}, u32[]{:S(2)}) collective-permute-start(f32[8,128]{1,0:T(8,128)S(1)} %shard_map.83.rad), channel_id=1, source_target_pairs={{0,16},{16,32},{32,48},{48,64},{64,80},{80,96},{96,112},{112,128},... | collective-permute-start | bytes 12296 | tf_op jit(solution)/shard_map/ppermute | solution.py:562
  79.8 11.1 %all-to-all-start.3 = ((f32[16,8,128]{2,1,0:T(8,128)}), f32[16,8,128]{2,1,0:T(8,128)S(1)}, u32[]{:S(2)}, u32[]{:S(2)}) async-start(f32[16,8,128]{2,1,0:T(8,128)} %get-tuple-element.84), calls=%async_computation.3 | async-start | bytes 131072 | tf_op jit(solution)/shard_map/all_to_all | solution.py:567
  84.6 10.6 %collective-permute-start.12 = (f32[9,16,128]{2,1,0:T(8,128)S(1)}, f32[9,16,128]{2,1,0:T(8,128)S(1)}, u32[]{:S(2)}, u32[]{:S(2)}) collective-permute-start(f32[9,16,128]{2,1,0:T(8,128)S(1)} %get-tuple-element.82), channel_id=1, source_target_pairs={{0,16},{16,32},{32,48},{48,64},{64,80},{80,96},{96,112},{112,128},... | collective-permute-start | bytes 221192 | tf_op jit(solution)/shard_map/ppermute | solution.py:562
  84.6 10.6 %collective-permute-start.13 = (f32[9,16,128]{2,1,0:T(8,128)S(1)}, f32[9,16,128]{2,1,0:T(8,128)S(1)}, u32[]{:S(2)}, u32[]{:S(2)}) collective-permute-start(f32[9,16,128]{2,1,0:T(8,128)S(1)} %get-tuple-element.83), channel_id=1, source_target_pairs={{16,0},{32,16},{48,32},{64,48},{80,64},{96,80},{112,96},{128,112},... | collective-permute-start | bytes 221192 | tf_op jit(solution)/shard_map/ppermute | solution.py:563
  90.9 1.3 %collective-permute-start.15 = (f32[8,128]{1,0:T(8,128)S(1)}, f32[8,128]{1,0:T(8,128)S(1)}, u32[]{:S(2)}, u32[]{:S(2)}) collective-permute-start(f32[8,128]{1,0:T(8,128)S(1)} %shard_map.86.rad), channel_id=1, source_target_pairs={{16,0},{32,16},{48,32},{64,48},{80,64},{96,80},{112,96},{128,112},... | collective-permute-start | bytes 12296 | tf_op jit(solution)/shard_map/ppermute | solution.py:563
  91.0 4.3 %collective-permute-start.14 = (f32[8,128]{1,0:T(8,128)S(1)}, f32[8,128]{1,0:T(8,128)S(1)}, u32[]{:S(2)}, u32[]{:S(2)}) collective-permute-start(f32[8,128]{1,0:T(8,128)S(1)} %shard_map.86.rad), channel_id=1, source_target_pairs={{0,16},{16,32},{32,48},{48,64},{64,80},{80,96},{96,112},{112,128},... | collective-permute-start | bytes 12296 | tf_op jit(solution)/shard_map/ppermute | solution.py:562

commit v4 on v3

--- a/solution.py
+++ b/solution.py
@@ -219,6 +219,13 @@
 def send_all(ref, tile):
     for j in range(ref.shape[0]):
         ref[j] = tile
+
+
+def send_off(send, send_v, sem, sums):
+    send_all(send_v, row_pick([sublane_total(v) for v in sums]))
+    store = pltpu.make_async_copy(send_v, send, sem)
+    store.start()
+    return store
 
 
 def sum_of(ref):
@@ -260,15 +267,16 @@
     store.wait()
 
 
-def rows_kernel(low, own, high, base_in, left_out, right_out, left_send, right_send):
+def rows_kernel(odd_ref, first, own, second, base_in, left_out, right_out, left_send, right_send):
     base = sum_of(base_in)
+    odd = odd_ref[0] == 1
     for half, out, send, planes in (
         (0, left_out, left_send, NEAR_FAR),
         (1, right_out, right_send, LEFT_PLANES),
     ):
         for (k, x), plane in OWN_PLANES.items():
-            for part, ref in enumerate((low, own, high)):
-                value = ref[k, 2 * half + x]
+            here, a, b = (ref[k, 2 * half + x] for ref in (own, first, second))
+            for part, value in enumerate((jnp.where(odd, a, b), here, jnp.where(odd, b, a))):
                 out[pl.ds(plane * WIDE + part * TILE, TILE), :] = value
                 if (k, x) in planes:
                     send[pl.ds(planes[k, x] * WIDE + part * TILE, TILE), :] = value
@@ -302,14 +310,13 @@
             post[i, slot, pl.ds(PAD + t * TILE, TILE), :] = values[i]
 
 
-def stream_first(post, open_, column, held, x, f_out, send_near, send_far, side, links_out):
+def stream_first(post, open_, column, held, x, f_out, send_near, send_far, side, links_out, bits_out, tiles):
     sums = None
-    bits_of = []
-    for t in range(WIDE // TILE):
+    for t in tiles:
         row = PAD + t * TILE
         rows = pl.ds(t * TILE, TILE)
         bits, count = open_bits(open_, column, row)
-        bits_of.append(bits)
+        bits_out[column - 1, rows, :] = bits
         f = pulled(post, column, row, bits)
         put_all(f_out.at[:, x], rows, f)
         fluid = field(held, 0, x, t * TILE) > 0.0
@@ -327,7 +334,7 @@
         unit = field(held, 4, x, t * TILE)
         start = [field(held, 1 + k, x, t * TILE) for k in range(3)]
         sums = [by_unit(v, unit) for v in (links * square(start), links * square(u), links)]
-    return bits_of, sums
+    return sums
 
 
 def open_bits(open_, column, row):
@@ -341,11 +348,6 @@
     return bits, count
 
 
-def put_bits(bits_out, column, bits_of):
-    for t, bits in enumerate(bits_of):
-        bits_out[column - 1, pl.ds(t * TILE, TILE), :] = bits
-
-
 def first_own_kernel(left, right, post, open_, f_l, f_r, send_l, send_r, bits_out, links_out, sums_out):
     pairs = ((left, OWN_PLANES), (right, OWN_PLANES))
     for column in range(4):
@@ -354,10 +356,9 @@
         mark_open(open_, column, pairs[part], x, None)
     held = {2 + k: (post, k) for k in range(4)}
     seen = {2 + k: (open_, k) for k in range(4)}
-    bits, sums_a = stream_first(held, seen, 3, pairs[0], 1, f_l, None, send_l, -1, links_out)
-    put_bits(bits_out, 3, bits)
-    bits, sums_b = stream_first(held, seen, 4, pairs[1], 0, f_r, None, send_r, 1, links_out)
-    put_bits(bits_out, 4, bits)
+    tiles = range(WIDE // TILE)
+    sums_a = stream_first(held, seen, 3, pairs[0], 1, f_l, None, send_l, -1, links_out, bits_out, tiles)
+    sums_b = stream_first(held, seen, 4, pairs[1], 0, f_r, None, send_r, 1, links_out, bits_out, tiles)
     for k in range(3):
         sums_out[k] = sums_a[k] + sums_b[k]
 
@@ -365,7 +366,7 @@
 def first_kernel(
     edge_ref, halo_l, left, right, halo_r, post_own, open_own, sums_in, *rest
 ):
-    f_l, f_r, send_l, send_r, bits_out, links_out, send, base_out, post_halo, open_halo = rest[6:]
+    f_l, f_r, send_l, send_r, bits_out, links_out, send, base_out, post_halo, open_halo, send_v, sem = rest[6:]
     fields = fields_of(halo_l, left, right, halo_r)
     base_out[...] = base_of(fields[1])
     post = {1: (post_halo, 0), 6: (post_halo, 1)} | {2 + k: (post_own, k) for k in range(4)}
@@ -376,13 +377,18 @@
         mark_open(open_halo, 2 + x, fields[3], x, edge_ref[1])
     start_column(post_halo, 0, fields[0], 1, base_of(fields[0]), TOWARD[1])
     start_column(post_halo, 1, fields[3], 0, base_of(fields[3]), TOWARD[-1])
+    outer = ((2, fields[1], 0, f_l, send_l), (5, fields[2], 1, f_r, send_r))
+    sums = [sums_in[k] for k in range(3)]
+    for column, held, x, f_out, near in outer:
+        part = stream_first(post, open_, column, held, x, f_out, near, None, None, links_out, bits_out, (1,))
+        sums = [a + b for a, b in zip(sums, part)]
+    store = send_off(send, send_v, sem, sums)
+    for column, held, x, f_out, near in outer:
+        stream_first(post, open_, column, held, x, f_out, near, None, None, links_out, bits_out, (0, 2))
     for column in (1, 6):
-        put_bits(bits_out, column, [open_bits(open_, column, PAD + t * TILE)[0] for t in range(WIDE // TILE)])
-    bits, sums_a = stream_first(post, open_, 2, fields[1], 0, f_l, send_l, None, None, links_out)
-    put_bits(bits_out, 2, bits)
-    bits, sums_b = stream_first(post, open_, 5, fields[2], 1, f_r, send_r, None, None, links_out)
-    put_bits(bits_out, 5, bits)
-    send_all(send, row_pick([sublane_total(sums_in[k] + sums_a[k] + sums_b[k]) for k in range(3)]))
+        for t in range(WIDE // TILE):
+            bits_out[column - 1, pl.ds(t * TILE, TILE), :] = open_bits(open_, column, PAD + t * TILE)[0]
+    store.wait()
 
 
 def response_kernel(gathered, base, links_in, radius_out, links_out=None):
@@ -460,7 +466,7 @@
 
 def two_steps_kernel(
     h_l, h_r, g_hl, g_a, g_b, g_hr, bits_in, links_in, rad, rad_l, rad_r, own_a, own_b, shear_in,
-    f_l, f_r, send_l, send_r, send, post_a, post_b, *, n_rows, last_halo,
+    f_l, f_r, send_l, send_r, send, post_a, post_b, send_v, sem, *, n_rows, last_halo,
 ):
     fields = g_hl, g_a, g_b, g_hr = fields_of(g_hl, g_a, g_b, g_hr)
     top = (WIDE - n_rows) // 2
@@ -479,6 +485,13 @@
     shear_a += advance(held, 2, g_a, 0, links_in, bits_in, own, skip, None, post_b, 1)
     shear_a += advance(held, 5, g_b, 1, links_in, bits_in, own, skip, None, post_b, 2)
     held = {1: (post_b, 0), 2: (post_b, 1), 3: (own_b, 0), 4: (own_b, 1), 5: (post_b, 2), 6: (post_b, 3)}
+    own = pl.ds(TILE, TILE)
+    for column in range(2, 6):
+        part, x = divmod(column, 2)
+        f = pulled(held, column, PAD + (MID - TILE) // 2, bits_in[column - 1, own, :])
+        _, u = moments(f, field(fields[part], 0, x, TILE) > 0.0)
+        shear_b += by_unit(links_in[column - 2, own, :] * square(u), field(fields[part], 4, x, TILE))
+    store = send_off(send, send_v, sem, (shear_a, shear_b))
     for column in range(2, 6):
         part, x = divmod(column, 2)
         out = f_l if part == 1 else f_r
@@ -489,7 +502,8 @@
             f = pulled(held, column, PAD + t * TILE, bits_in[column - 1, near, :])
             for i in range(19):
                 out[i, x, rows, :] = f[i]
-            rho, u = moments(f, field(fields[part], 0, x, row) > 0.0)
+            if column in ((2, 5) if last_halo else (3, 4)):
+                rho, u = moments(f, field(fields[part], 0, x, row) > 0.0)
             if last_halo:
                 if column == 2:
                     put_far(send_l, 0, rows, -1, f, rho, u)
@@ -503,10 +517,7 @@
                 put_far(send_r, 19, rows, 1, f, rho, u)
             else:
                 put_all(send_r, rows, f)
-            shear_b = shear_b + by_unit(
-                shear(links_in[column - 2, near, :], square(u)), field(fields[part], 4, x, row)
-            )
-    send_all(send, row_pick([sublane_total(s) for s in (shear_a, shear_b)]))
+    store.wait()
 
 
 def last_kernel(h_l, h_r, g_hl, g_a, g_b, g_hr, bits_in, rad_l, rad_r, own_post, density, velocity, post):
@@ -525,7 +536,7 @@
             velocity[k, column - 2] = u[k]
 
 
-def call(kernel, outs, scratch=(), scalars=0, mib=1, plain_out=False, aliases=()):
+def call(kernel, outs, scratch=(), scalars=0, mib=1, plain_out=False, aliases=(), hbm_out=None):
     vmem = pl.BlockSpec(memory_space=pltpu.VMEM)
     smem = pl.BlockSpec(memory_space=pltpu.SMEM)
 
@@ -536,10 +547,13 @@
         held = jax.ShapeDtypeStruct if plain_out else pltpu.VMEM
         return pl.pallas_call(
             kernel,
-            out_shape=[held(shape, dtype) for shape, dtype in outs],
+            out_shape=[
+                (jax.ShapeDtypeStruct if n == hbm_out else held)(shape, dtype) for n, (shape, dtype) in enumerate(outs)
+            ],
             in_specs=[smem] * scalars + [vmem] * (len(args) - scalars),
-            out_specs=[vmem] * len(outs),
-            scratch_shapes=[pltpu.VMEM(shape, dtype) for shape, dtype in scratch],
+            out_specs=[pl.BlockSpec(memory_space=pl.ANY) if n == hbm_out else vmem for n in range(len(outs))],
+            scratch_shapes=[pltpu.VMEM(shape, dtype) for shape, dtype in scratch]
+            + ([] if hbm_out is None else [pltpu.VMEM(*outs[hbm_out]), pltpu.SemaphoreType.DMA]),
             input_output_aliases=dict(aliases),
             compiler_params=pltpu.CompilerParams(vmem_limit_bytes=mib << 20),
         )(*args)
@@ -579,13 +593,16 @@
     )(place.reshape(1), *(pltpu.with_memory_space_constraint(a, pltpu.HBM) for a in arrays))
     base_in = exchange(base_send)
 
-    forward = [(i, i + 1) for i in range(count - 1)]
-    backward = [(target, source) for source, target in forward]
-    low = lax.ppermute(own, GY, forward)
-    high = lax.ppermute(own, GY, backward)
+    def swap(start):
+        pairs = [(i, i + 1) for i in range(start, count - 1, 2)]
+        return lax.ppermute(own, GY, pairs + [(b, a) for a, b in pairs])
+
+    swaps = swap(0), swap(1)
     pair = ((len(OWN_PLANES) * WIDE + TILE, LANES), F32)
     near_far = ((len(NEAR_FAR) * WIDE + TILE, LANES), F32)
-    g_l, g_r, go_l, go_r = call(rows_kernel, [pair, pair, near_far, near_far])(low, own, high, base_in)
+    g_l, g_r, go_l, go_r = call(rows_kernel, [pair, pair, near_far, near_far], scalars=1)(
+        (place % 2).reshape(1), swaps[0], own, swaps[1], base_in
+    )
     g_hl, g_hr = ring(go_l, go_r)
     fields = (g_hl, g_l, g_r, g_hr)
 
@@ -616,6 +633,7 @@
         [posts(2, WIDE), opens(4)],
         scalars=1,
         mib=3,
+        hbm_out=6,
         aliases=[(8 + k, k) for k in range(6)],
     )(edge, *fields, post_own, open_own, sums, *begun)
 
@@ -637,6 +655,7 @@
                 [*populations(MID), *halos(MID, last=turn == 1), sends],
                 [posts(4, rows), posts(4, MID)],
                 mib=4,
+                hbm_out=4,
             )(h_l, h_r, *fields, bits, links, rad, rad_l, rad_r, *own_part)
     (own_post,) = call(functools.partial(own_kernel, n_rows=MID, row=0), [posts(4, MID)])(
         f_l, f_r, g_l, g_r, rad

time: 96.4 us -> 94.9 us (0.984)
  starting transfers between devices: 44.7 us -> 42.9 us
    all_to_all x2, starting transfers between devices: 20.3 us -> 16.9 us  [exchange(): return lax.all_to_all(blocks, GY, split_axis=0, concat_axis=0, tiled=True)]
    ppermute x7, starting transfers between devices: 16 us -> 17.5 us  [ring(): after = lax.ppermute(low, 'gx', down)]
where the time goes in v4:
time: 94.9 us; the launch traced here: 94.5 us
  starting transfers between devices  42.9 us (45%)
  blocking collectives  22 us (23%)
  waiting for transfers between devices  20.8 us (22%)
  Pallas kernels  7.25 us (8%)
    all_to_all x2, blocking collectives, exchange(): return lax.all_to_all(blocks, GY, split_axis=0, concat_axis=0, tiled=True)  22 us
    ppermute x7, starting transfers between devices, ring(): after = lax.ppermute(low, 'gx', down)  17.5 us
    all_to_all x2, starting transfers between devices, exchange(): return lax.all_to_all(blocks, GY, split_axis=0, concat_axis=0, tiled=True)  16.9 us
    ppermute x7, waiting for transfers between devices, ring(): before = lax.ppermute(high, 'gx', up)  10.5 us
    all_to_all x2, waiting for transfers between devices, exchange(): return lax.all_to_all(blocks, GY, split_axis=0, concat_axis=0, tiled=True)  9.66 us
    ppermute x2, starting transfers between devices, swap(): return lax.ppermute(own, GY, pairs + [(b, a) for a, b in pairs])  6.97 us
    pallas_call x12, Pallas kernels, run(): pl.pallas_call(kernel, out_shape=[(jax.ShapeDtypeStruct if n == hbm_out e...  5.85 us
  transfers between devices with their start and end apart: 18, of which 8 were waited for; matrix products, arithmetic and copies ran while one was open for 1% of the time, Pallas kernels for 2%

profile of v4, /device:TPU:2, one launch (start us, length us, event | category | flops | bytes accessed | tf_op | source)
XLA Modules:
  0.0 94.5 jit_solution(8973382499780391335)
XLA Ops:
  0.6 1.4 %shard_map.76 = (f32[5,4,8,128]{3,2,1,0:T(8,128)S(1)}, f32[16,8,128]{2,1,0:T(8,128)}) custom-call(s32[1]{0:T(128)} %bitcast.3.place_ref, f32[4,8,128]{2,1,0:T(8,128)} %density.1, f32[3,4,8,128]{3,2,1,0:T(8,128)} %velocity.1, s32[4,8,128]{2,1,0:T(8,128)} %mask.1, s32[4,8]{1,0:T(4,128)} %unit.1, f32[1,8]{1,0:T(1,128)} %bitcast.7), custom_call_target="tpu_custom_call" | custom-call | tf_op jit(solution)/shard_map/pallas_call | solution.py:585
  2.1 4.9 %collective-permute-start.1 = (f32[5,4,8,128]{3,2,1,0:T(8,128)S(1)}, f32[5,4,8,128]{3,2,1,0:T(8,128)S(1)}, u32[]{:S(2)}, u32[]{:S(2)}) collective-permute-start(f32[5,4,8,128]{3,2,1,0:T(8,128)S(1)} %get-tuple-element.46.own), channel_id=1, source_target_pairs={{1,2},{3,4},{5,6},{7,8},{9,10},{11,12},{13,14},{2,1},{4,3},{6,5},{... | collective-permute-start | bytes 245768 | tf_op jit(solution)/shard_map/ppermute | solution.py:598
  7.0 2.1 %collective-permute-start = (f32[5,4,8,128]{3,2,1,0:T(8,128)S(1)}, f32[5,4,8,128]{3,2,1,0:T(8,128)S(1)}, u32[]{:S(2)}, u32[]{:S(2)}) collective-permute-start(f32[5,4,8,128]{3,2,1,0:T(8,128)S(1)} %get-tuple-element.46.own), channel_id=1, source_target_pairs={{0,1},{2,3},{4,5},{6,7},{8,9},{10,11},{12,13},{14,15},{1,0},{3,2},... | collective-permute-start | bytes 245768 | tf_op jit(solution)/shard_map/ppermute | solution.py:598
  9.0 12.1 %all-to-all-start = ((f32[16,8,128]{2,1,0:T(8,128)}), f32[16,8,128]{2,1,0:T(8,128)S(1)}, u32[]{:S(2)}, u32[]{:S(2)}) async-start(f32[16,8,128]{2,1,0:T(8,128)} %get-tuple-element.47), calls=%async_computation | async-start | bytes 131072 | tf_op jit(solution)/shard_map/all_to_all | solution.py:581
  21.1 6.3 %all-to-all-done.base_in = f32[16,8,128]{2,1,0:T(8,128)S(1)} async-done(((f32[16,8,128]{2,1,0:T(8,128)}), f32[16,8,128]{2,1,0:T(8,128)S(1)}, u32[]{:S(2)}, u32[]{:S(2)}) %all-to-all-start) | async-done | bytes 65568 | tf_op jit(solution)/shard_map/all_to_all | solution.py:581
  27.5 8.6 %collective-permute-start.3 = (f32[176,128]{1,0:T(8,128)S(1)}, f32[176,128]{1,0:T(8,128)S(1)}, u32[]{:S(2)}, u32[]{:S(2)}) collective-permute-start(f32[176,128]{1,0:T(8,128)S(1)} %get-tuple-element.51), channel_id=1, source_target_pairs={{16,0},{32,16},{48,32},{64,48},{80,64},{96,80},{112,96},{128,112},... | collective-permute-start | bytes 270344 | tf_op jit(solution)/shard_map/ppermute | solution.py:577
  36.5 1.7 %collective-permute-done.2.halo_l.g_hl = f32[176,128]{1,0:T(8,128)S(1)} collective-permute-done((f32[176,128]{1,0:T(8,128)S(1)}, f32[176,128]{1,0:T(8,128)S(1)}, u32[]{:S(2)}, u32[]{:S(2)}) %collective-permute-start.2) | collective-permute-done | bytes 90144 | tf_op jit(solution)/shard_map/ppermute | solution.py:576
  38.3 1.1 %shard_map.79 = (f32[19,2,24,128]{3,2,1,0:T(8,128)S(1)}, f32[19,2,24,128]{3,2,1,0:T(8,128)S(1)}, f32[28,24,128]{2,1,0:T(8,128)S(1)}, f32[28,24,128]{2,1,0:T(8,12...) custom-call(s32[2]{0:T(128)S(1)} %add_convert_fusion.edge_ref, ...), custom_call_target="tpu_custom_call", output_to_operand_aliasing={{0}: (8, {}), {1}: (9, {}), {2}: (10, {}), {3}: (11, {}), {... | custom-call | tf_op jit(solution)/shard_map/pallas_call | solution.py:548
  39.4 3.0 %collective-permute-start.5 = (f32[28,24,128]{2,1,0:T(8,128)S(1)}, f32[28,24,128]{2,1,0:T(8,128)S(1)}, u32[]{:S(2)}, u32[]{:S(2)}) collective-permute-start(f32[28,24,128]{2,1,0:T(8,128)S(1)} %get-tuple-element.62), channel_id=1, source_target_pairs={{16,0},{32,16},{48,32},{64,48},{80,64},{96,80},{112,96},{128,112},... | collective-permute-start | bytes 1032200 | tf_op jit(solution)/shard_map/ppermute | solution.py:577
  42.3 11.2 %all_to_all.20.gathered = f32[16,8,128]{2,1,0:T(8,128)S(1)} all-to-all(f32[16,8,128]{2,1,0:T(8,128)S(1)} %get-tuple-element.65), channel_id=1, replica_groups=mesh['gx'=64,'gy_0'=4,'gy_1'=4] {'gy_0','gy_1'}, dimensions={0} | all-to-all | bytes 131072 | tf_op jit(solution)/shard_map/all_to_all | solution.py:581
  53.6 0.5 collective-permute-start.6
  54.1 0.6 shard_map.81
  54.9 2.9 %collective-permute-done.6.rad_l = f32[8,128]{1,0:T(8,128)S(1)} collective-permute-done((f32[8,128]{1,0:T(8,128)S(1)}, f32[8,128]{1,0:T(8,128)S(1)}, u32[]{:S(2)}, u32[]{:S(2)}) %collective-permute-start.6) | collective-permute-done | bytes 4128 | tf_op jit(solution)/shard_map/ppermute | solution.py:576
  57.8 1.0 %shard_map.82 = (f32[19,2,16,128]{3,2,1,0:T(8,128)S(1)}, f32[19,2,16,128]{3,2,1,0:T(8,128)S(1)}, f32[28,16,128]{2,1,0:T(8,128)S(1)}, f32[28,16,128]{2,1,0:T(8,128)S(1)}, f32[16,8,128]{2,1,0:T(8,128)S(1)}) custom-call(f32[28,24,128]{2,1,0:T(8,128)S(1)} %collective-permute-done.4.h_l, f32[28,24,128]{2,1,0:T(8,128)S(1)} %collective-permute-done.5.h_r, ...), custom_call_target="tpu_custom_call" | custom-call | tf_op jit(solution)/shard_map/pallas_call | solution.py:548
  58.8 2.9 %collective-permute-start.9 = (f32[28,16,128]{2,1,0:T(8,128)S(1)}, f32[28,16,128]{2,1,0:T(8,128)S(1)}, u32[]{:S(2)}, u32[]{:S(2)}) collective-permute-start(f32[28,16,128]{2,1,0:T(8,128)S(1)} %get-tuple-element.74), channel_id=1, source_target_pairs={{16,0},{32,16},{48,32},{64,48},{80,64},{96,80},{112,96},{128,112},... | collective-permute-start | bytes 688136 | tf_op jit(solution)/shard_map/ppermute | solution.py:577
  61.7 10.9 %all_to_all.21.gathered = f32[16,8,128]{2,1,0:T(8,128)S(1)} all-to-all(f32[16,8,128]{2,1,0:T(8,128)S(1)} %get-tuple-element.75), channel_id=1, replica_groups=mesh['gx'=64,'gy_0'=4,'gy_1'=4] {'gy_0','gy_1'}, dimensions={0} | all-to-all | bytes 131072 | tf_op jit(solution)/shard_map/all_to_all | solution.py:581
  74.0 2.9 %collective-permute-done.10.rad_l = f32[8,128]{1,0:T(8,128)S(1)} collective-permute-done((f32[8,128]{1,0:T(8,128)S(1)}, f32[8,128]{1,0:T(8,128)S(1)}, u32[]{:S(2)}, u32[]{:S(2)}) %collective-permute-start.10) | collective-permute-done | bytes 4128 | tf_op jit(solution)/shard_map/ppermute | solution.py:576
  76.9 1.3 %shard_map.85 = (f32[19,2,16,128]{3,2,1,0:T(8,128)S(1)}, f32[19,2,16,128]{3,2,1,0:T(8,128)S(1)}, f32[9,16,128]{2,1,0:T(8,128)S(1)}, f32[9,16,128]{2,1,0:T(8,128)S(1)}, f32[16,8,128]{2,1,0:T(8,128)}) custom-call(f32[28,16,128]{2,1,0:T(8,128)S(1)} %collective-permute-done.8.h_l, f32[28,16,128]{2,1,0:T(8,128)S(1)} %collective-permute-done.9.h_r, ...), custom_call_target="tpu_custom_call" | custom-call | tf_op jit(solution)/shard_map/pallas_call | solution.py:548
  78.2 4.8 %all-to-all-start.3 = ((f32[16,8,128]{2,1,0:T(8,128)}), f32[16,8,128]{2,1,0:T(8,128)S(1)}, u32[]{:S(2)}, u32[]{:S(2)}) async-start(f32[16,8,128]{2,1,0:T(8,128)} %get-tuple-element.84), calls=%async_computation.3 | async-start | bytes 131072 | tf_op jit(solution)/shard_map/all_to_all | solution.py:581
  83.1 2.9 %collective-permute-start.13 = (f32[9,16,128]{2,1,0:T(8,128)S(1)}, f32[9,16,128]{2,1,0:T(8,128)S(1)}, u32[]{:S(2)}, u32[]{:S(2)}) collective-permute-start(f32[9,16,128]{2,1,0:T(8,128)S(1)} %get-tuple-element.83), channel_id=1, source_target_pairs={{16,0},{32,16},{48,32},{64,48},{80,64},{96,80},{112,96},{128,112},... | collective-permute-start | bytes 221192 | tf_op jit(solution)/shard_map/ppermute | solution.py:577
  86.0 3.3 %all-to-all-done.3.gathered = f32[16,8,128]{2,1,0:T(8,128)S(1)} async-done(((f32[16,8,128]{2,1,0:T(8,128)}), f32[16,8,128]{2,1,0:T(8,128)S(1)}, u32[]{:S(2)}, u32[]{:S(2)}) %all-to-all-start.3) | async-done | bytes 65568 | tf_op jit(solution)/shard_map/all_to_all | solution.py:581
  89.9 0.6 dynamic-slice_bitcast_fusion
  90.7 2.9 %collective-permute-done.14.rad_l = f32[8,128]{1,0:T(8,128)S(1)} collective-permute-done((f32[8,128]{1,0:T(8,128)S(1)}, f32[8,128]{1,0:T(8,128)S(1)}, u32[]{:S(2)}, u32[]{:S(2)}) %collective-permute-start.14) | collective-permute-done | bytes 4128 | tf_op jit(solution)/shard_map/ppermute | solution.py:576
  93.7 0.8 shard_map.88
  (30 shorter events, 2.9 us)
Async XLA Ops:
  2.1 25.4 %collective-permute-start.1 = (f32[5,4,8,128]{3,2,1,0:T(8,128)S(1)}, f32[5,4,8,128]{3,2,1,0:T(8,128)S(1)}, u32[]{:S(2)}, u32[]{:S(2)}) collective-permute-start(f32[5,4,8,128]{3,2,1,0:T(8,128)S(1)} %get-tuple-element.46.own), channel_id=1, source_target_pairs={{1,2},{3,4},{5,6},{7,8},{9,10},{11,12},{13,14},{2,1},{4,3},{6,5},{... | collective-permute-start | bytes 245768 | tf_op jit(solution)/shard_map/ppermute | solution.py:598
  7.0 20.5 %collective-permute-start = (f32[5,4,8,128]{3,2,1,0:T(8,128)S(1)}, f32[5,4,8,128]{3,2,1,0:T(8,128)S(1)}, u32[]{:S(2)}, u32[]{:S(2)}) collective-permute-start(f32[5,4,8,128]{3,2,1,0:T(8,128)S(1)} %get-tuple-element.46.own), channel_id=1, source_target_pairs={{0,1},{2,3},{4,5},{6,7},{8,9},{10,11},{12,13},{14,15},{1,0},{3,2},... | collective-permute-start | bytes 245768 | tf_op jit(solution)/shard_map/ppermute | solution.py:598
  9.0 18.4 %all-to-all-start = ((f32[16,8,128]{2,1,0:T(8,128)}), f32[16,8,128]{2,1,0:T(8,128)S(1)}, u32[]{:S(2)}, u32[]{:S(2)}) async-start(f32[16,8,128]{2,1,0:T(8,128)} %get-tuple-element.47), calls=%async_computation | async-start | bytes 131072 | tf_op jit(solution)/shard_map/all_to_all | solution.py:581
  27.5 10.8 %collective-permute-start.2 = (f32[176,128]{1,0:T(8,128)S(1)}, f32[176,128]{1,0:T(8,128)S(1)}, u32[]{:S(2)}, u32[]{:S(2)}) collective-permute-start(f32[176,128]{1,0:T(8,128)S(1)} %get-tuple-element.48), channel_id=1, source_target_pairs={{0,16},{16,32},{32,48},{48,64},{64,80},{80,96},{96,112},{112,128},... | collective-permute-start | bytes 270344 | tf_op jit(solution)/shard_map/ppermute | solution.py:576
  27.5 10.7 %collective-permute-start.3 = (f32[176,128]{1,0:T(8,128)S(1)}, f32[176,128]{1,0:T(8,128)S(1)}, u32[]{:S(2)}, u32[]{:S(2)}) collective-permute-start(f32[176,128]{1,0:T(8,128)S(1)} %get-tuple-element.51), channel_id=1, source_target_pairs={{16,0},{32,16},{48,32},{64,48},{80,64},{96,80},{112,96},{128,112},... | collective-permute-start | bytes 270344 | tf_op jit(solution)/shard_map/ppermute | solution.py:577
  39.3 18.5 %collective-permute-start.4 = (f32[28,24,128]{2,1,0:T(8,128)S(1)}, f32[28,24,128]{2,1,0:T(8,128)S(1)}, u32[]{:S(2)}, u32[]{:S(2)}) collective-permute-start(f32[28,24,128]{2,1,0:T(8,128)S(1)} %get-tuple-element.61), channel_id=1, source_target_pairs={{0,16},{16,32},{32,48},{48,64},{64,80},{80,96},{96,112},{112,128},... | collective-permute-start | bytes 1032200 | tf_op jit(solution)/shard_map/ppermute | solution.py:576
  39.4 18.5 %collective-permute-start.5 = (f32[28,24,128]{2,1,0:T(8,128)S(1)}, f32[28,24,128]{2,1,0:T(8,128)S(1)}, u32[]{:S(2)}, u32[]{:S(2)}) collective-permute-start(f32[28,24,128]{2,1,0:T(8,128)S(1)} %get-tuple-element.62), channel_id=1, source_target_pairs={{16,0},{32,16},{48,32},{64,48},{80,64},{96,80},{112,96},{128,112},... | collective-permute-start | bytes 1032200 | tf_op jit(solution)/shard_map/ppermute | solution.py:577
  53.5 1.3 %collective-permute-start.7 = (f32[8,128]{1,0:T(8,128)S(1)}, f32[8,128]{1,0:T(8,128)S(1)}, u32[]{:S(2)}, u32[]{:S(2)}) collective-permute-start(f32[8,128]{1,0:T(8,128)S(1)} %get-tuple-element.67.rad), channel_id=1, source_target_pairs={{16,0},{32,16},{48,32},{64,48},{80,64},{96,80},{112,96},{128,112},... | collective-permute-start | bytes 12296 | tf_op jit(solution)/shard_map/ppermute | solution.py:577
  53.6 4.3 %collective-permute-start.6 = (f32[8,128]{1,0:T(8,128)S(1)}, f32[8,128]{1,0:T(8,128)S(1)}, u32[]{:S(2)}, u32[]{:S(2)}) collective-permute-start(f32[8,128]{1,0:T(8,128)S(1)} %get-tuple-element.67.rad), channel_id=1, source_target_pairs={{0,16},{16,32},{32,48},{48,64},{64,80},{80,96},{96,112},{112,128},... | collective-permute-start | bytes 12296 | tf_op jit(solution)/shard_map/ppermute | solution.py:576
  58.8 18.1 %collective-permute-start.8 = (f32[28,16,128]{2,1,0:T(8,128)S(1)}, f32[28,16,128]{2,1,0:T(8,128)S(1)}, u32[]{:S(2)}, u32[]{:S(2)}) collective-permute-start(f32[28,16,128]{2,1,0:T(8,128)S(1)} %get-tuple-element.73), channel_id=1, source_target_pairs={{0,16},{16,32},{32,48},{48,64},{64,80},{80,96},{96,112},{112,128},... | collective-permute-start | bytes 688136 | tf_op jit(solution)/shard_map/ppermute | solution.py:576
  58.8 18.1 %collective-permute-start.9 = (f32[28,16,128]{2,1,0:T(8,128)S(1)}, f32[28,16,128]{2,1,0:T(8,128)S(1)}, u32[]{:S(2)}, u32[]{:S(2)}) collective-permute-start(f32[28,16,128]{2,1,0:T(8,128)S(1)} %get-tuple-element.74), channel_id=1, source_target_pairs={{16,0},{32,16},{48,32},{64,48},{80,64},{96,80},{112,96},{128,112},... | collective-permute-start | bytes 688136 | tf_op jit(solution)/shard_map/ppermute | solution.py:577
  72.6 1.3 %collective-permute-start.11 = (f32[8,128]{1,0:T(8,128)S(1)}, f32[8,128]{1,0:T(8,128)S(1)}, u32[]{:S(2)}, u32[]{:S(2)}) collective-permute-start(f32[8,128]{1,0:T(8,128)S(1)} %shard_map.83.rad), channel_id=1, source_target_pairs={{16,0},{32,16},{48,32},{64,48},{80,64},{96,80},{112,96},{128,112},... | collective-permute-start | bytes 12296 | tf_op jit(solution)/shard_map/ppermute | solution.py:577
  72.7 4.3 %collective-permute-start.10 = (f32[8,128]{1,0:T(8,128)S(1)}, f32[8,128]{1,0:T(8,128)S(1)}, u32[]{:S(2)}, u32[]{:S(2)}) collective-permute-start(f32[8,128]{1,0:T(8,128)S(1)} %shard_map.83.rad), channel_id=1, source_target_pairs={{0,16},{16,32},{32,48},{48,64},{64,80},{80,96},{96,112},{112,128},... | collective-permute-start | bytes 12296 | tf_op jit(solution)/shard_map/ppermute | solution.py:576
  78.2 11.1 %all-to-all-start.3 = ((f32[16,8,128]{2,1,0:T(8,128)}), f32[16,8,128]{2,1,0:T(8,128)S(1)}, u32[]{:S(2)}, u32[]{:S(2)}) async-start(f32[16,8,128]{2,1,0:T(8,128)} %get-tuple-element.84), calls=%async_computation.3 | async-start | bytes 131072 | tf_op jit(solution)/shard_map/all_to_all | solution.py:581
  83.1 10.6 %collective-permute-start.12 = (f32[9,16,128]{2,1,0:T(8,128)S(1)}, f32[9,16,128]{2,1,0:T(8,128)S(1)}, u32[]{:S(2)}, u32[]{:S(2)}) collective-permute-start(f32[9,16,128]{2,1,0:T(8,128)S(1)} %get-tuple-element.82), channel_id=1, source_target_pairs={{0,16},{16,32},{32,48},{48,64},{64,80},{80,96},{96,112},{112,128},... | collective-permute-start | bytes 221192 | tf_op jit(solution)/shard_map/ppermute | solution.py:576
  83.1 10.6 %collective-permute-start.13 = (f32[9,16,128]{2,1,0:T(8,128)S(1)}, f32[9,16,128]{2,1,0:T(8,128)S(1)}, u32[]{:S(2)}, u32[]{:S(2)}) collective-permute-start(f32[9,16,128]{2,1,0:T(8,128)S(1)} %get-tuple-element.83), channel_id=1, source_target_pairs={{16,0},{32,16},{48,32},{64,48},{80,64},{96,80},{112,96},{128,112},... | collective-permute-start | bytes 221192 | tf_op jit(solution)/shard_map/ppermute | solution.py:577
  89.4 1.3 %collective-permute-start.15 = (f32[8,128]{1,0:T(8,128)S(1)}, f32[8,128]{1,0:T(8,128)S(1)}, u32[]{:S(2)}, u32[]{:S(2)}) collective-permute-start(f32[8,128]{1,0:T(8,128)S(1)} %shard_map.86.rad), channel_id=1, source_target_pairs={{16,0},{32,16},{48,32},{64,48},{80,64},{96,80},{112,96},{128,112},... | collective-permute-start | bytes 12296 | tf_op jit(solution)/shard_map/ppermute | solution.py:577
  89.4 4.3 %collective-permute-start.14 = (f32[8,128]{1,0:T(8,128)S(1)}, f32[8,128]{1,0:T(8,128)S(1)}, u32[]{:S(2)}, u32[]{:S(2)}) collective-permute-start(f32[8,128]{1,0:T(8,128)S(1)} %shard_map.86.rad), channel_id=1, source_target_pairs={{0,16},{16,32},{32,48},{48,64},{64,80},{80,96},{96,112},{112,128},... | collective-permute-start | bytes 12296 | tf_op jit(solution)/shard_map/ppermute | solution.py:576

commit v5 on v4

--- a/solution.py
+++ b/solution.py
@@ -42,6 +42,8 @@
 
 TILE = 8
 LANES = 128
+HALO = 6
+Y_ROWS = 16 * HALO + TILE
 PAD = 8
 WIDE = 24
 MID = 16
@@ -238,7 +240,7 @@
 
 
 def gather_kernel(
-    place_ref, density, velocity, mask, unit, radius, out, send, density_v, velocity_v, mask_v, unit_v, radius_v, send_v, sems
+    place_ref, density, velocity, mask, unit, radius, out, first, second, send, density_v, velocity_v, mask_v, unit_v, radius_v, send_v, sems
 ):
     pairs = ((radius, radius_v), (density, density_v), (velocity, velocity_v), (mask, mask_v), (unit, unit_v))
     loads = [pltpu.make_async_copy(a, b, sems.at[n]) for n, (a, b) in enumerate(pairs)]
@@ -257,6 +259,8 @@
     store.start()
     for load in loads[1:]:
         load.wait()
+    odd = (place_ref[0] & 1) == 1
+    unit_tile = jnp.zeros((TILE, LANES), F32)
     for x in range(4):
         out[0, x] = jnp.where(mask_v[x] != 0, density_v[x], 0.0)
         for k in range(3):
@@ -264,22 +268,50 @@
         units = jnp.broadcast_to(unit_v[x : x + 1, :].astype(F32), narrow)
         column = jnp.sum(jnp.where(diagonal, units, 0.0), axis=1, keepdims=True)
         out[4, x] = jnp.broadcast_to(column, (TILE, LANES))
+        unit_tile = jnp.where(lane == x, column, unit_tile)
+    for k in range(4):
+        for x in range(4):
+            to_before = out[k, x, pl.ds(0, HALO), :]
+            to_after = out[k, x, pl.ds(TILE - HALO, HALO), :]
+            rows = pl.ds((4 * k + x) * HALO, HALO)
+            first[rows, :] = jnp.where(odd, to_before, to_after)
+            second[rows, :] = jnp.where(odd, to_after, to_before)
+    for ref in (first, second):
+        ref[pl.ds(16 * HALO, TILE), :] = unit_tile
     store.wait()
 
 
 def rows_kernel(odd_ref, first, own, second, base_in, left_out, right_out, left_send, right_send):
     base = sum_of(base_in)
     odd = odd_ref[0] == 1
+    zero = jnp.zeros((TILE, LANES), F32)
+    lane = lax.broadcasted_iota(jnp.int32, (TILE, LANES), 1)
+
+    def unit_column(ref, column):
+        picked = jnp.where(lane == column, ref[pl.ds(16 * HALO, TILE), :], 0.0)
+        return jnp.broadcast_to(jnp.sum(picked, axis=1, keepdims=True), (TILE, LANES))
+
     for half, out, send, planes in (
         (0, left_out, left_send, NEAR_FAR),
         (1, right_out, right_send, LEFT_PLANES),
     ):
         for (k, x), plane in OWN_PLANES.items():
-            here, a, b = (ref[k, 2 * half + x] for ref in (own, first, second))
-            for part, value in enumerate((jnp.where(odd, a, b), here, jnp.where(odd, b, a))):
-                out[pl.ds(plane * WIDE + part * TILE, TILE), :] = value
-                if (k, x) in planes:
-                    send[pl.ds(planes[k, x] * WIDE + part * TILE, TILE), :] = value
+            column = 2 * half + x
+            targets = [(out, plane)] + ([(send, planes[k, x])] if (k, x) in planes else [])
+            if k < 4:
+                rows = pl.ds((4 * k + column) * HALO, HALO)
+                a, b = first[rows, :], second[rows, :]
+            else:
+                a, b = (unit_column(ref, column) for ref in (first, second))
+            before, after = jnp.where(odd, a, b), jnp.where(odd, b, a)
+            for ref, at in targets:
+                at = at * WIDE
+                if k < 4:
+                    ref[pl.ds(at, TILE), :] = zero
+                    ref[pl.ds(at + 2 * TILE, TILE), :] = zero
+                ref[pl.ds(at + TILE - before.shape[0], before.shape[0]), :] = before
+                ref[pl.ds(at + TILE, TILE), :] = own[k, column]
+                ref[pl.ds(at + 2 * TILE, after.shape[0]), :] = after
         out[pl.ds(len(OWN_PLANES) * WIDE, TILE), :] = base
         send[pl.ds(len(planes) * WIDE, TILE), :] = base
 
@@ -582,26 +614,28 @@
 
     arrays = (density, velocity, fluid_mask, unit_of_column, radius_base.reshape(1, -1))
     anywhere = pl.BlockSpec(memory_space=pl.ANY)
-    own, base_send = pl.pallas_call(
+    own, to_first, to_second, base_send = pl.pallas_call(
         gather_kernel,
-        out_shape=[pltpu.VMEM((5, 4, TILE, LANES), F32), jax.ShapeDtypeStruct(*sends)],
+        out_shape=[pltpu.VMEM((5, 4, TILE, LANES), F32)]
+        + [pltpu.VMEM((Y_ROWS, LANES), F32)] * 2
+        + [jax.ShapeDtypeStruct(*sends)],
         in_specs=[pl.BlockSpec(memory_space=pltpu.SMEM)] + [anywhere] * 5,
-        out_specs=[pl.BlockSpec(memory_space=pltpu.VMEM), anywhere],
+        out_specs=[pl.BlockSpec(memory_space=pltpu.VMEM)] * 3 + [anywhere],
         scratch_shapes=[pltpu.VMEM(a.shape, a.dtype) for a in arrays]
         + [pltpu.VMEM(*sends), pltpu.SemaphoreType.DMA((6,))],
         compiler_params=pltpu.CompilerParams(vmem_limit_bytes=1 << 20),
     )(place.reshape(1), *(pltpu.with_memory_space_constraint(a, pltpu.HBM) for a in arrays))
     base_in = exchange(base_send)
 
-    def swap(start):
+    def swap(start, rows):
         pairs = [(i, i + 1) for i in range(start, count - 1, 2)]
-        return lax.ppermute(own, GY, pairs + [(b, a) for a, b in pairs])
-
-    swaps = swap(0), swap(1)
+        return lax.ppermute(rows, GY, pairs + [(b, a) for a, b in pairs])
+
+    swaps = swap(0, to_first), swap(1, to_second)
     pair = ((len(OWN_PLANES) * WIDE + TILE, LANES), F32)
     near_far = ((len(NEAR_FAR) * WIDE + TILE, LANES), F32)
     g_l, g_r, go_l, go_r = call(rows_kernel, [pair, pair, near_far, near_far], scalars=1)(
-        (place % 2).reshape(1), swaps[0], own, swaps[1], base_in
+        (place & 1).reshape(1), swaps[0], own, swaps[1], base_in
     )
     g_hl, g_hr = ring(go_l, go_r)
     fields = (g_hl, g_l, g_r, g_hr)

time: 94.9 us -> 95.7 us (level)
  waiting for transfers between devices: 20.8 us -> 18.8 us
  starting transfers between devices: 42.9 us -> 44.4 us
  blocking collectives: 22 us -> 23.3 us
    all_to_all x2, waiting for transfers between devices: 9.66 us -> 3.34 us  [exchange(): return lax.all_to_all(blocks, GY, split_axis=0, concat_axis=0, tiled=True)]
    all_to_all x2, starting transfers between devices: 16.9 us -> 21.3 us  [exchange(): return lax.all_to_all(blocks, GY, split_axis=0, concat_axis=0, tiled=True)]
    ppermute x2, waiting for transfers between devices: 0.01 us -> 4.15 us  [swap(): return lax.ppermute(rows, GY, pairs + [(b, a) for a, b in pairs])]
    ppermute x7, starting transfers between devices: 17.5 us -> 14.2 us  [ring(): after = lax.ppermute(low, 'gx', down)]
    all_to_all x2, blocking collectives: 22 us -> 23.3 us  [exchange(): return lax.all_to_all(blocks, GY, split_axis=0, concat_axis=0, tiled=True)]
where the time goes in v5:
time: 95.7 us; the launch traced here: 95.3 us
  starting transfers between devices  44.4 us (46%)
  blocking collectives  23.3 us (24%)
  waiting for transfers between devices  18.8 us (20%)
  Pallas kernels  7.31 us (8%)
    all_to_all x2, blocking collectives, exchange(): return lax.all_to_all(blocks, GY, split_axis=0, concat_axis=0, tiled=True)  23.3 us
    all_to_all x2, starting transfers between devices, exchange(): return lax.all_to_all(blocks, GY, split_axis=0, concat_axis=0, tiled=True)  21.3 us
    ppermute x7, starting transfers between devices, ring(): after = lax.ppermute(low, 'gx', down)  14.2 us
    ppermute x7, waiting for transfers between devices, ring(): before = lax.ppermute(high, 'gx', up)  10.7 us
    ppermute x2, starting transfers between devices, swap(): return lax.ppermute(rows, GY, pairs + [(b, a) for a, b in pairs])  7.32 us
    pallas_call x12, Pallas kernels, run(): pl.pallas_call(kernel, out_shape=[(jax.ShapeDtypeStruct if n == hbm_out e...  5.9 us
    ppermute x2, waiting for transfers between devices, swap(): return lax.ppermute(rows, GY, pairs + [(b, a) for a, b in pairs])  4.15 us
    all_to_all x2, waiting for transfers between devices, exchange(): return lax.all_to_all(blocks, GY, split_axis=0, concat_axis=0, tiled=True)  3.34 us
  transfers between devices with their start and end apart: 18, of which 8 were waited for; matrix products, arithmetic and copies ran while one was open for 1% of the time, Pallas kernels for 2%

profile of v5, /device:TPU:2, one launch (start us, length us, event | category | flops | bytes accessed | tf_op | source)
XLA Modules:
  0.0 95.3 jit_solution(7070541804233603299)
XLA Ops:
  0.6 1.4 %shard_map.76 = (f32[5,4,8,128]{3,2,1,0:T(8,128)S(1)}, f32[104,128]{1,0:T(8,128)S(1)}, f32[104,128]{1,0:T(8,128)S(1)}, f32[16,8,128]{2,1,0:T(8,128)}) custom-call(s32[1]{0:T(128)} %bitcast.3.place_ref, f32[4,8,128]{2,1,0:T(8,128)} %density.1, f32[3,4,8,128]{3,2,1,0:T(8,128)} %velocity.1, s32[4,8,128]{2,1,0:T(8,128)} %mask.1, s32[4,8]{1,0:T(4,128)} %unit.1, ...), custom_call_target="tpu_custom_call" | custom-call | tf_op jit(solution)/shard_map/pallas_call | solution.py:617
  2.1 16.5 %all-to-all-start = ((f32[16,8,128]{2,1,0:T(8,128)}), f32[16,8,128]{2,1,0:T(8,128)S(1)}, u32[]{:S(2)}, u32[]{:S(2)}) async-start(f32[16,8,128]{2,1,0:T(8,128)} %get-tuple-element.51), calls=%async_computation | async-start | bytes 131072 | tf_op jit(solution)/shard_map/all_to_all | solution.py:613
  18.5 3.4 %collective-permute-start = (f32[104,128]{1,0:T(8,128)S(1)}, f32[104,128]{1,0:T(8,128)S(1)}, u32[]{:S(2)}, u32[]{:S(2)}) collective-permute-start(f32[104,128]{1,0:T(8,128)S(1)} %get-tuple-element.48), channel_id=1, source_target_pairs={{0,1},{2,3},{4,5},{6,7},{8,9},{10,11},{12,13},{14,15},{1,0},{3,2},... | collective-permute-start | bytes 159752 | tf_op jit(solution)/shard_map/ppermute | solution.py:632
  21.9 4.0 %collective-permute-start.1 = (f32[104,128]{1,0:T(8,128)S(1)}, f32[104,128]{1,0:T(8,128)S(1)}, u32[]{:S(2)}, u32[]{:S(2)}) collective-permute-start(f32[104,128]{1,0:T(8,128)S(1)} %get-tuple-element.50), channel_id=1, source_target_pairs={{1,2},{3,4},{5,6},{7,8},{9,10},{11,12},{13,14},{2,1},{4,3},{6,5},{... | collective-permute-start | bytes 159752 | tf_op jit(solution)/shard_map/ppermute | solution.py:632
  25.9 4.2 %collective-permute-done.1.second = f32[104,128]{1,0:T(8,128)S(1)} collective-permute-done((f32[104,128]{1,0:T(8,128)S(1)}, f32[104,128]{1,0:T(8,128)S(1)}, u32[]{:S(2)}, u32[]{:S(2)}) %collective-permute-start.1) | collective-permute-done | bytes 53280 | tf_op jit(solution)/shard_map/ppermute | solution.py:632
  30.1 5.2 %collective-permute-start.3 = (f32[176,128]{1,0:T(8,128)S(1)}, f32[176,128]{1,0:T(8,128)S(1)}, u32[]{:S(2)}, u32[]{:S(2)}) collective-permute-start(f32[176,128]{1,0:T(8,128)S(1)} %get-tuple-element.55), channel_id=1, source_target_pairs={{16,0},{32,16},{48,32},{64,48},{80,64},{96,80},{112,96},{128,112},... | collective-permute-start | bytes 270344 | tf_op jit(solution)/shard_map/ppermute | solution.py:609
  35.8 1.7 %collective-permute-done.2.halo_l.g_hl = f32[176,128]{1,0:T(8,128)S(1)} collective-permute-done((f32[176,128]{1,0:T(8,128)S(1)}, f32[176,128]{1,0:T(8,128)S(1)}, u32[]{:S(2)}, u32[]{:S(2)}) %collective-permute-start.2) | collective-permute-done | bytes 90144 | tf_op jit(solution)/shard_map/ppermute | solution.py:608
  37.6 1.1 %shard_map.79 = (f32[19,2,24,128]{3,2,1,0:T(8,128)S(1)}, f32[19,2,24,128]{3,2,1,0:T(8,128)S(1)}, f32[28,24,128]{2,1,0:T(8,128)S(1)}, f32[28,24,128]{2,1,0:T(8,12...) custom-call(s32[2]{0:T(128)S(1)} %add_convert_fusion.edge_ref, ...), custom_call_target="tpu_custom_call", output_to_operand_aliasing={{0}: (8, {}), {1}: (9, {}), {2}: (10, {}), {3}: (11, {}), {... | custom-call | tf_op jit(solution)/shard_map/pallas_call | solution.py:580
  38.7 3.0 %collective-permute-start.5 = (f32[28,24,128]{2,1,0:T(8,128)S(1)}, f32[28,24,128]{2,1,0:T(8,128)S(1)}, u32[]{:S(2)}, u32[]{:S(2)}) collective-permute-start(f32[28,24,128]{2,1,0:T(8,128)S(1)} %get-tuple-element.66), channel_id=1, source_target_pairs={{16,0},{32,16},{48,32},{64,48},{80,64},{96,80},{112,96},{128,112},... | collective-permute-start | bytes 1032200 | tf_op jit(solution)/shard_map/ppermute | solution.py:609
  41.7 12.4 %all_to_all.20.gathered = f32[16,8,128]{2,1,0:T(8,128)S(1)} all-to-all(f32[16,8,128]{2,1,0:T(8,128)S(1)} %get-tuple-element.69), channel_id=1, replica_groups=mesh['gx'=64,'gy_0'=4,'gy_1'=4] {'gy_0','gy_1'}, dimensions={0} | all-to-all | bytes 131072 | tf_op jit(solution)/shard_map/all_to_all | solution.py:613
  54.1 0.5 collective-permute-start.6
  54.6 0.6 shard_map.81
  55.4 3.1 %collective-permute-done.6.rad_l = f32[8,128]{1,0:T(8,128)S(1)} collective-permute-done((f32[8,128]{1,0:T(8,128)S(1)}, f32[8,128]{1,0:T(8,128)S(1)}, u32[]{:S(2)}, u32[]{:S(2)}) %collective-permute-start.6) | collective-permute-done | bytes 4128 | tf_op jit(solution)/shard_map/ppermute | solution.py:608
  58.5 1.0 shard_map.82
  59.5 2.9 %collective-permute-start.9 = (f32[28,16,128]{2,1,0:T(8,128)S(1)}, f32[28,16,128]{2,1,0:T(8,128)S(1)}, u32[]{:S(2)}, u32[]{:S(2)}) collective-permute-start(f32[28,16,128]{2,1,0:T(8,128)S(1)} %get-tuple-element.78), channel_id=1, source_target_pairs={{16,0},{32,16},{48,32},{64,48},{80,64},{96,80},{112,96},{128,112},... | collective-permute-start | bytes 688136 | tf_op jit(solution)/shard_map/ppermute | solution.py:609
  62.5 11.0 %all_to_all.21.gathered = f32[16,8,128]{2,1,0:T(8,128)S(1)} all-to-all(f32[16,8,128]{2,1,0:T(8,128)S(1)} %get-tuple-element.79), channel_id=1, replica_groups=mesh['gx'=64,'gy_0'=4,'gy_1'=4] {'gy_0','gy_1'}, dimensions={0} | all-to-all | bytes 131072 | tf_op jit(solution)/shard_map/all_to_all | solution.py:613
  74.8 2.9 %collective-permute-done.10.rad_l = f32[8,128]{1,0:T(8,128)S(1)} collective-permute-done((f32[8,128]{1,0:T(8,128)S(1)}, f32[8,128]{1,0:T(8,128)S(1)}, u32[]{:S(2)}, u32[]{:S(2)}) %collective-permute-start.10) | collective-permute-done | bytes 4128 | tf_op jit(solution)/shard_map/ppermute | solution.py:608
  77.7 1.3 %shard_map.85 = (f32[19,2,16,128]{3,2,1,0:T(8,128)S(1)}, f32[19,2,16,128]{3,2,1,0:T(8,128)S(1)}, f32[9,16,128]{2,1,0:T(8,128)S(1)}, f32[9,16,128]{2,1,0:T(8,128)S(1)}, f32[16,8,128]{2,1,0:T(8,128)}) custom-call(f32[28,16,128]{2,1,0:T(8,128)S(1)} %collective-permute-done.8.h_l, f32[28,16,128]{2,1,0:T(8,128)S(1)} %collective-permute-done.9.h_r, ...), custom_call_target="tpu_custom_call" | custom-call | tf_op jit(solution)/shard_map/pallas_call | solution.py:580
  79.0 4.8 %all-to-all-start.3 = ((f32[16,8,128]{2,1,0:T(8,128)}), f32[16,8,128]{2,1,0:T(8,128)S(1)}, u32[]{:S(2)}, u32[]{:S(2)}) async-start(f32[16,8,128]{2,1,0:T(8,128)} %get-tuple-element.88), calls=%async_computation.3 | async-start | bytes 131072 | tf_op jit(solution)/shard_map/all_to_all | solution.py:613
  83.9 2.9 %collective-permute-start.13 = (f32[9,16,128]{2,1,0:T(8,128)S(1)}, f32[9,16,128]{2,1,0:T(8,128)S(1)}, u32[]{:S(2)}, u32[]{:S(2)}) collective-permute-start(f32[9,16,128]{2,1,0:T(8,128)S(1)} %get-tuple-element.87), channel_id=1, source_target_pairs={{16,0},{32,16},{48,32},{64,48},{80,64},{96,80},{112,96},{128,112},... | collective-permute-start | bytes 221192 | tf_op jit(solution)/shard_map/ppermute | solution.py:609
  86.8 3.3 %all-to-all-done.3.gathered = f32[16,8,128]{2,1,0:T(8,128)S(1)} async-done(((f32[16,8,128]{2,1,0:T(8,128)}), f32[16,8,128]{2,1,0:T(8,128)S(1)}, u32[]{:S(2)}, u32[]{:S(2)}) %all-to-all-start.3) | async-done | bytes 65568 | tf_op jit(solution)/shard_map/all_to_all | solution.py:613
  90.7 0.6 dynamic-slice_bitcast_fusion
  91.5 2.9 %collective-permute-done.14.rad_l = f32[8,128]{1,0:T(8,128)S(1)} collective-permute-done((f32[8,128]{1,0:T(8,128)S(1)}, f32[8,128]{1,0:T(8,128)S(1)}, u32[]{:S(2)}, u32[]{:S(2)}) %collective-permute-start.14) | collective-permute-done | bytes 4128 | tf_op jit(solution)/shard_map/ppermute | solution.py:608
  94.5 0.8 shard_map.88
  (30 shorter events, 3.0 us)
Async XLA Ops:
  2.1 28.0 %all-to-all-start = ((f32[16,8,128]{2,1,0:T(8,128)}), f32[16,8,128]{2,1,0:T(8,128)S(1)}, u32[]{:S(2)}, u32[]{:S(2)}) async-start(f32[16,8,128]{2,1,0:T(8,128)} %get-tuple-element.51), calls=%async_computation | async-start | bytes 131072 | tf_op jit(solution)/shard_map/all_to_all | solution.py:613
  18.5 7.4 %collective-permute-start = (f32[104,128]{1,0:T(8,128)S(1)}, f32[104,128]{1,0:T(8,128)S(1)}, u32[]{:S(2)}, u32[]{:S(2)}) collective-permute-start(f32[104,128]{1,0:T(8,128)S(1)} %get-tuple-element.48), channel_id=1, source_target_pairs={{0,1},{2,3},{4,5},{6,7},{8,9},{10,11},{12,13},{14,15},{1,0},{3,2},... | collective-permute-start | bytes 159752 | tf_op jit(solution)/shard_map/ppermute | solution.py:632
  21.9 8.1 %collective-permute-start.1 = (f32[104,128]{1,0:T(8,128)S(1)}, f32[104,128]{1,0:T(8,128)S(1)}, u32[]{:S(2)}, u32[]{:S(2)}) collective-permute-start(f32[104,128]{1,0:T(8,128)S(1)} %get-tuple-element.50), channel_id=1, source_target_pairs={{1,2},{3,4},{5,6},{7,8},{9,10},{11,12},{13,14},{2,1},{4,3},{6,5},{... | collective-permute-start | bytes 159752 | tf_op jit(solution)/shard_map/ppermute | solution.py:632
  30.1 7.5 %collective-permute-start.2 = (f32[176,128]{1,0:T(8,128)S(1)}, f32[176,128]{1,0:T(8,128)S(1)}, u32[]{:S(2)}, u32[]{:S(2)}) collective-permute-start(f32[176,128]{1,0:T(8,128)S(1)} %get-tuple-element.52), channel_id=1, source_target_pairs={{0,16},{16,32},{32,48},{48,64},{64,80},{80,96},{96,112},{112,128},... | collective-permute-start | bytes 270344 | tf_op jit(solution)/shard_map/ppermute | solution.py:608
  30.1 7.4 %collective-permute-start.3 = (f32[176,128]{1,0:T(8,128)S(1)}, f32[176,128]{1,0:T(8,128)S(1)}, u32[]{:S(2)}, u32[]{:S(2)}) collective-permute-start(f32[176,128]{1,0:T(8,128)S(1)} %get-tuple-element.55), channel_id=1, source_target_pairs={{16,0},{32,16},{48,32},{64,48},{80,64},{96,80},{112,96},{128,112},... | collective-permute-start | bytes 270344 | tf_op jit(solution)/shard_map/ppermute | solution.py:609
  38.6 19.9 %collective-permute-start.4 = (f32[28,24,128]{2,1,0:T(8,128)S(1)}, f32[28,24,128]{2,1,0:T(8,128)S(1)}, u32[]{:S(2)}, u32[]{:S(2)}) collective-permute-start(f32[28,24,128]{2,1,0:T(8,128)S(1)} %get-tuple-element.65), channel_id=1, source_target_pairs={{0,16},{16,32},{32,48},{48,64},{64,80},{80,96},{96,112},{112,128},... | collective-permute-start | bytes 1032200 | tf_op jit(solution)/shard_map/ppermute | solution.py:608
  38.7 19.9 %collective-permute-start.5 = (f32[28,24,128]{2,1,0:T(8,128)S(1)}, f32[28,24,128]{2,1,0:T(8,128)S(1)}, u32[]{:S(2)}, u32[]{:S(2)}) collective-permute-start(f32[28,24,128]{2,1,0:T(8,128)S(1)} %get-tuple-element.66), channel_id=1, source_target_pairs={{16,0},{32,16},{48,32},{64,48},{80,64},{96,80},{112,96},{128,112},... | collective-permute-start | bytes 1032200 | tf_op jit(solution)/shard_map/ppermute | solution.py:609
  54.0 1.3 %collective-permute-start.7 = (f32[8,128]{1,0:T(8,128)S(1)}, f32[8,128]{1,0:T(8,128)S(1)}, u32[]{:S(2)}, u32[]{:S(2)}) collective-permute-start(f32[8,128]{1,0:T(8,128)S(1)} %get-tuple-element.71.rad), channel_id=1, source_target_pairs={{16,0},{32,16},{48,32},{64,48},{80,64},{96,80},{112,96},{128,112},... | collective-permute-start | bytes 12296 | tf_op jit(solution)/shard_map/ppermute | solution.py:609
  54.1 4.5 %collective-permute-start.6 = (f32[8,128]{1,0:T(8,128)S(1)}, f32[8,128]{1,0:T(8,128)S(1)}, u32[]{:S(2)}, u32[]{:S(2)}) collective-permute-start(f32[8,128]{1,0:T(8,128)S(1)} %get-tuple-element.71.rad), channel_id=1, source_target_pairs={{0,16},{16,32},{32,48},{48,64},{64,80},{80,96},{96,112},{112,128},... | collective-permute-start | bytes 12296 | tf_op jit(solution)/shard_map/ppermute | solution.py:608
  59.5 18.2 %collective-permute-start.8 = (f32[28,16,128]{2,1,0:T(8,128)S(1)}, f32[28,16,128]{2,1,0:T(8,128)S(1)}, u32[]{:S(2)}, u32[]{:S(2)}) collective-permute-start(f32[28,16,128]{2,1,0:T(8,128)S(1)} %get-tuple-element.77), channel_id=1, source_target_pairs={{0,16},{16,32},{32,48},{48,64},{64,80},{80,96},{96,112},{112,128},... | collective-permute-start | bytes 688136 | tf_op jit(solution)/shard_map/ppermute | solution.py:608
  59.5 18.2 %collective-permute-start.9 = (f32[28,16,128]{2,1,0:T(8,128)S(1)}, f32[28,16,128]{2,1,0:T(8,128)S(1)}, u32[]{:S(2)}, u32[]{:S(2)}) collective-permute-start(f32[28,16,128]{2,1,0:T(8,128)S(1)} %get-tuple-element.78), channel_id=1, source_target_pairs={{16,0},{32,16},{48,32},{64,48},{80,64},{96,80},{112,96},{128,112},... | collective-permute-start | bytes 688136 | tf_op jit(solution)/shard_map/ppermute | solution.py:609
  73.4 1.3 %collective-permute-start.11 = (f32[8,128]{1,0:T(8,128)S(1)}, f32[8,128]{1,0:T(8,128)S(1)}, u32[]{:S(2)}, u32[]{:S(2)}) collective-permute-start(f32[8,128]{1,0:T(8,128)S(1)} %shard_map.83.rad), channel_id=1, source_target_pairs={{16,0},{32,16},{48,32},{64,48},{80,64},{96,80},{112,96},{128,112},... | collective-permute-start | bytes 12296 | tf_op jit(solution)/shard_map/ppermute | solution.py:609
  73.5 4.3 %collective-permute-start.10 = (f32[8,128]{1,0:T(8,128)S(1)}, f32[8,128]{1,0:T(8,128)S(1)}, u32[]{:S(2)}, u32[]{:S(2)}) collective-permute-start(f32[8,128]{1,0:T(8,128)S(1)} %shard_map.83.rad), channel_id=1, source_target_pairs={{0,16},{16,32},{32,48},{48,64},{64,80},{80,96},{96,112},{112,128},... | collective-permute-start | bytes 12296 | tf_op jit(solution)/shard_map/ppermute | solution.py:608
  79.0 11.1 %all-to-all-start.3 = ((f32[16,8,128]{2,1,0:T(8,128)}), f32[16,8,128]{2,1,0:T(8,128)S(1)}, u32[]{:S(2)}, u32[]{:S(2)}) async-start(f32[16,8,128]{2,1,0:T(8,128)} %get-tuple-element.88), calls=%async_computation.3 | async-start | bytes 131072 | tf_op jit(solution)/shard_map/all_to_all | solution.py:613
  83.9 10.6 %collective-permute-start.12 = (f32[9,16,128]{2,1,0:T(8,128)S(1)}, f32[9,16,128]{2,1,0:T(8,128)S(1)}, u32[]{:S(2)}, u32[]{:S(2)}) collective-permute-start(f32[9,16,128]{2,1,0:T(8,128)S(1)} %get-tuple-element.86), channel_id=1, source_target_pairs={{0,16},{16,32},{32,48},{48,64},{64,80},{80,96},{96,112},{112,128},... | collective-permute-start | bytes 221192 | tf_op jit(solution)/shard_map/ppermute | solution.py:608
  83.9 10.6 %collective-permute-start.13 = (f32[9,16,128]{2,1,0:T(8,128)S(1)}, f32[9,16,128]{2,1,0:T(8,128)S(1)}, u32[]{:S(2)}, u32[]{:S(2)}) collective-permute-start(f32[9,16,128]{2,1,0:T(8,128)S(1)} %get-tuple-element.87), channel_id=1, source_target_pairs={{16,0},{32,16},{48,32},{64,48},{80,64},{96,80},{112,96},{128,112},... | collective-permute-start | bytes 221192 | tf_op jit(solution)/shard_map/ppermute | solution.py:609
  90.2 1.3 %collective-permute-start.15 = (f32[8,128]{1,0:T(8,128)S(1)}, f32[8,128]{1,0:T(8,128)S(1)}, u32[]{:S(2)}, u32[]{:S(2)}) collective-permute-start(f32[8,128]{1,0:T(8,128)S(1)} %shard_map.86.rad), channel_id=1, source_target_pairs={{16,0},{32,16},{48,32},{64,48},{80,64},{96,80},{112,96},{128,112},... | collective-permute-start | bytes 12296 | tf_op jit(solution)/shard_map/ppermute | solution.py:609
  90.2 4.3 %collective-permute-start.14 = (f32[8,128]{1,0:T(8,128)S(1)}, f32[8,128]{1,0:T(8,128)S(1)}, u32[]{:S(2)}, u32[]{:S(2)}) collective-permute-start(f32[8,128]{1,0:T(8,128)S(1)} %shard_map.86.rad), channel_id=1, source_target_pairs={{0,16},{16,32},{32,48},{48,64},{64,80},{80,96},{96,112},{112,128},... | collective-permute-start | bytes 12296 | tf_op jit(solution)/shard_map/ppermute | solution.py:608

commit v6 on v5

--- a/solution.py
+++ b/solution.py
@@ -631,11 +631,12 @@
         pairs = [(i, i + 1) for i in range(start, count - 1, 2)]
         return lax.ppermute(rows, GY, pairs + [(b, a) for a, b in pairs])
 
-    swaps = swap(0, to_first), swap(1, to_second)
+    by_first = swap(0, to_first)
+    by_second = swap(1, to_second)
     pair = ((len(OWN_PLANES) * WIDE + TILE, LANES), F32)
     near_far = ((len(NEAR_FAR) * WIDE + TILE, LANES), F32)
     g_l, g_r, go_l, go_r = call(rows_kernel, [pair, pair, near_far, near_far], scalars=1)(
-        (place & 1).reshape(1), swaps[0], own, swaps[1], base_in
+        (place & 1).reshape(1), by_first, own, by_second, base_in
     )
     g_hl, g_hr = ring(go_l, go_r)
     fields = (g_hl, g_l, g_r, g_hr)

time: 95.7 us -> 95.7 us (level)
  no operation moved by 1% of the time
where the time goes in v6:
time: 95.7 us; the launch traced here: 95.3 us
  starting transfers between devices  44.4 us (46%)
  blocking collectives  23.3 us (24%)
  waiting for transfers between devices  18.8 us (20%)
  Pallas kernels  7.31 us (8%)
    all_to_all x2, blocking collectives, exchange(): return lax.all_to_all(blocks, GY, split_axis=0, concat_axis=0, tiled=True)  23.3 us
    all_to_all x2, starting transfers between devices, exchange(): return lax.all_to_all(blocks, GY, split_axis=0, concat_axis=0, tiled=True)  21.3 us
    ppermute x7, starting transfers between devices, ring(): after = lax.ppermute(low, 'gx', down)  14.2 us
    ppermute x7, waiting for transfers between devices, ring(): before = lax.ppermute(high, 'gx', up)  10.7 us
    ppermute x2, starting transfers between devices, swap(): return lax.ppermute(rows, GY, pairs + [(b, a) for a, b in pairs])  7.32 us
    pallas_call x12, Pallas kernels, run(): pl.pallas_call(kernel, out_shape=[(jax.ShapeDtypeStruct if n == hbm_out e...  5.9 us
    ppermute x2, waiting for transfers between devices, swap(): return lax.ppermute(rows, GY, pairs + [(b, a) for a, b in pairs])  4.15 us
    all_to_all x2, waiting for transfers between devices, exchange(): return lax.all_to_all(blocks, GY, split_axis=0, concat_axis=0, tiled=True)  3.34 us
  transfers between devices with their start and end apart: 18, of which 8 were waited for; matrix products, arithmetic and copies ran while one was open for 1% of the time, Pallas kernels for 2%

profile of v6, /device:TPU:2, one launch (start us, length us, event | category | flops | bytes accessed | tf_op | source)
XLA Modules:
  0.0 95.3 jit_solution(7070541804233603299)
XLA Ops:
  0.6 1.4 %shard_map.76 = (f32[5,4,8,128]{3,2,1,0:T(8,128)S(1)}, f32[104,128]{1,0:T(8,128)S(1)}, f32[104,128]{1,0:T(8,128)S(1)}, f32[16,8,128]{2,1,0:T(8,128)}) custom-call(s32[1]{0:T(128)} %bitcast.3.place_ref, f32[4,8,128]{2,1,0:T(8,128)} %density.1, f32[3,4,8,128]{3,2,1,0:T(8,128)} %velocity.1, s32[4,8,128]{2,1,0:T(8,128)} %mask.1, s32[4,8]{1,0:T(4,128)} %unit.1, ...), custom_call_target="tpu_custom_call" | custom-call | tf_op jit(solution)/shard_map/pallas_call | solution.py:617
  2.1 16.5 %all-to-all-start = ((f32[16,8,128]{2,1,0:T(8,128)}), f32[16,8,128]{2,1,0:T(8,128)S(1)}, u32[]{:S(2)}, u32[]{:S(2)}) async-start(f32[16,8,128]{2,1,0:T(8,128)} %get-tuple-element.51), calls=%async_computation | async-start | bytes 131072 | tf_op jit(solution)/shard_map/all_to_all | solution.py:613
  18.5 3.4 %collective-permute-start = (f32[104,128]{1,0:T(8,128)S(1)}, f32[104,128]{1,0:T(8,128)S(1)}, u32[]{:S(2)}, u32[]{:S(2)}) collective-permute-start(f32[104,128]{1,0:T(8,128)S(1)} %get-tuple-element.48), channel_id=1, source_target_pairs={{0,1},{2,3},{4,5},{6,7},{8,9},{10,11},{12,13},{14,15},{1,0},{3,2},... | collective-permute-start | bytes 159752 | tf_op jit(solution)/shard_map/ppermute | solution.py:632
  21.9 4.0 %collective-permute-start.1 = (f32[104,128]{1,0:T(8,128)S(1)}, f32[104,128]{1,0:T(8,128)S(1)}, u32[]{:S(2)}, u32[]{:S(2)}) collective-permute-start(f32[104,128]{1,0:T(8,128)S(1)} %get-tuple-element.50), channel_id=1, source_target_pairs={{1,2},{3,4},{5,6},{7,8},{9,10},{11,12},{13,14},{2,1},{4,3},{6,5},{... | collective-permute-start | bytes 159752 | tf_op jit(solution)/shard_map/ppermute | solution.py:632
  25.9 4.2 %collective-permute-done.1.second = f32[104,128]{1,0:T(8,128)S(1)} collective-permute-done((f32[104,128]{1,0:T(8,128)S(1)}, f32[104,128]{1,0:T(8,128)S(1)}, u32[]{:S(2)}, u32[]{:S(2)}) %collective-permute-start.1) | collective-permute-done | bytes 53280 | tf_op jit(solution)/shard_map/ppermute | solution.py:632
  30.1 5.2 %collective-permute-start.3 = (f32[176,128]{1,0:T(8,128)S(1)}, f32[176,128]{1,0:T(8,128)S(1)}, u32[]{:S(2)}, u32[]{:S(2)}) collective-permute-start(f32[176,128]{1,0:T(8,128)S(1)} %get-tuple-element.55), channel_id=1, source_target_pairs={{16,0},{32,16},{48,32},{64,48},{80,64},{96,80},{112,96},{128,112},... | collective-permute-start | bytes 270344 | tf_op jit(solution)/shard_map/ppermute | solution.py:609
  35.8 1.7 %collective-permute-done.2.halo_l.g_hl = f32[176,128]{1,0:T(8,128)S(1)} collective-permute-done((f32[176,128]{1,0:T(8,128)S(1)}, f32[176,128]{1,0:T(8,128)S(1)}, u32[]{:S(2)}, u32[]{:S(2)}) %collective-permute-start.2) | collective-permute-done | bytes 90144 | tf_op jit(solution)/shard_map/ppermute | solution.py:608
  37.6 1.1 %shard_map.79 = (f32[19,2,24,128]{3,2,1,0:T(8,128)S(1)}, f32[19,2,24,128]{3,2,1,0:T(8,128)S(1)}, f32[28,24,128]{2,1,0:T(8,128)S(1)}, f32[28,24,128]{2,1,0:T(8,12...) custom-call(s32[2]{0:T(128)S(1)} %add_convert_fusion.edge_ref, ...), custom_call_target="tpu_custom_call", output_to_operand_aliasing={{0}: (8, {}), {1}: (9, {}), {2}: (10, {}), {3}: (11, {}), {... | custom-call | tf_op jit(solution)/shard_map/pallas_call | solution.py:580
  38.7 3.0 %collective-permute-start.5 = (f32[28,24,128]{2,1,0:T(8,128)S(1)}, f32[28,24,128]{2,1,0:T(8,128)S(1)}, u32[]{:S(2)}, u32[]{:S(2)}) collective-permute-start(f32[28,24,128]{2,1,0:T(8,128)S(1)} %get-tuple-element.66), channel_id=1, source_target_pairs={{16,0},{32,16},{48,32},{64,48},{80,64},{96,80},{112,96},{128,112},... | collective-permute-start | bytes 1032200 | tf_op jit(solution)/shard_map/ppermute | solution.py:609
  41.7 12.4 %all_to_all.20.gathered = f32[16,8,128]{2,1,0:T(8,128)S(1)} all-to-all(f32[16,8,128]{2,1,0:T(8,128)S(1)} %get-tuple-element.69), channel_id=1, replica_groups=mesh['gx'=64,'gy_0'=4,'gy_1'=4] {'gy_0','gy_1'}, dimensions={0} | all-to-all | bytes 131072 | tf_op jit(solution)/shard_map/all_to_all | solution.py:613
  54.1 0.5 collective-permute-start.6
  54.6 0.6 shard_map.81
  55.4 3.1 %collective-permute-done.6.rad_l = f32[8,128]{1,0:T(8,128)S(1)} collective-permute-done((f32[8,128]{1,0:T(8,128)S(1)}, f32[8,128]{1,0:T(8,128)S(1)}, u32[]{:S(2)}, u32[]{:S(2)}) %collective-permute-start.6) | collective-permute-done | bytes 4128 | tf_op jit(solution)/shard_map/ppermute | solution.py:608
  58.5 1.0 shard_map.82
  59.5 2.9 %collective-permute-start.9 = (f32[28,16,128]{2,1,0:T(8,128)S(1)}, f32[28,16,128]{2,1,0:T(8,128)S(1)}, u32[]{:S(2)}, u32[]{:S(2)}) collective-permute-start(f32[28,16,128]{2,1,0:T(8,128)S(1)} %get-tuple-element.78), channel_id=1, source_target_pairs={{16,0},{32,16},{48,32},{64,48},{80,64},{96,80},{112,96},{128,112},... | collective-permute-start | bytes 688136 | tf_op jit(solution)/shard_map/ppermute | solution.py:609
  62.5 11.0 %all_to_all.21.gathered = f32[16,8,128]{2,1,0:T(8,128)S(1)} all-to-all(f32[16,8,128]{2,1,0:T(8,128)S(1)} %get-tuple-element.79), channel_id=1, replica_groups=mesh['gx'=64,'gy_0'=4,'gy_1'=4] {'gy_0','gy_1'}, dimensions={0} | all-to-all | bytes 131072 | tf_op jit(solution)/shard_map/all_to_all | solution.py:613
  74.8 2.9 %collective-permute-done.10.rad_l = f32[8,128]{1,0:T(8,128)S(1)} collective-permute-done((f32[8,128]{1,0:T(8,128)S(1)}, f32[8,128]{1,0:T(8,128)S(1)}, u32[]{:S(2)}, u32[]{:S(2)}) %collective-permute-start.10) | collective-permute-done | bytes 4128 | tf_op jit(solution)/shard_map/ppermute | solution.py:608
  77.7 1.3 %shard_map.85 = (f32[19,2,16,128]{3,2,1,0:T(8,128)S(1)}, f32[19,2,16,128]{3,2,1,0:T(8,128)S(1)}, f32[9,16,128]{2,1,0:T(8,128)S(1)}, f32[9,16,128]{2,1,0:T(8,128)S(1)}, f32[16,8,128]{2,1,0:T(8,128)}) custom-call(f32[28,16,128]{2,1,0:T(8,128)S(1)} %collective-permute-done.8.h_l, f32[28,16,128]{2,1,0:T(8,128)S(1)} %collective-permute-done.9.h_r, ...), custom_call_target="tpu_custom_call" | custom-call | tf_op jit(solution)/shard_map/pallas_call | solution.py:580
  79.0 4.8 %all-to-all-start.3 = ((f32[16,8,128]{2,1,0:T(8,128)}), f32[16,8,128]{2,1,0:T(8,128)S(1)}, u32[]{:S(2)}, u32[]{:S(2)}) async-start(f32[16,8,128]{2,1,0:T(8,128)} %get-tuple-element.88), calls=%async_computation.3 | async-start | bytes 131072 | tf_op jit(solution)/shard_map/all_to_all | solution.py:613
  83.9 2.9 %collective-permute-start.13 = (f32[9,16,128]{2,1,0:T(8,128)S(1)}, f32[9,16,128]{2,1,0:T(8,128)S(1)}, u32[]{:S(2)}, u32[]{:S(2)}) collective-permute-start(f32[9,16,128]{2,1,0:T(8,128)S(1)} %get-tuple-element.87), channel_id=1, source_target_pairs={{16,0},{32,16},{48,32},{64,48},{80,64},{96,80},{112,96},{128,112},... | collective-permute-start | bytes 221192 | tf_op jit(solution)/shard_map/ppermute | solution.py:609
  86.8 3.3 %all-to-all-done.3.gathered = f32[16,8,128]{2,1,0:T(8,128)S(1)} async-done(((f32[16,8,128]{2,1,0:T(8,128)}), f32[16,8,128]{2,1,0:T(8,128)S(1)}, u32[]{:S(2)}, u32[]{:S(2)}) %all-to-all-start.3) | async-done | bytes 65568 | tf_op jit(solution)/shard_map/all_to_all | solution.py:613
  90.7 0.6 dynamic-slice_bitcast_fusion
  91.5 2.9 %collective-permute-done.14.rad_l = f32[8,128]{1,0:T(8,128)S(1)} collective-permute-done((f32[8,128]{1,0:T(8,128)S(1)}, f32[8,128]{1,0:T(8,128)S(1)}, u32[]{:S(2)}, u32[]{:S(2)}) %collective-permute-start.14) | collective-permute-done | bytes 4128 | tf_op jit(solution)/shard_map/ppermute | solution.py:608
  94.5 0.8 shard_map.88
  (30 shorter events, 3.0 us)
Async XLA Ops:
  2.1 28.0 %all-to-all-start = ((f32[16,8,128]{2,1,0:T(8,128)}), f32[16,8,128]{2,1,0:T(8,128)S(1)}, u32[]{:S(2)}, u32[]{:S(2)}) async-start(f32[16,8,128]{2,1,0:T(8,128)} %get-tuple-element.51), calls=%async_computation | async-start | bytes 131072 | tf_op jit(solution)/shard_map/all_to_all | solution.py:613
  18.5 7.4 %collective-permute-start = (f32[104,128]{1,0:T(8,128)S(1)}, f32[104,128]{1,0:T(8,128)S(1)}, u32[]{:S(2)}, u32[]{:S(2)}) collective-permute-start(f32[104,128]{1,0:T(8,128)S(1)} %get-tuple-element.48), channel_id=1, source_target_pairs={{0,1},{2,3},{4,5},{6,7},{8,9},{10,11},{12,13},{14,15},{1,0},{3,2},... | collective-permute-start | bytes 159752 | tf_op jit(solution)/shard_map/ppermute | solution.py:632
  21.9 8.1 %collective-permute-start.1 = (f32[104,128]{1,0:T(8,128)S(1)}, f32[104,128]{1,0:T(8,128)S(1)}, u32[]{:S(2)}, u32[]{:S(2)}) collective-permute-start(f32[104,128]{1,0:T(8,128)S(1)} %get-tuple-element.50), channel_id=1, source_target_pairs={{1,2},{3,4},{5,6},{7,8},{9,10},{11,12},{13,14},{2,1},{4,3},{6,5},{... | collective-permute-start | bytes 159752 | tf_op jit(solution)/shard_map/ppermute | solution.py:632
  30.1 7.5 %collective-permute-start.2 = (f32[176,128]{1,0:T(8,128)S(1)}, f32[176,128]{1,0:T(8,128)S(1)}, u32[]{:S(2)}, u32[]{:S(2)}) collective-permute-start(f32[176,128]{1,0:T(8,128)S(1)} %get-tuple-element.52), channel_id=1, source_target_pairs={{0,16},{16,32},{32,48},{48,64},{64,80},{80,96},{96,112},{112,128},... | collective-permute-start | bytes 270344 | tf_op jit(solution)/shard_map/ppermute | solution.py:608
  30.1 7.4 %collective-permute-start.3 = (f32[176,128]{1,0:T(8,128)S(1)}, f32[176,128]{1,0:T(8,128)S(1)}, u32[]{:S(2)}, u32[]{:S(2)}) collective-permute-start(f32[176,128]{1,0:T(8,128)S(1)} %get-tuple-element.55), channel_id=1, source_target_pairs={{16,0},{32,16},{48,32},{64,48},{80,64},{96,80},{112,96},{128,112},... | collective-permute-start | bytes 270344 | tf_op jit(solution)/shard_map/ppermute | solution.py:609
  38.6 19.9 %collective-permute-start.4 = (f32[28,24,128]{2,1,0:T(8,128)S(1)}, f32[28,24,128]{2,1,0:T(8,128)S(1)}, u32[]{:S(2)}, u32[]{:S(2)}) collective-permute-start(f32[28,24,128]{2,1,0:T(8,128)S(1)} %get-tuple-element.65), channel_id=1, source_target_pairs={{0,16},{16,32},{32,48},{48,64},{64,80},{80,96},{96,112},{112,128},... | collective-permute-start | bytes 1032200 | tf_op jit(solution)/shard_map/ppermute | solution.py:608
  38.7 19.9 %collective-permute-start.5 = (f32[28,24,128]{2,1,0:T(8,128)S(1)}, f32[28,24,128]{2,1,0:T(8,128)S(1)}, u32[]{:S(2)}, u32[]{:S(2)}) collective-permute-start(f32[28,24,128]{2,1,0:T(8,128)S(1)} %get-tuple-element.66), channel_id=1, source_target_pairs={{16,0},{32,16},{48,32},{64,48},{80,64},{96,80},{112,96},{128,112},... | collective-permute-start | bytes 1032200 | tf_op jit(solution)/shard_map/ppermute | solution.py:609
  54.0 1.3 %collective-permute-start.7 = (f32[8,128]{1,0:T(8,128)S(1)}, f32[8,128]{1,0:T(8,128)S(1)}, u32[]{:S(2)}, u32[]{:S(2)}) collective-permute-start(f32[8,128]{1,0:T(8,128)S(1)} %get-tuple-element.71.rad), channel_id=1, source_target_pairs={{16,0},{32,16},{48,32},{64,48},{80,64},{96,80},{112,96},{128,112},... | collective-permute-start | bytes 12296 | tf_op jit(solution)/shard_map/ppermute | solution.py:609
  54.1 4.5 %collective-permute-start.6 = (f32[8,128]{1,0:T(8,128)S(1)}, f32[8,128]{1,0:T(8,128)S(1)}, u32[]{:S(2)}, u32[]{:S(2)}) collective-permute-start(f32[8,128]{1,0:T(8,128)S(1)} %get-tuple-element.71.rad), channel_id=1, source_target_pairs={{0,16},{16,32},{32,48},{48,64},{64,80},{80,96},{96,112},{112,128},... | collective-permute-start | bytes 12296 | tf_op jit(solution)/shard_map/ppermute | solution.py:608
  59.5 18.2 %collective-permute-start.8 = (f32[28,16,128]{2,1,0:T(8,128)S(1)}, f32[28,16,128]{2,1,0:T(8,128)S(1)}, u32[]{:S(2)}, u32[]{:S(2)}) collective-permute-start(f32[28,16,128]{2,1,0:T(8,128)S(1)} %get-tuple-element.77), channel_id=1, source_target_pairs={{0,16},{16,32},{32,48},{48,64},{64,80},{80,96},{96,112},{112,128},... | collective-permute-start | bytes 688136 | tf_op jit(solution)/shard_map/ppermute | solution.py:608
  59.5 18.2 %collective-permute-start.9 = (f32[28,16,128]{2,1,0:T(8,128)S(1)}, f32[28,16,128]{2,1,0:T(8,128)S(1)}, u32[]{:S(2)}, u32[]{:S(2)}) collective-permute-start(f32[28,16,128]{2,1,0:T(8,128)S(1)} %get-tuple-element.78), channel_id=1, source_target_pairs={{16,0},{32,16},{48,32},{64,48},{80,64},{96,80},{112,96},{128,112},... | collective-permute-start | bytes 688136 | tf_op jit(solution)/shard_map/ppermute | solution.py:609
  73.4 1.3 %collective-permute-start.11 = (f32[8,128]{1,0:T(8,128)S(1)}, f32[8,128]{1,0:T(8,128)S(1)}, u32[]{:S(2)}, u32[]{:S(2)}) collective-permute-start(f32[8,128]{1,0:T(8,128)S(1)} %shard_map.83.rad), channel_id=1, source_target_pairs={{16,0},{32,16},{48,32},{64,48},{80,64},{96,80},{112,96},{128,112},... | collective-permute-start | bytes 12296 | tf_op jit(solution)/shard_map/ppermute | solution.py:609
  73.5 4.3 %collective-permute-start.10 = (f32[8,128]{1,0:T(8,128)S(1)}, f32[8,128]{1,0:T(8,128)S(1)}, u32[]{:S(2)}, u32[]{:S(2)}) collective-permute-start(f32[8,128]{1,0:T(8,128)S(1)} %shard_map.83.rad), channel_id=1, source_target_pairs={{0,16},{16,32},{32,48},{48,64},{64,80},{80,96},{96,112},{112,128},... | collective-permute-start | bytes 12296 | tf_op jit(solution)/shard_map/ppermute | solution.py:608
  79.0 11.1 %all-to-all-start.3 = ((f32[16,8,128]{2,1,0:T(8,128)}), f32[16,8,128]{2,1,0:T(8,128)S(1)}, u32[]{:S(2)}, u32[]{:S(2)}) async-start(f32[16,8,128]{2,1,0:T(8,128)} %get-tuple-element.88), calls=%async_computation.3 | async-start | bytes 131072 | tf_op jit(solution)/shard_map/all_to_all | solution.py:613
  83.9 10.6 %collective-permute-start.12 = (f32[9,16,128]{2,1,0:T(8,128)S(1)}, f32[9,16,128]{2,1,0:T(8,128)S(1)}, u32[]{:S(2)}, u32[]{:S(2)}) collective-permute-start(f32[9,16,128]{2,1,0:T(8,128)S(1)} %get-tuple-element.86), channel_id=1, source_target_pairs={{0,16},{16,32},{32,48},{48,64},{64,80},{80,96},{96,112},{112,128},... | collective-permute-start | bytes 221192 | tf_op jit(solution)/shard_map/ppermute | solution.py:608
  83.9 10.6 %collective-permute-start.13 = (f32[9,16,128]{2,1,0:T(8,128)S(1)}, f32[9,16,128]{2,1,0:T(8,128)S(1)}, u32[]{:S(2)}, u32[]{:S(2)}) collective-permute-start(f32[9,16,128]{2,1,0:T(8,128)S(1)} %get-tuple-element.87), channel_id=1, source_target_pairs={{16,0},{32,16},{48,32},{64,48},{80,64},{96,80},{112,96},{128,112},... | collective-permute-start | bytes 221192 | tf_op jit(solution)/shard_map/ppermute | solution.py:609
  90.2 1.3 %collective-permute-start.15 = (f32[8,128]{1,0:T(8,128)S(1)}, f32[8,128]{1,0:T(8,128)S(1)}, u32[]{:S(2)}, u32[]{:S(2)}) collective-permute-start(f32[8,128]{1,0:T(8,128)S(1)} %shard_map.86.rad), channel_id=1, source_target_pairs={{16,0},{32,16},{48,32},{64,48},{80,64},{96,80},{112,96},{128,112},... | collective-permute-start | bytes 12296 | tf_op jit(solution)/shard_map/ppermute | solution.py:609
  90.2 4.3 %collective-permute-start.14 = (f32[8,128]{1,0:T(8,128)S(1)}, f32[8,128]{1,0:T(8,128)S(1)}, u32[]{:S(2)}, u32[]{:S(2)}) collective-permute-start(f32[8,128]{1,0:T(8,128)S(1)} %shard_map.86.rad), channel_id=1, source_target_pairs={{0,16},{16,32},{32,48},{48,64},{64,80},{80,96},{96,112},{112,128},... | collective-permute-start | bytes 12296 | tf_op jit(solution)/shard_map/ppermute | solution.py:608
